TPU v7x, 512 devices: a whole 4x8x8 slice. The times are simulated.
512 devices in a mesh: ctx: 64 (over z, y_hi, core), head: 8 (over x, y_lo).
Axes of the slice: x: 4, y: 8 (y_hi: 4, y_lo: 2; y = y_hi * 2 + y_lo), z: 8, core: 2. Of those that a mesh axis runs over, the one named last changes fastest.
Arguments:
- queries: bfloat16 [65536, 4096], P('ctx', 'head'), may hold values from -10 to 10, as said below
- keys: bfloat16 [65536, 4096], P('ctx', 'head'), may hold values from -4.6 to 4.6, as said below
- values: bfloat16 [65536, 4096], P('ctx', 'head'), may hold values from -6 to 6
Outputs:
- attended: bfloat16 [65536, 4096], P('ctx', 'head')
Inputs may be any that keep to these rules, and one draw needn't show every extreme that they name: real-valued queries. real-valued keys.
All inputs are finite; a program needn't handle non-finite values.
Results may differ from a plain program's by a relative error of at most 0.0099.
Values may be sent and summed in bfloat16 or wider, within the bound.
No kernel may reach another device: no remote copies, remote signals or barrier semaphores. Data moves between devices by JAX's collectives and lax.ppermute only.
A program may use at most 64 MiB of HBM per device.

v0:
```python
import jax
import jax.numpy as jnp
from jax import lax
from jax.sharding import PartitionSpec as P

HD = 128
POOL = 256
EDGE = 256


def extended(value, sides, width):
    for axis, dim in sides:
        size, length = (lax.axis_size(axis), value.shape[dim])
        up = [(i, (i + 1) % size) for i in range(size - 1)]
        down = [(j, i) for i, j in up]
        last = lax.slice_in_dim(value, length - width, length, axis=dim)
        leading = lax.slice_in_dim(value, 0, width, axis=dim)
        before = lax.ppermute(last, axis, up)
        after = lax.ppermute(leading, axis, down)
        value = jnp.concatenate([before, value, after], axis=dim)
    return value


def from_partner(value, axis, apart):
    mask = 2**apart
    pairs = [(source, source ^ mask) for source in range(lax.axis_size(axis))]
    return lax.ppermute(value, axis, pairs)


def pool_rows(block, group):
    shape = block.shape
    grouped = block.reshape(shape[:-2] + (shape[-2] // group, group, shape[-1])).astype(jnp.float32)
    return (jnp.sum(grouped, axis=-2) / jnp.float32(group**0.5)).astype(jnp.bfloat16)


def on_device(queries, keys, values):
    tok_rows, width = queries.shape
    heads_dev = width // HD
    count = lax.axis_size("ctx")
    depth_count = count.bit_length() - 1
    position = lax.axis_index("ctx")
    scale = jnp.float32(HD ** (-0.5))
    paired = jnp.stack((keys, values))
    level = pool_rows(paired, tok_rows // POOL)
    siblings = []
    partner = level
    padded = extended(paired, (("ctx", 1),), EDGE)
    left = padded[:, :EDGE]
    right = padded[:, EDGE + tok_rows :]
    for depth in range(depth_count):
        partner = from_partner(level, "ctx", depth)
        siblings.append(partner)
        if depth + 1 < depth_count:
            upper_half = position // 2**depth % 2 == 1
            lower = jnp.where(upper_half, partner, level)
            upper = jnp.where(upper_half, level, partner)
            level = pool_rows(jnp.concatenate([lower, upper], axis=1), 2)
    key_set = jnp.concatenate([paired, left, right] + siblings, axis=1)
    total = key_set.shape[1]
    valid = jnp.concatenate(
        [
            jnp.ones((tok_rows,), bool),
            jnp.broadcast_to(position > 0, (EDGE,)),
            jnp.broadcast_to(position < count - 1, (EDGE,)),
            jnp.ones((total - tok_rows - 2 * EDGE,), bool),
        ]
    )
    block_rows = min(512, tok_rows)
    block_count = tok_rows // block_rows

    def one_head(head_index):
        key_head = lax.dynamic_slice_in_dim(key_set[0], head_index * HD, HD, 1)
        value_head = lax.dynamic_slice_in_dim(key_set[1], head_index * HD, HD, 1)
        query_head = lax.dynamic_slice_in_dim(queries, head_index * HD, HD, 1)

        def one_block(block_index):
            query = lax.dynamic_slice_in_dim(query_head, block_index * block_rows, block_rows, 0)
            scores = (
                lax.dot_general(
                    query, key_head, (((1,), (1,)), ((), ())), preferred_element_type=jnp.float32
                )
                * scale
            )
            scores = jnp.where(valid[None, :], scores, jnp.float32(-1e30))
            peak = jnp.max(scores, axis=-1, keepdims=True)
            probs = jnp.exp(scores - peak)
            denom = jnp.sum(probs, axis=-1)
            weights = probs.astype(jnp.bfloat16)
            numer = jnp.dot(weights, value_head, preferred_element_type=jnp.float32)
            return (numer / denom[:, None]).astype(jnp.bfloat16)

        blocks = lax.map(one_block, jnp.arange(block_count, dtype=jnp.int32))
        return blocks.reshape(tok_rows, HD)

    per_head = lax.map(one_head, jnp.arange(heads_dev, dtype=jnp.int32))
    return jnp.transpose(per_head, (1, 0, 2)).reshape(tok_rows, width)


def solution(mesh):
    return jax.shard_map(
        on_device,
        mesh=mesh,
        in_specs=(P("ctx", "head"), P("ctx", "head"), P("ctx", "head")),
        out_specs=P("ctx", "head"),
        check_vma=False,
    )
```

profile of v0, /device:TPU:1, one launch (start us, length us, event | category | flops | bytes accessed | tf_op | source)
XLA Modules:
  0.0 269.5 jit_solution(10652032423691510950)
XLA Ops:
  0.0 2.3 fusion.25
  2.4 5.6 %collective-permute-start = (bf16[2,256,512]{2,1,0:T(8,128)(2,1)}, bf16[2,256,512]{2,1,0:T(8,128)(2,1)}, u32[]{:S(2)}, u32[]{:S(2)}) collective-permute-start(bf16[2,256,512]{2,1,0:T(8,128)(2,1)} %get-tuple-element.108), channel_id=1, source_target_pairs={{0,8},{8,16},{16,24},{24,32},{32,40},{40,48},{48,56},{56,64},{64,7... | collective-permute-start | bytes 1572872 | tf_op jit(solution)/shard_map/ppermute | solution.py:18
  8.0 5.4 %collective-permute-start.1 = (bf16[2,256,512]{2,1,0:T(8,128)(2,1)}, bf16[2,256,512]{2,1,0:T(8,128)(2,1)}, u32[]{:S(2)}, u32[]{:S(2)}) collective-permute-start(bf16[2,256,512]{2,1,0:T(8,128)(2,1)} %get-tuple-element.107), channel_id=1, source_target_pairs={{8,0},{16,8},{24,16},{32,24},{40,32},{48,40},{56,48},{64,56},{72,6... | collective-permute-start | bytes 1572872 | tf_op jit(solution)/shard_map/ppermute | solution.py:19
  13.4 2.2 stack.18
  16.6 4.4 %convert_reduce_fusion = f32[2,256,512]{2,1,0:T(8,128)S(1)} fusion(bf16[1,256,4,512]{3,2,1,0:T(4,128)(2,1)} %stack.19, bf16[1,256,4,512]{3,2,1,0:T(4,128)(2,1)} %stack.18), kind=kLoop, calls=%fused_computation.20 | loop fusion | flops 2883584 | bytes 3145728 | tf_op jit(solution)/shard_map/reduce_sum | solution.py:33
  22.0 1.9 collective-permute-start.2
  23.9 1.4 fusion.23
  25.3 1.9 constant_dynamic-update-slice_fusion.7
  27.2 1.9 constant_dynamic-update-slice_fusion.6
  29.1 2.1 broadcast_select_fusion.9
  31.5 2.2 reshape.35
  33.8 4.1 %reduce_sum.64 = f32[2,256,512]{2,1,0:T(8,128)S(1)} reduce(f32[2,256,2,512]{3,2,1,0:T(2,128)} %reshape.35, f32[]{:T(128)} %constant.130.clone.1), dimensions={2}, to_apply=%region_1.2 | reduce | flops 262144 | bytes 3145732 | tf_op jit(solution)/shard_map/reduce_sum | solution.py:33
  38.0 4.2 %collective-permute-start.3 = (bf16[2,256,512]{2,1,0:T(8,128)(2,1)S(1)}, bf16[2,256,512]{2,1,0:T(8,128)(2,1)S(1)}, u32[]{:S(2)}, u32[]{:S(2)}) collective-permute-start(bf16[2,256,512]{2,1,0:T(8,128)(2,1)S(1)} %multiply_convert_fusion.4), channel_id=1, source_target_pairs={{0,16},{8,24},{16,0},{24,8},{32,48},{40,56},{48,32},{56,40},{64,80... | collective-permute-start | bytes 1572872 | tf_op jit(solution)/shard_map/ppermute | solution.py:27
  42.2 22.3 %collective-permute-done.3 = bf16[2,256,512]{2,1,0:T(8,128)(2,1)S(1)} collective-permute-done((bf16[2,256,512]{2,1,0:T(8,128)(2,1)S(1)}, bf16[2,256,512]{2,1,0:T(8,128)(2,1)S(1)}, u32[]{:S(2)}, u32[]{:S(2)}) %collective-permute-start.3) | collective-permute-done | bytes 524320 | tf_op jit(solution)/shard_map/ppermute | solution.py:27
  65.8 2.2 reshape.36
  68.1 4.1 %reduce_sum.65 = f32[2,256,512]{2,1,0:T(8,128)S(1)} reduce(f32[2,256,2,512]{3,2,1,0:T(2,128)} %reshape.36, f32[]{:T(128)} %constant.130.clone.1), dimensions={2}, to_apply=%region_2.3 | reduce | flops 262144 | bytes 3145732 | tf_op jit(solution)/shard_map/reduce_sum | solution.py:33
  72.3 7.0 %collective-permute-start.4 = (bf16[2,256,512]{2,1,0:T(8,128)(2,1)S(1)}, bf16[2,256,512]{2,1,0:T(8,128)(2,1)S(1)}, u32[]{:S(2)}, u32[]{:S(2)}) collective-permute-start(bf16[2,256,512]{2,1,0:T(8,128)(2,1)S(1)} %multiply_convert_fusion.3), channel_id=1, source_target_pairs={{0,32},{8,40},{16,48},{24,56},{32,0},{40,8},{48,16},{56,24},{64,96... | collective-permute-start | bytes 1572872 | tf_op jit(solution)/shard_map/ppermute | solution.py:27
  79.3 23.1 %collective-permute-done.4 = bf16[2,256,512]{2,1,0:T(8,128)(2,1)S(1)} collective-permute-done((bf16[2,256,512]{2,1,0:T(8,128)(2,1)S(1)}, bf16[2,256,512]{2,1,0:T(8,128)(2,1)S(1)}, u32[]{:S(2)}, u32[]{:S(2)}) %collective-permute-start.4) | collective-permute-done | bytes 524320 | tf_op jit(solution)/shard_map/ppermute | solution.py:27
  103.8 2.2 reshape.37
  106.0 4.1 %reduce_sum.66 = f32[2,256,512]{2,1,0:T(8,128)S(1)} reduce(f32[2,256,2,512]{3,2,1,0:T(2,128)} %reshape.37, f32[]{:T(128)} %constant.130.clone.1), dimensions={2}, to_apply=%region_3.4 | reduce | flops 262144 | bytes 3145732 | tf_op jit(solution)/shard_map/reduce_sum | solution.py:33
  110.2 5.1 %collective-permute-start.5 = (bf16[2,256,512]{2,1,0:T(8,128)(2,1)S(1)}, bf16[2,256,512]{2,1,0:T(8,128)(2,1)S(1)}, u32[]{:S(2)}, u32[]{:S(2)}) collective-permute-start(bf16[2,256,512]{2,1,0:T(8,128)(2,1)S(1)} %multiply_convert_fusion.2), channel_id=1, source_target_pairs={{0,64},{8,72},{16,80},{24,88},{32,96},{40,104},{48,112},{56,120},{... | collective-permute-start | bytes 1572872 | tf_op jit(solution)/shard_map/ppermute | solution.py:27
  115.4 11.0 %collective-permute-done.5 = bf16[2,256,512]{2,1,0:T(8,128)(2,1)S(1)} collective-permute-done((bf16[2,256,512]{2,1,0:T(8,128)(2,1)S(1)}, bf16[2,256,512]{2,1,0:T(8,128)(2,1)S(1)}, u32[]{:S(2)}, u32[]{:S(2)}) %collective-permute-start.5) | collective-permute-done | bytes 524320 | tf_op jit(solution)/shard_map/ppermute | solution.py:27
  127.7 2.2 reshape.38
  129.9 4.1 %reduce_sum.67 = f32[2,256,512]{2,1,0:T(8,128)S(1)} reduce(f32[2,256,2,512]{3,2,1,0:T(2,128)} %reshape.38, f32[]{:T(128)} %constant.130.clone.1), dimensions={2}, to_apply=%region_4.5 | reduce | flops 262144 | bytes 3145732 | tf_op jit(solution)/shard_map/reduce_sum | solution.py:33
  134.1 6.1 %collective-permute-start.6 = (bf16[2,256,512]{2,1,0:T(8,128)(2,1)S(1)}, bf16[2,256,512]{2,1,0:T(8,128)(2,1)S(1)}, u32[]{:S(2)}, u32[]{:S(2)}) collective-permute-start(bf16[2,256,512]{2,1,0:T(8,128)(2,1)S(1)} %multiply_convert_fusion.1), channel_id=1, source_target_pairs={{0,128},{8,136},{16,144},{24,152},{32,160},{40,168},{48,176},{56,1... | collective-permute-start | bytes 1572872 | tf_op jit(solution)/shard_map/ppermute | solution.py:27
  140.3 22.5 %collective-permute-done.6 = bf16[2,256,512]{2,1,0:T(8,128)(2,1)S(1)} collective-permute-done((bf16[2,256,512]{2,1,0:T(8,128)(2,1)S(1)}, bf16[2,256,512]{2,1,0:T(8,128)(2,1)S(1)}, u32[]{:S(2)}, u32[]{:S(2)}) %collective-permute-start.6) | collective-permute-done | bytes 524320 | tf_op jit(solution)/shard_map/ppermute | solution.py:27
  164.0 2.2 reshape.39
  166.3 4.1 %reduce_sum.68 = f32[2,256,512]{2,1,0:T(8,128)S(1)} reduce(f32[2,256,2,512]{3,2,1,0:T(2,128)} %reshape.39, f32[]{:T(128)} %constant.130.clone.1), dimensions={2}, to_apply=%region_5.6 | reduce | flops 262144 | bytes 3145732 | tf_op jit(solution)/shard_map/reduce_sum | solution.py:33
  170.5 9.4 %collective-permute-start.7 = (bf16[2,256,512]{2,1,0:T(8,128)(2,1)S(1)}, bf16[2,256,512]{2,1,0:T(8,128)(2,1)S(1)}, u32[]{:S(2)}, u32[]{:S(2)}) collective-permute-start(bf16[2,256,512]{2,1,0:T(8,128)(2,1)S(1)} %multiply_convert_fusion), channel_id=1, source_target_pairs={{0,256},{8,264},{16,272},{24,280},{32,288},{40,296},{48,304},{56,3... | collective-permute-start | bytes 1572872 | tf_op jit(solution)/shard_map/ppermute | solution.py:27
  180.0 22.8 %collective-permute-done.7 = bf16[2,256,512]{2,1,0:T(8,128)(2,1)S(1)} collective-permute-done((bf16[2,256,512]{2,1,0:T(8,128)(2,1)S(1)}, bf16[2,256,512]{2,1,0:T(8,128)(2,1)S(1)}, u32[]{:S(2)}, u32[]{:S(2)}) %collective-permute-start.7) | collective-permute-done | bytes 524320 | tf_op jit(solution)/shard_map/ppermute | solution.py:27
  203.6 64.8 %while.21 = (s32[]{:T(128)}, bf16[4,1024,128]{2,1,0:T(8,128)(2,1)S(1)}, s32[4]{0:T(128)S(1)}, bf16[1024,512]{1,0:T(8,128)(2,1)}, bf16[2,3072,512]{2,1,0:T(8,128)...) while((s32[]{:T(128)}, ...), condition=%wide.region_11.12_spmd, body=%wide.region_6.11_spmd.sunk | while | flops 822737920 | bytes 37506532 | solution.py:95
  204.8 3.3 %fusion.37 = (bf16[1,3072,512]{2,1,0:T(8,128)(2,1)S(1)}, bf16[1,3072,512]{2,1,0:T(8,128)(2,1)S(1)}) fusion(bf16[2,3072,512]{2,1,0:T(8,128)(2,1)} %get-tuple-element.298), kind=kLoop, calls=%fused_computation.60.clone.1 | loop fusion | bytes 12582912 | tf_op jit(solution)/shard_map/while/body/eval_jaxpr/slice | solution.py:73
  209.2 10.5 %while.22 = (s32[]{:T(128)}, bf16[2,512,128]{2,1,0:T(8,128)(2,1)S(1)}, pred[3072]{0:T(1024)(128)(4,1)S(1)}, s32[2]{0:T(128)S(1)}, bf16[1024,128]{1,0:T(8,128)(2,...) while((s32[]{:T(128)}, ...), condition=%wide.region_10.10_spmd, body=%wide.region_7.9_spmd.sunk | while | flops 822737920 | bytes 20729008 | solution.py:92
  213.0 1.5 fusion.43
  216.9 1.4 fusion.42
  218.3 1.5 fusion.43
  221.0 3.3 %fusion.37 = (bf16[1,3072,512]{2,1,0:T(8,128)(2,1)S(1)}, bf16[1,3072,512]{2,1,0:T(8,128)(2,1)S(1)}) fusion(bf16[2,3072,512]{2,1,0:T(8,128)(2,1)} %get-tuple-element.298), kind=kLoop, calls=%fused_computation.60.clone.1 | loop fusion | bytes 12582912 | tf_op jit(solution)/shard_map/while/body/eval_jaxpr/slice | solution.py:73
  225.5 10.5 %while.22 = (s32[]{:T(128)}, bf16[2,512,128]{2,1,0:T(8,128)(2,1)S(1)}, pred[3072]{0:T(1024)(128)(4,1)S(1)}, s32[2]{0:T(128)S(1)}, bf16[1024,128]{1,0:T(8,128)(2,...) while((s32[]{:T(128)}, ...), condition=%wide.region_10.10_spmd, body=%wide.region_7.9_spmd.sunk | while | flops 822737920 | bytes 20729008 | solution.py:92
  229.2 1.5 fusion.43
  234.5 1.5 fusion.43
  237.2 3.3 %fusion.37 = (bf16[1,3072,512]{2,1,0:T(8,128)(2,1)S(1)}, bf16[1,3072,512]{2,1,0:T(8,128)(2,1)S(1)}) fusion(bf16[2,3072,512]{2,1,0:T(8,128)(2,1)} %get-tuple-element.298), kind=kLoop, calls=%fused_computation.60.clone.1 | loop fusion | bytes 12582912 | tf_op jit(solution)/shard_map/while/body/eval_jaxpr/slice | solution.py:73
  241.7 10.5 %while.22 = (s32[]{:T(128)}, bf16[2,512,128]{2,1,0:T(8,128)(2,1)S(1)}, pred[3072]{0:T(1024)(128)(4,1)S(1)}, s32[2]{0:T(128)S(1)}, bf16[1024,128]{1,0:T(8,128)(2,...) while((s32[]{:T(128)}, ...), condition=%wide.region_10.10_spmd, body=%wide.region_7.9_spmd.sunk | while | flops 822737920 | bytes 20729008 | solution.py:92
  245.5 1.5 fusion.43
  250.7 1.5 fusion.43
  253.4 3.3 %fusion.37 = (bf16[1,3072,512]{2,1,0:T(8,128)(2,1)S(1)}, bf16[1,3072,512]{2,1,0:T(8,128)(2,1)S(1)}) fusion(bf16[2,3072,512]{2,1,0:T(8,128)(2,1)} %get-tuple-element.298), kind=kLoop, calls=%fused_computation.60.clone.1 | loop fusion | bytes 12582912 | tf_op jit(solution)/shard_map/while/body/eval_jaxpr/slice | solution.py:73
  257.9 10.5 %while.22 = (s32[]{:T(128)}, bf16[2,512,128]{2,1,0:T(8,128)(2,1)S(1)}, pred[3072]{0:T(1024)(128)(4,1)S(1)}, s32[2]{0:T(128)S(1)}, bf16[1024,128]{1,0:T(8,128)(2,...) while((s32[]{:T(128)}, ...), condition=%wide.region_10.10_spmd, body=%wide.region_7.9_spmd.sunk | while | flops 822737920 | bytes 20729008 | solution.py:92
  261.7 1.5 fusion.43
  266.9 1.5 fusion.43
  (79 shorter events, 41.6 us)
Async XLA Ops:
  0.0 15.5 %copy-start = (bf16[1024,512]{1,0:T(8,128)(2,1)S(1)}, bf16[1024,512]{1,0:T(8,128)(2,1)}, u32[]{:S(2)}) copy-start(bf16[1024,512]{1,0:T(8,128)(2,1)} %param.9) | copy-start | bytes 3145732
  2.4 23.0 %collective-permute-start = (bf16[2,256,512]{2,1,0:T(8,128)(2,1)}, bf16[2,256,512]{2,1,0:T(8,128)(2,1)}, u32[]{:S(2)}, u32[]{:S(2)}) collective-permute-start(bf16[2,256,512]{2,1,0:T(8,128)(2,1)} %get-tuple-element.108), channel_id=1, source_target_pairs={{0,8},{8,16},{16,24},{24,32},{32,40},{40,48},{48,56},{56,64},{64,7... | collective-permute-start | bytes 1572872 | tf_op jit(solution)/shard_map/ppermute | solution.py:18
  7.9 16.0 %copy-start.1 = (bf16[1024,512]{1,0:T(8,128)(2,1)S(1)}, bf16[1024,512]{1,0:T(8,128)(2,1)}, u32[]{:S(2)}) copy-start(bf16[1024,512]{1,0:T(8,128)(2,1)} %param.8) | copy-start | bytes 3145732
  8.0 19.3 %collective-permute-start.1 = (bf16[2,256,512]{2,1,0:T(8,128)(2,1)}, bf16[2,256,512]{2,1,0:T(8,128)(2,1)}, u32[]{:S(2)}, u32[]{:S(2)}) collective-permute-start(bf16[2,256,512]{2,1,0:T(8,128)(2,1)} %get-tuple-element.107), channel_id=1, source_target_pairs={{8,0},{16,8},{24,16},{32,24},{40,32},{48,40},{56,48},{64,56},{72,6... | collective-permute-start | bytes 1572872 | tf_op jit(solution)/shard_map/ppermute | solution.py:19
  22.0 7.2 %collective-permute-start.2 = (bf16[2,256,512]{2,1,0:T(8,128)(2,1)}, bf16[2,256,512]{2,1,0:T(8,128)(2,1)}, u32[]{:S(2)}, u32[]{:S(2)}) collective-permute-start(bf16[2,256,512]{2,1,0:T(8,128)(2,1)} %multiply_convert_fusion.5), channel_id=1, source_target_pairs={{0,8},{8,0},{16,24},{24,16},{32,40},{40,32},{48,56},{56,48},{64,72... | collective-permute-start | bytes 1572872 | tf_op jit(solution)/shard_map/ppermute | solution.py:27
  38.0 26.5 %collective-permute-start.3 = (bf16[2,256,512]{2,1,0:T(8,128)(2,1)S(1)}, bf16[2,256,512]{2,1,0:T(8,128)(2,1)S(1)}, u32[]{:S(2)}, u32[]{:S(2)}) collective-permute-start(bf16[2,256,512]{2,1,0:T(8,128)(2,1)S(1)} %multiply_convert_fusion.4), channel_id=1, source_target_pairs={{0,16},{8,24},{16,0},{24,8},{32,48},{40,56},{48,32},{56,40},{64,80... | collective-permute-start | bytes 1572872 | tf_op jit(solution)/shard_map/ppermute | solution.py:27
  72.3 30.1 %collective-permute-start.4 = (bf16[2,256,512]{2,1,0:T(8,128)(2,1)S(1)}, bf16[2,256,512]{2,1,0:T(8,128)(2,1)S(1)}, u32[]{:S(2)}, u32[]{:S(2)}) collective-permute-start(bf16[2,256,512]{2,1,0:T(8,128)(2,1)S(1)} %multiply_convert_fusion.3), channel_id=1, source_target_pairs={{0,32},{8,40},{16,48},{24,56},{32,0},{40,8},{48,16},{56,24},{64,96... | collective-permute-start | bytes 1572872 | tf_op jit(solution)/shard_map/ppermute | solution.py:27
  110.2 16.1 %collective-permute-start.5 = (bf16[2,256,512]{2,1,0:T(8,128)(2,1)S(1)}, bf16[2,256,512]{2,1,0:T(8,128)(2,1)S(1)}, u32[]{:S(2)}, u32[]{:S(2)}) collective-permute-start(bf16[2,256,512]{2,1,0:T(8,128)(2,1)S(1)} %multiply_convert_fusion.2), channel_id=1, source_target_pairs={{0,64},{8,72},{16,80},{24,88},{32,96},{40,104},{48,112},{56,120},{... | collective-permute-start | bytes 1572872 | tf_op jit(solution)/shard_map/ppermute | solution.py:27
  134.1 28.6 %collective-permute-start.6 = (bf16[2,256,512]{2,1,0:T(8,128)(2,1)S(1)}, bf16[2,256,512]{2,1,0:T(8,128)(2,1)S(1)}, u32[]{:S(2)}, u32[]{:S(2)}) collective-permute-start(bf16[2,256,512]{2,1,0:T(8,128)(2,1)S(1)} %multiply_convert_fusion.1), channel_id=1, source_target_pairs={{0,128},{8,136},{16,144},{24,152},{32,160},{40,168},{48,176},{56,1... | collective-permute-start | bytes 1572872 | tf_op jit(solution)/shard_map/ppermute | solution.py:27
  170.5 32.3 %collective-permute-start.7 = (bf16[2,256,512]{2,1,0:T(8,128)(2,1)S(1)}, bf16[2,256,512]{2,1,0:T(8,128)(2,1)S(1)}, u32[]{:S(2)}, u32[]{:S(2)}) collective-permute-start(bf16[2,256,512]{2,1,0:T(8,128)(2,1)S(1)} %multiply_convert_fusion), channel_id=1, source_target_pairs={{0,256},{8,264},{16,272},{24,280},{32,288},{40,296},{48,304},{56,3... | collective-permute-start | bytes 1572872 | tf_op jit(solution)/shard_map/ppermute | solution.py:27
where the time goes:
time: 270 us
  waiting for transfers between devices  102 us (38%)
  other arithmetic  49.3 us (18%)
  local copies, waits for them, and re-layouts  45.3 us (17%)
  starting transfers between devices  44.6 us (17%)
  matrix products  21 us (8%)
  loops' own time  7.35 us (3%)
    ppermute x6, waiting for transfers between devices, from_partner(): return lax.ppermute(value, axis, pairs)  102 us
    ppermute x6, starting transfers between devices, from_partner(): return lax.ppermute(value, axis, pairs)  33.6 us
    reduce_sum x6, other arithmetic, pool_rows(): jnp.sum(grouped, axis=-2) / jnp.float32(group ** 0.5)  24.8 us
    slice x4, local copies, waits for them, and re-layouts, one_head(): value_head = lax.dynamic_slice_in_dim(key_set[1], head_index * HD, HD, 1)  13 us
    dot_general x8, matrix products, one_block(): numer = jnp.dot(weights, value_head, preferred_element_type=jnp.float32)  11.7 us
    reduce_sum x8, other arithmetic, one_block(): denom = jnp.sum(probs, axis=-1)  11.4 us
    convert_element_type x5, local copies, waits for them, and re-layouts, pool_rows(): block.reshape(shape[:-2] + (shape[-2] // group, group, shape[-1]))  11.2 us
    dot_general x8, matrix products, one_block(): lax.dot_general(query, key_head, (((1,), (1,)), ((), ())), preferred_elem...  9.36 us
  transfers between devices with their start and end apart: 8, of which 5 were waited for; matrix products, arithmetic and copies ran while one was open for 5% of the time, Pallas kernels for 0%

commit v1 on v0

v1 whole, which is shorter than its diff:
```python
import functools

import jax
import jax.numpy as jnp
from jax import lax
from jax.experimental import pallas as pl
from jax.experimental.pallas import tpu as pltpu
from jax.sharding import PartitionSpec as P


HD = 128
HEADS_DEV = 4
WIDTH = HEADS_DEV * HD
TOK = 1024
POOL = 256
EDGE = 256
N_CTX = 64
SCALE_LOG2 = (HD**-0.5) * 1.4426950408889634
Q_TILE = 256


def swap(value, partner):
    pairs = []
    for source in range(N_CTX):
        z, y, core = source // 8, (source // 2) % 4, source % 2
        target = partner(z, y, core)
        if target is not None:
            pairs.append((source, target))
    return lax.ppermute(value, "ctx", pairs)


def index_of(z, y, core):
    return (z * 4 + y) * 2 + core


def other_core(z, y, core):
    return index_of(z, y, 1 - core)


def along_y(bits):
    return lambda z, y, core: index_of(z, y ^ bits, core)


def along_z(bits):
    return lambda z, y, core: index_of(z ^ bits, y, core)


def beside(z, y, core):
    here = index_of(z, y, core)
    there = here + 1 if core else here - 1
    return there if 0 <= there < N_CTX else None


def pooling_matrix(rows, group):
    out = lax.broadcasted_iota(jnp.int32, (rows // group, rows), 0)
    src = lax.broadcasted_iota(jnp.int32, (rows // group, rows), 1)
    return (src // group == out).astype(jnp.float32).astype(jnp.bfloat16)


def pool(value, group, matrix):
    total = jnp.dot(matrix, value, preferred_element_type=jnp.float32)
    return (total / jnp.float32(group**0.5)).astype(jnp.bfloat16)


def first_kernel(core_ref, k_ref, v_ref, near_ref, far_ref, one_ref, two_ref):
    core = core_ref[0]
    by4 = pooling_matrix(256, 4)
    by2 = pooling_matrix(256, 2)
    for side, ref in enumerate((k_ref, v_ref)):
        cols = pl.ds(side * WIDTH, WIDTH)
        for part in range(4):
            near_ref[pl.ds(part * 64, 64), cols] = pool(ref[pl.ds(part * 256, 256), :], 4, by4)
        one = pool(near_ref[pl.ds(0, 256), cols], 2, by2)
        one_ref[:, cols] = one
        two_ref[:, cols] = pool(one, 2, by2[:64, :128])
        last = pl.multiple_of((1 - core) * (TOK - EDGE), EDGE)
        near_ref[pl.ds(POOL, EDGE), cols] = ref[pl.ds(last, EDGE), :]
        first = pl.multiple_of(core * (TOK - EDGE), EDGE)
        far_ref[:, cols] = ref[pl.ds(first, EDGE), :]


def first_pools(core, keys, values):
    shape = lambda rows: jax.ShapeDtypeStruct((rows, 2 * WIDTH), jnp.bfloat16)
    vmem = pl.BlockSpec(memory_space=pltpu.VMEM)
    return pl.pallas_call(
        first_kernel,
        in_specs=[pl.BlockSpec(memory_space=pltpu.SMEM), vmem, vmem],
        out_specs=[vmem] * 4,
        out_shape=[shape(512), shape(256), shape(128), shape(64)],
        cost_estimate=pl.CostEstimate(flops=10**8, bytes_accessed=4 * 2**20, transcendentals=0),
        name="first_pools",
    )(core, keys, values)


def plane_kernel(own_ref, a_ref, b_ref, c_ref, got_ref, three_ref, four_ref, five_ref):
    by2 = pooling_matrix(256, 2)
    a, b, c = a_ref[...], b_ref[...], c_ref[...]
    got_ref[pl.ds(0, 128), :] = a
    got_ref[pl.ds(128, 64), :] = b
    got_ref[pl.ds(192, 64), :] = c
    a = pool(a, 2, by2[:64, :128])
    rows = jnp.concatenate([own_ref[...], a, b, c], axis=0)
    three = pool(rows, 2, by2)
    four = pool(three, 2, by2[:64, :128])
    three_ref[...] = three
    four_ref[...] = four
    five_ref[...] = pool(four, 2, by2[:32, :64])


def plane_pools(own, a, b, c):
    shape = lambda rows: jax.ShapeDtypeStruct((rows, 2 * WIDTH), jnp.bfloat16)
    vmem = pl.BlockSpec(memory_space=pltpu.VMEM)
    return pl.pallas_call(
        plane_kernel,
        in_specs=[vmem] * 4,
        out_specs=[vmem] * 4,
        out_shape=[shape(256), shape(128), shape(64), shape(32)],
        cost_estimate=pl.CostEstimate(flops=10**8, bytes_accessed=2 * 2**20, transcendentals=0),
        name="plane_pools",
    )(own, a, b, c)


def attend_kernel(plan, carried, final, *refs):
    refs = list(refs)
    bias = refs.pop(0)[0]
    q_ref = refs.pop(0)
    pieces = []
    for masked in plan:
        pieces.append((refs.pop(0), refs.pop(0), masked))
    if carried:
        acc_in, m_in, l_in = refs.pop(0), refs.pop(0), refs.pop(0)
    for tile in range(TOK // Q_TILE):
        cols = pl.ds(tile * Q_TILE, Q_TILE)
        query = q_ref[cols, :]
        scores = []
        for k_ref, _, masked in pieces:
            s = lax.dot_general(
                k_ref[...], query, (((1,), (1,)), ((), ())), preferred_element_type=jnp.float32
            )
            scores.append(s + bias if masked else s)
        peak = functools.reduce(jnp.maximum, [jnp.max(s, axis=0, keepdims=True) for s in scores])
        if carried:
            before = m_in[0, :, cols]
            peak = jnp.maximum(peak, before)
            fade = jnp.exp2((before - peak) * SCALE_LOG2)
            total = l_in[0, :, cols] * fade
            acc = acc_in[0, :, cols] * fade
        else:
            total, acc = 0.0, 0.0
        for s, (_, v_ref, _) in zip(scores, pieces):
            p = jnp.exp2((s - peak) * SCALE_LOG2)
            total = total + jnp.sum(p, axis=0, keepdims=True)
            acc = acc + lax.dot_general(
                v_ref[...],
                p.astype(jnp.bfloat16),
                (((0,), (0,)), ((), ())),
                preferred_element_type=jnp.float32,
            )
        if final:
            refs[0][cols, :] = (acc / total).T.astype(jnp.bfloat16)
        else:
            refs[0][0, :, cols] = acc
            refs[1][0, :, cols] = peak
            refs[2][0, :, cols] = total


def attend(bias, queries, pieces, state, final):
    head = lambda rows, first: pl.BlockSpec((rows, HD), lambda h: (0, first + h))
    per_head = lambda rows: pl.BlockSpec((1, rows, TOK), lambda h: (h, 0, 0))
    in_specs = [pl.BlockSpec(memory_space=pltpu.SMEM), head(TOK, 0)]
    operands = [bias, queries]
    count = 0
    for k, v, first, _ in pieces:
        in_specs += [head(k.shape[0], 0), head(v.shape[0], first)]
        operands += [k, v]
        count += k.shape[0]
    if state is not None:
        in_specs += [per_head(HD), per_head(1), per_head(1)]
        operands += list(state)
    if final:
        out_specs = head(TOK, 0)
        out_shape = jax.ShapeDtypeStruct((TOK, WIDTH), jnp.bfloat16)
    else:
        out_specs = [per_head(HD), per_head(1), per_head(1)]
        out_shape = [
            jax.ShapeDtypeStruct((HEADS_DEV, rows, TOK), jnp.float32) for rows in (HD, 1, 1)
        ]
    return pl.pallas_call(
        functools.partial(attend_kernel, tuple(p[3] for p in pieces), state is not None, final),
        grid=(HEADS_DEV,),
        in_specs=in_specs,
        out_specs=out_specs,
        out_shape=out_shape,
        compiler_params=pltpu.CompilerParams(
            dimension_semantics=("arbitrary",), vmem_limit_bytes=48 * 2**20
        ),
        cost_estimate=pl.CostEstimate(
            flops=4 * TOK * count * WIDTH,
            bytes_accessed=2 * TOK * WIDTH + 4 * count * WIDTH + 4 * TOK * WIDTH,
            transcendentals=TOK * count * HEADS_DEV,
        ),
    )(*operands)


def on_device(queries, keys, values):
    position = lax.axis_index("ctx")
    core = (position % 2).astype(jnp.int32).reshape(1)
    outer = (position == 0) | (position == N_CTX - 1)
    bias = jnp.where(outer, jnp.float32(-1e30), jnp.float32(0)).reshape(1)

    near, far, one, two = first_pools(core, keys, values)
    got2 = swap(two, along_y(2))
    got1 = swap(one, along_y(1))
    got3 = swap(two, along_y(3))
    near_got = swap(near, other_core)
    state = attend(bias, queries, [(keys, values, 0, False)], None, False)
    planes, three, four, five = plane_pools(two, got1, got2, got3)
    from_z = [swap(five, along_z(b)) for b in (4, 5, 6, 7)]
    from_z += [swap(four, along_z(b)) for b in (2, 3)]
    from_z += [swap(three, along_z(1))]
    far_got = swap(far, beside)
    planes_got = swap(planes, other_core)
    pieces = [(x, x, HEADS_DEV, False) for x in (near_got, planes, planes_got)]
    pieces += [(far_got, far_got, HEADS_DEV, True)]
    state = attend(bias, queries, pieces, state, False)
    upper = jnp.concatenate(from_z, axis=0)
    upper_got = swap(upper, other_core)
    state = attend(bias, queries, [(upper, upper, HEADS_DEV, False)], state, False)
    return attend(bias, queries, [(upper_got, upper_got, HEADS_DEV, False)], state, True)


def solution(mesh):
    return jax.shard_map(
        on_device,
        mesh=mesh,
        in_specs=(P("ctx", "head"), P("ctx", "head"), P("ctx", "head")),
        out_specs=P("ctx", "head"),
        check_vma=False,
    )
```

time: 270 us -> 132 us (0.49)
  the two profiles are of different devices: /device:TPU:1 before, /device:TPU:53 now
where the time goes in v1:
time: 132 us
  starting transfers between devices  69.8 us (53%)
  Pallas kernels  46.6 us (35%)
  waiting for transfers between devices  9.83 us (7%)
  local copies, waits for them, and re-layouts  5.12 us (4%)
    ppermute x14, starting transfers between devices, swap(): return lax.ppermute(value, 'ctx', pairs)  69.8 us
    pallas_call x4, Pallas kernels, attend(): pl.pallas_call(functools.partial(attend_kernel, tuple((p[3] for p in piec...  40.3 us
    ppermute x14, waiting for transfers between devices, swap(): return lax.ppermute(value, 'ctx', pairs)  9.83 us
    unnamed x22, local copies, waits for them, and re-layouts  5.1 us
    pallas_call x1, Pallas kernels, first_pools(): pl.pallas_call(first_kernel, in_specs=[pl.BlockSpec(memory_space=pltpu.SM...  3.88 us
  transfers between devices with their start and end apart: 14, of which 3 were waited for; matrix products, arithmetic and copies ran while one was open for 0% of the time, Pallas kernels for 25%

profile of v1, /device:TPU:53, one launch (start us, length us, event | category | flops | bytes accessed | tf_op | source)
XLA Modules:
  0.0 131.7 jit_solution(6741139133159376708)
XLA Ops:
  0.0 3.9 %first_pools.1 = (bf16[512,1024]{1,0:T(8,128)(2,1)}, bf16[256,1024]{1,0:T(8,128)(2,1)}, bf16[128,1024]{1,0:T(8,128)(2,1)}, bf16[64,1024]{1,0:T(8,128)(2,1)}) custom-call(s32[1]{0:T(128)} %bitcast.1.core_ref, bf16[1024,512]{1,0:T(8,128)(2,1)} %refs_2_.1, bf16[1024,512]{1,0:T(8,128)(2,1)} %refs_3_.1), custom_call_target="tpu_custom_call" | custom-call | flops 100000000 | bytes 4194304 | tf_op jit(solution)/shard_map/first_pools/pallas_call | solution.py:85
  3.9 3.7 %collective-permute-start = (bf16[128,1024]{1,0:T(8,128)(2,1)}, bf16[128,1024]{1,0:T(8,128)(2,1)S(1)}, u32[]{:S(2)}, u32[]{:S(2)}) collective-permute-start(bf16[128,1024]{1,0:T(8,128)(2,1)} %get-tuple-element.23), channel_id=1, source_target_pairs={{0,16},{8,24},{16,0},{24,8},{32,48},{40,56},{48,32},{56,40},{64,80... | collective-permute-start | bytes 786440 | tf_op jit(solution)/shard_map/ppermute | solution.py:29
  7.6 1.9 %collective-permute-start.1 = (bf16[64,1024]{1,0:T(8,128)(2,1)}, bf16[64,1024]{1,0:T(8,128)(2,1)S(1)}, u32[]{:S(2)}, u32[]{:S(2)}) collective-permute-start(bf16[64,1024]{1,0:T(8,128)(2,1)} %get-tuple-element.22.own_ref), channel_id=1, source_target_pairs={{0,32},{8,40},{16,48},{24,56},{32,0},{40,8},{48,16},{56,24},{64,96... | collective-permute-start | bytes 393224 | tf_op jit(solution)/shard_map/ppermute | solution.py:29
  9.6 5.7 %collective-permute-start.2 = (bf16[64,1024]{1,0:T(8,128)(2,1)}, bf16[64,1024]{1,0:T(8,128)(2,1)S(1)}, u32[]{:S(2)}, u32[]{:S(2)}) collective-permute-start(bf16[64,1024]{1,0:T(8,128)(2,1)} %get-tuple-element.22.own_ref), channel_id=1, source_target_pairs={{0,48},{8,56},{16,32},{24,40},{32,16},{40,24},{48,0},{56,8},{64,11... | collective-permute-start | bytes 393224 | tf_op jit(solution)/shard_map/ppermute | solution.py:29
  15.3 2.3 %collective-permute-done.1.b_ref = bf16[64,1024]{1,0:T(8,128)(2,1)S(1)} collective-permute-done((bf16[64,1024]{1,0:T(8,128)(2,1)}, bf16[64,1024]{1,0:T(8,128)(2,1)S(1)}, u32[]{:S(2)}, u32[]{:S(2)}) %collective-permute-start.1) | collective-permute-done | bytes 131104 | tf_op jit(solution)/shard_map/ppermute | solution.py:29
  17.6 0.0 copy-start.6
  17.6 7.4 %collective-permute-done.2.c_ref = bf16[64,1024]{1,0:T(8,128)(2,1)S(1)} collective-permute-done((bf16[64,1024]{1,0:T(8,128)(2,1)}, bf16[64,1024]{1,0:T(8,128)(2,1)S(1)}, u32[]{:S(2)}, u32[]{:S(2)}) %collective-permute-start.2) | collective-permute-done | bytes 131104 | tf_op jit(solution)/shard_map/ppermute | solution.py:29
  25.0 0.0 copy-start.7
  25.0 0.1 collective-permute-done.a_ref
  25.1 0.0 copy-done.6
  25.1 0.6 copy-done.7
  25.7 0.0 copy-start.5
  25.7 0.7 copy-done.5
  26.4 2.4 %plane_pools.1 = (bf16[256,1024]{1,0:T(8,128)(2,1)}, bf16[128,1024]{1,0:T(8,128)(2,1)}, bf16[64,1024]{1,0:T(8,128)(2,1)}, bf16[32,1024]{1,0:T(8,128)(2,1)}) custom-call(bf16[64,1024]{1,0:T(8,128)(2,1)} %get-tuple-element.22.own_ref, bf16[128,1024]{1,0:T(8,128)(2,1)} %copy-done.5, bf16[64,1024]{1,0:T(8,128)(2,1)} %copy-done.6, bf16[64,1024]{1,0:T(8,128)(2,1)} %copy-done.7), custom_call_target="tpu_custom_call" | custom-call | flops 100000000 | bytes 2097152 | tf_op jit(solution)/shard_map/plane_pools/pallas_call | solution.py:113
  28.8 10.6 %collective-permute-start.3 = (bf16[32,1024]{1,0:T(8,128)(2,1)}, bf16[32,1024]{1,0:T(8,128)(2,1)S(1)}, u32[]{:S(2)}, u32[]{:S(2)}) collective-permute-start(bf16[32,1024]{1,0:T(8,128)(2,1)} %get-tuple-element.24), channel_id=1, source_target_pairs={{0,256},{8,264},{16,272},{24,280},{32,288},{40,296},{48,304},{56,3... | collective-permute-start | bytes 196616 | tf_op jit(solution)/shard_map/ppermute | solution.py:29
  39.4 6.0 %collective-permute-start.11 = (bf16[512,1024]{1,0:T(8,128)(2,1)}, bf16[512,1024]{1,0:T(8,128)(2,1)}, u32[]{:S(2)}, u32[]{:S(2)}) collective-permute-start(bf16[512,1024]{1,0:T(8,128)(2,1)} %get-tuple-element.27), channel_id=1, source_target_pairs={{0,8},{8,0},{16,24},{24,16},{32,40},{40,32},{48,56},{56,48},{64,72... | collective-permute-start | bytes 3145736 | tf_op jit(solution)/shard_map/ppermute | solution.py:29
  45.4 3.9 %collective-permute-start.13 = (bf16[256,1024]{1,0:T(8,128)(2,1)}, bf16[256,1024]{1,0:T(8,128)(2,1)S(1)}, u32[]{:S(2)}, u32[]{:S(2)}) collective-permute-start(bf16[256,1024]{1,0:T(8,128)(2,1)} %get-tuple-element.29), channel_id=1, source_target_pairs={{8,16},{16,8},{24,32},{32,24},{40,48},{48,40},{56,64},{64,56},{72,... | collective-permute-start | bytes 1572872 | tf_op jit(solution)/shard_map/ppermute | solution.py:29
  49.4 1.9 %collective-permute-start.4 = (bf16[32,1024]{1,0:T(8,128)(2,1)}, bf16[32,1024]{1,0:T(8,128)(2,1)S(1)}, u32[]{:S(2)}, u32[]{:S(2)}) collective-permute-start(bf16[32,1024]{1,0:T(8,128)(2,1)} %get-tuple-element.24), channel_id=1, source_target_pairs={{0,320},{8,328},{16,336},{24,344},{32,352},{40,360},{48,368},{56,3... | collective-permute-start | bytes 196616 | tf_op jit(solution)/shard_map/ppermute | solution.py:29
  51.3 5.3 %collective-permute-start.5 = (bf16[32,1024]{1,0:T(8,128)(2,1)}, bf16[32,1024]{1,0:T(8,128)(2,1)S(1)}, u32[]{:S(2)}, u32[]{:S(2)}) collective-permute-start(bf16[32,1024]{1,0:T(8,128)(2,1)} %get-tuple-element.24), channel_id=1, source_target_pairs={{0,384},{8,392},{16,400},{24,408},{32,416},{40,424},{48,432},{56,4... | collective-permute-start | bytes 196616 | tf_op jit(solution)/shard_map/ppermute | solution.py:29
  56.6 0.0 collective-permute-done.3
  56.6 3.0 %collective-permute-start.6 = (bf16[32,1024]{1,0:T(8,128)(2,1)}, bf16[32,1024]{1,0:T(8,128)(2,1)S(1)}, u32[]{:S(2)}, u32[]{:S(2)}) collective-permute-start(bf16[32,1024]{1,0:T(8,128)(2,1)} %get-tuple-element.24), channel_id=1, source_target_pairs={{0,448},{8,456},{16,464},{24,472},{32,480},{40,488},{48,496},{56,5... | collective-permute-start | bytes 196616 | tf_op jit(solution)/shard_map/ppermute | solution.py:29
  59.6 0.0 collective-permute-done.4
  59.6 4.7 %collective-permute-start.7 = (bf16[64,1024]{1,0:T(8,128)(2,1)}, bf16[64,1024]{1,0:T(8,128)(2,1)S(1)}, u32[]{:S(2)}, u32[]{:S(2)}) collective-permute-start(bf16[64,1024]{1,0:T(8,128)(2,1)} %get-tuple-element.25), channel_id=1, source_target_pairs={{0,128},{8,136},{16,144},{24,152},{32,160},{40,168},{48,176},{56,1... | collective-permute-start | bytes 393224 | tf_op jit(solution)/shard_map/ppermute | solution.py:29
  64.4 0.0 collective-permute-done.5
  64.4 5.5 %collective-permute-start.8 = (bf16[64,1024]{1,0:T(8,128)(2,1)}, bf16[64,1024]{1,0:T(8,128)(2,1)S(1)}, u32[]{:S(2)}, u32[]{:S(2)}) collective-permute-start(bf16[64,1024]{1,0:T(8,128)(2,1)} %get-tuple-element.25), channel_id=1, source_target_pairs={{0,192},{8,200},{16,208},{24,216},{32,224},{40,232},{48,240},{56,2... | collective-permute-start | bytes 393224 | tf_op jit(solution)/shard_map/ppermute | solution.py:29
  70.0 0.0 collective-permute-done.6
  70.0 4.5 %collective-permute-start.9 = (bf16[128,1024]{1,0:T(8,128)(2,1)}, bf16[128,1024]{1,0:T(8,128)(2,1)S(1)}, u32[]{:S(2)}, u32[]{:S(2)}) collective-permute-start(bf16[128,1024]{1,0:T(8,128)(2,1)} %get-tuple-element.26), channel_id=1, source_target_pairs={{0,64},{8,72},{16,80},{24,88},{32,96},{40,104},{48,112},{56,120},{... | collective-permute-start | bytes 786440 | tf_op jit(solution)/shard_map/ppermute | solution.py:29
  74.6 0.0 collective-permute-done.7
  74.6 6.4 %collective-permute-start.12 = (bf16[256,1024]{1,0:T(8,128)(2,1)}, bf16[256,1024]{1,0:T(8,128)(2,1)}, u32[]{:S(2)}, u32[]{:S(2)}) collective-permute-start(bf16[256,1024]{1,0:T(8,128)(2,1)} %get-tuple-element.28.refs_4_.refs_5_), channel_id=1, source_target_pairs={{0,8},{8,0},{16,24},{24,16},{32,40},{40,32},{48,56},{56,48},{64,72... | collective-permute-start | bytes 1572872 | tf_op jit(solution)/shard_map/ppermute | solution.py:29
  81.0 0.0 collective-permute-done.8
  81.0 0.0 collective-permute-done.9
  81.0 6.4 %collective-permute-start.10 = (bf16[384,1024]{1,0:T(8,128)(2,1)S(1)}, bf16[384,1024]{1,0:T(8,128)(2,1)S(1)}, u32[]{:S(2)}, u32[]{:S(2)}) collective-permute-start(bf16[384,1024]{1,0:T(8,128)(2,1)S(1)} %constant_dynamic-update-slice_fusion.refs_2_.refs_3_), channel_id=1, source_target_pairs={{0,8},{8,0},{16,24},{24,16},{32,40},{40,32},{48,56},{56,48},{64,72... | collective-permute-start | bytes 2359304 | tf_op jit(solution)/shard_map/ppermute | solution.py:29
  87.5 0.0 copy-done
  87.5 0.0 copy-start.1
  87.5 1.2 copy-done.1
  88.8 0.0 copy-start.2
  88.8 1.2 copy-done.2
  90.0 12.0 %shard_map.37 = (f32[4,128,1024]{2,1,0:T(8,128)S(1)}, f32[4,1,1024]{2,1,0:T(1,128)S(1)}, f32[4,1,1024]{2,1,0:T(1,128)S(1)}) custom-call(f32[1]{0:T(128)} %bitcast.refs_0_, bf16[1024,512]{1,0:T(8,128)(2,1)S(1)} %copy-done, bf16[1024,512]{1,0:T(8,128)(2,1)S(1)} %copy-done.1, bf16[1024,512]{1,0:T(8,128)(2,1)S(1)} %copy-done.2), custom_call_target="tpu_custom_call" | custom-call | flops 2147483648 | bytes 5242880 | tf_op jit(solution)/shard_map/pallas_call | solution.py:188
  102.0 0.0 copy-start.4
  102.0 1.3 %copy-done.4 = f32[4,128,1024]{2,1,0:T(8,128)} copy-done((f32[4,128,1024]{2,1,0:T(8,128)}, f32[4,128,1024]{2,1,0:T(8,128)S(1)}, u32[]{:S(2)}) %copy-start.4) | copy-done | bytes 2097176
  103.4 0.0 collective-permute-done.13.refs_8_.refs_9_
  103.4 0.0 collective-permute-done.12.refs_6_.refs_7_
  103.4 0.0 collective-permute-done.11.refs_2_.refs_3_
  103.4 0.0 copy-done.3
  103.4 13.2 %shard_map.38 = (f32[4,128,1024]{2,1,0:T(8,128)S(1)}, f32[4,1,1024]{2,1,0:T(1,128)S(1)}, f32[4,1,1024]{2,1,0:T(1,128)S(1)}) custom-call(f32[1]{0:T(128)} %bitcast.refs_0_, bf16[1024,512]{1,0:T(8,128)(2,1)S(1)} %copy-done, bf16[512,1024]{1,0:T(8,128)(2,1)} %collective-permute-done.11.refs_2_.refs_3_, ...), custom_call_target="tpu_custom_call" | custom-call | flops 2684354560 | bytes 5767168 | tf_op jit(solution)/shard_map/pallas_call | solution.py:188
  116.6 7.0 %shard_map.39 = (f32[4,128,1024]{2,1,0:T(8,128)S(1)}, f32[4,1,1024]{2,1,0:T(1,128)S(1)}, f32[4,1,1024]{2,1,0:T(1,128)S(1)}) custom-call(f32[1]{0:T(128)} %bitcast.refs_0_, bf16[1024,512]{1,0:T(8,128)(2,1)S(1)} %copy-done, bf16[384,1024]{1,0:T(8,128)(2,1)S(1)} %constant_dynamic-update-slice_fusion.refs_2_.refs_3_, ...), custom_call_target="tpu_custom_call" | custom-call | flops 805306368 | bytes 3932160 | tf_op jit(solution)/shard_map/pallas_call | solution.py:188
  123.6 0.0 collective-permute-done.10.refs_2_.refs_3_
  123.6 8.0 %shard_map.40 = bf16[1024,512]{1,0:T(8,128)(2,1)} custom-call(f32[1]{0:T(128)} %bitcast.refs_0_, bf16[1024,512]{1,0:T(8,128)(2,1)S(1)} %copy-done, bf16[384,1024]{1,0:T(8,128)(2,1)S(1)} %collective-permute-done.10.refs_2_.refs_3_, bf16[384,1024]{1,0:T(8,128)(2,1)S(1)} %collective-permute-done.10.refs_2_.refs_3_, ...), custom_call_target="tpu_custom_call" | custom-call | flops 805306368 | bytes 3932160 | tf_op jit(solution)/shard_map/pallas_call | solution.py:188
  (9 shorter events, 0.1 us)
Async XLA Ops:
  0.0 87.5 %copy-start = (bf16[1024,512]{1,0:T(8,128)(2,1)S(1)}, bf16[1024,512]{1,0:T(8,128)(2,1)}, u32[]{:S(2)}) copy-start(bf16[1024,512]{1,0:T(8,128)(2,1)} %refs_1_.7) | copy-start | bytes 3145732
  3.9 21.2 %collective-permute-start = (bf16[128,1024]{1,0:T(8,128)(2,1)}, bf16[128,1024]{1,0:T(8,128)(2,1)S(1)}, u32[]{:S(2)}, u32[]{:S(2)}) collective-permute-start(bf16[128,1024]{1,0:T(8,128)(2,1)} %get-tuple-element.23), channel_id=1, source_target_pairs={{0,16},{8,24},{16,0},{24,8},{32,48},{40,56},{48,32},{56,40},{64,80... | collective-permute-start | bytes 786440 | tf_op jit(solution)/shard_map/ppermute | solution.py:29
  7.6 10.0 %collective-permute-start.1 = (bf16[64,1024]{1,0:T(8,128)(2,1)}, bf16[64,1024]{1,0:T(8,128)(2,1)S(1)}, u32[]{:S(2)}, u32[]{:S(2)}) collective-permute-start(bf16[64,1024]{1,0:T(8,128)(2,1)} %get-tuple-element.22.own_ref), channel_id=1, source_target_pairs={{0,32},{8,40},{16,48},{24,56},{32,0},{40,8},{48,16},{56,24},{64,96... | collective-permute-start | bytes 393224 | tf_op jit(solution)/shard_map/ppermute | solution.py:29
  9.6 15.4 %collective-permute-start.2 = (bf16[64,1024]{1,0:T(8,128)(2,1)}, bf16[64,1024]{1,0:T(8,128)(2,1)S(1)}, u32[]{:S(2)}, u32[]{:S(2)}) collective-permute-start(bf16[64,1024]{1,0:T(8,128)(2,1)} %get-tuple-element.22.own_ref), channel_id=1, source_target_pairs={{0,48},{8,56},{16,32},{24,40},{32,16},{40,24},{48,0},{56,8},{64,11... | collective-permute-start | bytes 393224 | tf_op jit(solution)/shard_map/ppermute | solution.py:29
  17.6 7.5 %copy-start.6 = (bf16[64,1024]{1,0:T(8,128)(2,1)}, bf16[64,1024]{1,0:T(8,128)(2,1)S(1)}, u32[]{:S(2)}) copy-start(bf16[64,1024]{1,0:T(8,128)(2,1)S(1)} %collective-permute-done.1.b_ref) | copy-start | bytes 393220
  25.0 0.7 copy-start.7
  25.7 0.7 copy-start.5
  28.8 27.8 %collective-permute-start.3 = (bf16[32,1024]{1,0:T(8,128)(2,1)}, bf16[32,1024]{1,0:T(8,128)(2,1)S(1)}, u32[]{:S(2)}, u32[]{:S(2)}) collective-permute-start(bf16[32,1024]{1,0:T(8,128)(2,1)} %get-tuple-element.24), channel_id=1, source_target_pairs={{0,256},{8,264},{16,272},{24,280},{32,288},{40,296},{48,304},{56,3... | collective-permute-start | bytes 196616 | tf_op jit(solution)/shard_map/ppermute | solution.py:29
  39.4 64.0 %collective-permute-start.11 = (bf16[512,1024]{1,0:T(8,128)(2,1)}, bf16[512,1024]{1,0:T(8,128)(2,1)}, u32[]{:S(2)}, u32[]{:S(2)}) collective-permute-start(bf16[512,1024]{1,0:T(8,128)(2,1)} %get-tuple-element.27), channel_id=1, source_target_pairs={{0,8},{8,0},{16,24},{24,16},{32,40},{40,32},{48,56},{56,48},{64,72... | collective-permute-start | bytes 3145736 | tf_op jit(solution)/shard_map/ppermute | solution.py:29
  45.4 57.9 %collective-permute-start.13 = (bf16[256,1024]{1,0:T(8,128)(2,1)}, bf16[256,1024]{1,0:T(8,128)(2,1)S(1)}, u32[]{:S(2)}, u32[]{:S(2)}) collective-permute-start(bf16[256,1024]{1,0:T(8,128)(2,1)} %get-tuple-element.29), channel_id=1, source_target_pairs={{8,16},{16,8},{24,32},{32,24},{40,48},{48,40},{56,64},{64,56},{72,... | collective-permute-start | bytes 1572872 | tf_op jit(solution)/shard_map/ppermute | solution.py:29
  49.4 10.3 %collective-permute-start.4 = (bf16[32,1024]{1,0:T(8,128)(2,1)}, bf16[32,1024]{1,0:T(8,128)(2,1)S(1)}, u32[]{:S(2)}, u32[]{:S(2)}) collective-permute-start(bf16[32,1024]{1,0:T(8,128)(2,1)} %get-tuple-element.24), channel_id=1, source_target_pairs={{0,320},{8,328},{16,336},{24,344},{32,352},{40,360},{48,368},{56,3... | collective-permute-start | bytes 196616 | tf_op jit(solution)/shard_map/ppermute | solution.py:29
  51.3 13.1 %collective-permute-start.5 = (bf16[32,1024]{1,0:T(8,128)(2,1)}, bf16[32,1024]{1,0:T(8,128)(2,1)S(1)}, u32[]{:S(2)}, u32[]{:S(2)}) collective-permute-start(bf16[32,1024]{1,0:T(8,128)(2,1)} %get-tuple-element.24), channel_id=1, source_target_pairs={{0,384},{8,392},{16,400},{24,408},{32,416},{40,424},{48,432},{56,4... | collective-permute-start | bytes 196616 | tf_op jit(solution)/shard_map/ppermute | solution.py:29
  56.6 13.4 %collective-permute-start.6 = (bf16[32,1024]{1,0:T(8,128)(2,1)}, bf16[32,1024]{1,0:T(8,128)(2,1)S(1)}, u32[]{:S(2)}, u32[]{:S(2)}) collective-permute-start(bf16[32,1024]{1,0:T(8,128)(2,1)} %get-tuple-element.24), channel_id=1, source_target_pairs={{0,448},{8,456},{16,464},{24,472},{32,480},{40,488},{48,496},{56,5... | collective-permute-start | bytes 196616 | tf_op jit(solution)/shard_map/ppermute | solution.py:29
  59.6 14.9 %collective-permute-start.7 = (bf16[64,1024]{1,0:T(8,128)(2,1)}, bf16[64,1024]{1,0:T(8,128)(2,1)S(1)}, u32[]{:S(2)}, u32[]{:S(2)}) collective-permute-start(bf16[64,1024]{1,0:T(8,128)(2,1)} %get-tuple-element.25), channel_id=1, source_target_pairs={{0,128},{8,136},{16,144},{24,152},{32,160},{40,168},{48,176},{56,1... | collective-permute-start | bytes 393224 | tf_op jit(solution)/shard_map/ppermute | solution.py:29
  64.4 16.6 %collective-permute-start.8 = (bf16[64,1024]{1,0:T(8,128)(2,1)}, bf16[64,1024]{1,0:T(8,128)(2,1)S(1)}, u32[]{:S(2)}, u32[]{:S(2)}) collective-permute-start(bf16[64,1024]{1,0:T(8,128)(2,1)} %get-tuple-element.25), channel_id=1, source_target_pairs={{0,192},{8,200},{16,208},{24,216},{32,224},{40,232},{48,240},{56,2... | collective-permute-start | bytes 393224 | tf_op jit(solution)/shard_map/ppermute | solution.py:29
  70.0 11.0 %collective-permute-start.9 = (bf16[128,1024]{1,0:T(8,128)(2,1)}, bf16[128,1024]{1,0:T(8,128)(2,1)S(1)}, u32[]{:S(2)}, u32[]{:S(2)}) collective-permute-start(bf16[128,1024]{1,0:T(8,128)(2,1)} %get-tuple-element.26), channel_id=1, source_target_pairs={{0,64},{8,72},{16,80},{24,88},{32,96},{40,104},{48,112},{56,120},{... | collective-permute-start | bytes 786440 | tf_op jit(solution)/shard_map/ppermute | solution.py:29
  74.6 28.8 %collective-permute-start.12 = (bf16[256,1024]{1,0:T(8,128)(2,1)}, bf16[256,1024]{1,0:T(8,128)(2,1)}, u32[]{:S(2)}, u32[]{:S(2)}) collective-permute-start(bf16[256,1024]{1,0:T(8,128)(2,1)} %get-tuple-element.28.refs_4_.refs_5_), channel_id=1, source_target_pairs={{0,8},{8,0},{16,24},{24,16},{32,40},{40,32},{48,56},{56,48},{64,72... | collective-permute-start | bytes 1572872 | tf_op jit(solution)/shard_map/ppermute | solution.py:29
  81.0 42.6 %collective-permute-start.10 = (bf16[384,1024]{1,0:T(8,128)(2,1)S(1)}, bf16[384,1024]{1,0:T(8,128)(2,1)S(1)}, u32[]{:S(2)}, u32[]{:S(2)}) collective-permute-start(bf16[384,1024]{1,0:T(8,128)(2,1)S(1)} %constant_dynamic-update-slice_fusion.refs_2_.refs_3_), channel_id=1, source_target_pairs={{0,8},{8,0},{16,24},{24,16},{32,40},{40,32},{48,56},{56,48},{64,72... | collective-permute-start | bytes 2359304 | tf_op jit(solution)/shard_map/ppermute | solution.py:29
  87.5 1.2 copy-start.1
  88.8 1.2 copy-start.2
  90.0 13.4 %copy-start.3 = (bf16[256,1024]{1,0:T(8,128)(2,1)S(1)}, bf16[256,1024]{1,0:T(8,128)(2,1)}, u32[]{:S(2)}) copy-start(bf16[256,1024]{1,0:T(8,128)(2,1)} %get-tuple-element.28.refs_4_.refs_5_) | copy-start | bytes 1572868
  102.0 1.3 %copy-start.4 = (f32[4,128,1024]{2,1,0:T(8,128)}, f32[4,128,1024]{2,1,0:T(8,128)S(1)}, u32[]{:S(2)}) copy-start(f32[4,128,1024]{2,1,0:T(8,128)S(1)} %get-tuple-element.30.refs_10_) | copy-start | bytes 6291460

commit v2 on v1

v2 whole, which is shorter than its diff:
```python
import functools

import jax
import jax.numpy as jnp
from jax import lax
from jax.experimental import pallas as pl
from jax.experimental.pallas import tpu as pltpu
from jax.sharding import PartitionSpec as P


HD = 128
HEADS_DEV = 4
WIDTH = HEADS_DEV * HD
TOK = 1024
POOL = 256
EDGE = 256
N_CTX = 64
SCALE_LOG2 = (HD**-0.5) * 1.4426950408889634
Q_TILE = 128
TOTAL_LIMIT = 2.0**100
VMEM_LIMIT = 24 * 2**20


def swap(value, partner):
    pairs = []
    for source in range(N_CTX):
        z, y, core = source // 8, (source // 2) % 4, source % 2
        target = partner(z, y, core)
        if target is not None:
            pairs.append((source, target))
    return lax.ppermute(value, "ctx", pairs)


def index_of(z, y, core):
    return (z * 4 + y) * 2 + core


def other_core(z, y, core):
    return index_of(z, y, 1 - core)


def along_y(bits):
    return lambda z, y, core: index_of(z, y ^ bits, core)


def along_z(bits):
    return lambda z, y, core: index_of(z ^ bits, y, core)


def beside(z, y, core):
    here = index_of(z, y, core)
    there = here + 1 if core else here - 1
    return there if 0 <= there < N_CTX else None


def pooling_matrix(rows, group):
    out = lax.broadcasted_iota(jnp.int32, (rows // group, rows), 0)
    src = lax.broadcasted_iota(jnp.int32, (rows // group, rows), 1)
    return (src // group == out).astype(jnp.float32).astype(jnp.bfloat16)


def pool(value, group, matrix):
    total = jnp.dot(matrix, value, preferred_element_type=jnp.float32)
    return (total / jnp.float32(group**0.5)).astype(jnp.bfloat16)


def first_kernel(core_ref, k_ref, v_ref, near_ref, far_ref, one_ref, two_ref):
    core = core_ref[0]
    by4 = pooling_matrix(256, 4)
    by2 = pooling_matrix(256, 2)
    for side, ref in enumerate((k_ref, v_ref)):
        cols = pl.ds(side * WIDTH, WIDTH)
        for part in range(4):
            near_ref[pl.ds(part * 64, 64), cols] = pool(ref[pl.ds(part * 256, 256), :], 4, by4)
        one = pool(near_ref[pl.ds(0, 256), cols], 2, by2)
        one_ref[:, cols] = one
        two_ref[:, cols] = pool(one, 2, by2[:64, :128])
        last = pl.multiple_of((1 - core) * (TOK - EDGE), EDGE)
        near_ref[pl.ds(POOL, EDGE), cols] = ref[pl.ds(last, EDGE), :]
        first = pl.multiple_of(core * (TOK - EDGE), EDGE)
        far_ref[:, cols] = ref[pl.ds(first, EDGE), :]


def first_pools(core, keys, values):
    shape = lambda rows: jax.ShapeDtypeStruct((rows, 2 * WIDTH), jnp.bfloat16)
    vmem = pl.BlockSpec(memory_space=pltpu.VMEM)
    return pl.pallas_call(
        first_kernel,
        in_specs=[pl.BlockSpec(memory_space=pltpu.SMEM), vmem, vmem],
        out_specs=[vmem] * 4,
        out_shape=[shape(512), shape(256), shape(128), shape(64)],
        compiler_params=pltpu.CompilerParams(vmem_limit_bytes=VMEM_LIMIT),
        cost_estimate=pl.CostEstimate(flops=10**8, bytes_accessed=4 * 2**20, transcendentals=0),
        name="first_pools",
    )(core, keys, values)


def small_call(kernel, rows, *operands):
    vmem = pl.BlockSpec(memory_space=pltpu.VMEM)
    return pl.pallas_call(
        kernel,
        in_specs=[vmem] * len(operands),
        out_specs=[vmem] * len(rows),
        out_shape=[jax.ShapeDtypeStruct((r, 2 * WIDTH), jnp.bfloat16) for r in rows],
        compiler_params=pltpu.CompilerParams(vmem_limit_bytes=VMEM_LIMIT),
        cost_estimate=pl.CostEstimate(flops=10**8, bytes_accessed=2**20, transcendentals=0),
    )(*operands)


def plane_kernel(own_ref, a_ref, b_ref, c_ref, got_ref, three_ref, four_ref):
    by2 = pooling_matrix(256, 2)
    a, b, c = a_ref[...], b_ref[...], c_ref[...]
    got_ref[pl.ds(0, 128), :] = a
    got_ref[pl.ds(128, 64), :] = b
    got_ref[pl.ds(192, 64), :] = c
    rows = jnp.concatenate([own_ref[...], pool(a, 2, by2[:64, :128]), b, c], axis=0)
    three = pool(rows, 2, by2)
    three_ref[...] = three
    four_ref[...] = pool(three, 2, by2[:64, :128])


def pair_kernel(four_ref, three_ref, fours_ref, fives_ref):
    by2 = pooling_matrix(128, 2)
    fours = jnp.concatenate([four_ref[...], pool(three_ref[...], 2, by2)], axis=0)
    fours_ref[...] = fours
    fives_ref[...] = pool(fours, 2, by2)


def times(a, b, dims):
    return lax.dot_general(a, b, (dims, ((), ())), preferred_element_type=jnp.float32)


def attend_kernel(plan, carried, final, *refs):
    refs = list(refs)
    bias = refs.pop(0)[0]
    q_ref = refs.pop(0)
    arrays = [refs.pop(0) for _ in range(1 + max(max(p[0], p[1]) for p in plan))]
    if carried:
        acc_in, m_in, l_in = refs.pop(0), refs.pop(0), refs.pop(0)

    def one_head(h, _):
        def lanes(first):
            return pl.ds(pl.multiple_of(first + h * HD, HD), HD)

        def put(rows, acc, peak, total):
            if final:
                refs[0][rows, lanes(0)] = (acc * (1.0 / total)).astype(jnp.bfloat16).T
            else:
                refs[0][h, :, rows] = acc
                refs[1][h, :, rows] = peak
                refs[2][h, :, rows] = total

        pieces = []
        for k_at, v_at, first, count, v_lane, masked in plan:
            rows = pl.ds(first, count)
            pieces.append((arrays[k_at][rows, lanes(0)], arrays[v_at][rows, lanes(v_lane)].T, masked))

        query = q_ref[:, lanes(0)]
        acc, total = 0.0, 0.0
        if carried:
            acc, peak, total = acc_in[h], m_in[h], l_in[h]
            parts = pieces
        else:
            (k, v, masked), *rest = pieces
            parts = [(k[:256], v[:, :256], masked), (k[256:], v[:, 256:], masked), *rest]
            peak = None
        for k, v, masked in parts:
            s = times(k, query, ((1,), (1,)))
            if masked:
                s = s + bias
            if peak is None:
                peak = jnp.max(s, axis=0, keepdims=True)
            p = jnp.exp2((s - peak) * SCALE_LOG2)
            total = total + jnp.sum(p, axis=0, keepdims=True)
            acc = acc + times(v, p.astype(jnp.bfloat16), ((1,), (0,)))
        put(pl.ds(0, TOK), acc, peak, total)

        @pl.when(jnp.logical_not(jnp.max(total) < TOTAL_LIMIT))
        def _():
            def one_tile(tile, _):
                rows = pl.ds(pl.multiple_of(tile * Q_TILE, Q_TILE), Q_TILE)
                query = q_ref[rows, lanes(0)]
                scores = []
                for k, _, masked in pieces:
                    s = times(k, query, ((1,), (1,)))
                    scores.append(s + bias if masked else s)
                peaks = [jnp.max(s, axis=0, keepdims=True) for s in scores]
                acc, total = 0.0, 0.0
                if carried:
                    before = m_in[h, :, rows]
                    peaks.append(before)
                peak = functools.reduce(jnp.maximum, peaks)
                if carried:
                    fade = jnp.exp2((before - peak) * SCALE_LOG2)
                    acc, total = acc_in[h, :, rows] * fade, l_in[h, :, rows] * fade
                for s, (_, v, _) in zip(scores, pieces):
                    p = jnp.exp2((s - peak) * SCALE_LOG2)
                    total = total + jnp.sum(p, axis=0, keepdims=True)
                    acc = acc + times(v, p.astype(jnp.bfloat16), ((1,), (0,)))
                put(rows, acc, peak, total)
                return 0

            lax.fori_loop(0, TOK // Q_TILE, one_tile, 0)

        return 0

    lax.fori_loop(0, HEADS_DEV, one_head, 0)


def attend(bias, queries, arrays, plan, state, final):
    vmem = pl.BlockSpec(memory_space=pltpu.VMEM)
    operands = [bias, queries, *arrays, *state]
    count = sum(piece[3] for piece in plan)
    if final:
        out_specs = vmem
        out_shape = jax.ShapeDtypeStruct((TOK, WIDTH), jnp.bfloat16)
    else:
        out_specs = [vmem] * 3
        out_shape = [
            jax.ShapeDtypeStruct((HEADS_DEV, rows, TOK), jnp.float32) for rows in (HD, 1, 1)
        ]
    return pl.pallas_call(
        functools.partial(attend_kernel, plan, bool(state), final),
        in_specs=[pl.BlockSpec(memory_space=pltpu.SMEM)] + [vmem] * (len(operands) - 1),
        out_specs=out_specs,
        out_shape=out_shape,
        compiler_params=pltpu.CompilerParams(vmem_limit_bytes=VMEM_LIMIT),
        cost_estimate=pl.CostEstimate(
            flops=4 * TOK * count * WIDTH,
            bytes_accessed=2 * TOK * WIDTH + 4 * count * WIDTH + 4 * TOK * WIDTH,
            transcendentals=TOK * count * HEADS_DEV,
        ),
    )(*operands)


def on_device(queries, keys, values):
    position = lax.axis_index("ctx")
    core = (position % 2).astype(jnp.int32).reshape(1)
    outer = (position == 0) | (position == N_CTX - 1)
    bias = jnp.where(outer, jnp.float32(-1e30), jnp.float32(0)).reshape(1)

    near, far, one, two = first_pools(core, keys, values)
    got2 = swap(two, along_y(2))
    got1 = swap(one, along_y(1))
    got3 = swap(two, along_y(3))
    near_got = swap(near, other_core)
    own = (0, 1, 0, TOK, 0, False)
    state = attend(bias, queries, [keys, values], (own,), (), False)

    planes, three, four = small_call(plane_kernel, (256, 128, 64), two, got1, got2, got3)
    three_got = swap(three, along_z(1))
    far_got = swap(far, beside)
    planes_got = swap(planes, other_core)
    plan = ((0, 0, 0, 512, WIDTH, False), (1, 1, 0, 256, WIDTH, False))
    state = attend(bias, queries, [near_got, planes], plan, state, False)

    fours, fives = small_call(pair_kernel, (128, 64), four, three_got)
    fives5 = swap(fives, along_z(5))
    fours2 = swap(fours, along_z(2))
    fives6 = swap(fives, along_z(6))
    plan = ((0, 0, 0, 256, WIDTH, False), (1, 1, 0, 256, WIDTH, True))
    state = attend(bias, queries, [planes_got, far_got], plan, state, False)

    upper = jnp.concatenate([three_got, fives5, fives6, fours2], axis=0)
    upper_got = swap(upper, other_core)
    plan = ((0, 0, 0, 384, WIDTH, False),)
    state = attend(bias, queries, [upper], plan, state, False)
    return attend(bias, queries, [upper_got], plan, state, True)


def solution(mesh):
    return jax.shard_map(
        on_device,
        mesh=mesh,
        in_specs=(P("ctx", "head"), P("ctx", "head"), P("ctx", "head")),
        out_specs=P("ctx", "head"),
        check_vma=False,
    )
```

time: 132 us -> 120 us (0.909)
  the two profiles are of different devices: /device:TPU:53 before, /device:TPU:6 now
where the time goes in v2:
time: 120 us; the launch traced here: 119 us
  Pallas kernels  45.7 us (38%)
  starting transfers between devices  43.4 us (36%)
  waiting for transfers between devices  26 us (22%)
  local copies, waits for them, and re-layouts  3.73 us (3%)
    ppermute x11, starting transfers between devices, swap(): return lax.ppermute(value, 'ctx', pairs)  43.4 us
    pallas_call x5, Pallas kernels, attend(): pl.pallas_call(functools.partial(attend_kernel, plan, bool(state), final)...  42 us
    ppermute x11, waiting for transfers between devices, swap(): return lax.ppermute(value, 'ctx', pairs)  26 us
    unnamed x13, local copies, waits for them, and re-layouts  3.71 us
  transfers between devices with their start and end apart: 11, of which 6 were waited for; matrix products, arithmetic and copies ran while one was open for 0% of the time, Pallas kernels for 32%

profile of v2, /device:TPU:6, one launch (start us, length us, event | category | flops | bytes accessed | tf_op | source)
XLA Modules:
  0.0 119.0 jit_solution(10946123253128809740)
XLA Ops:
  0.0 0.0 copy-start.1
  0.0 1.2 %copy-done.1 = bf16[1024,512]{1,0:T(8,128)(2,1)S(1)} copy-done((bf16[1024,512]{1,0:T(8,128)(2,1)S(1)}, bf16[1024,512]{1,0:T(8,128)(2,1)}, u32[]{:S(2)}) %copy-start.1) | copy-done | bytes 1048600
  1.2 0.0 copy-start.3
  1.2 1.2 %copy-done.3 = bf16[1024,512]{1,0:T(8,128)(2,1)S(1)} copy-done((bf16[1024,512]{1,0:T(8,128)(2,1)S(1)}, bf16[1024,512]{1,0:T(8,128)(2,1)}, u32[]{:S(2)}) %copy-start.3) | copy-done | bytes 1048600
  2.5 0.0 copy-start
  2.5 0.0 copy-start.2
  2.5 2.1 %first_pools.1 = (bf16[512,1024]{1,0:T(8,128)(2,1)}, bf16[256,1024]{1,0:T(8,128)(2,1)}, bf16[128,1024]{1,0:T(8,128)(2,1)S(1)}, bf16[64,1024]{1,0:T(8,128)(2,1)S(1)}) custom-call(s32[1]{0:T(128)} %bitcast.1.core_ref, bf16[1024,512]{1,0:T(8,128)(2,1)S(1)} %copy-done.1, bf16[1024,512]{1,0:T(8,128)(2,1)S(1)} %copy-done.3), custom_call_target="tpu_custom_call" | custom-call | flops 100000000 | bytes 4194304 | tf_op jit(solution)/shard_map/first_pools/pallas_call | solution.py:87
  4.6 4.5 %collective-permute-start = (bf16[128,1024]{1,0:T(8,128)(2,1)S(1)}, bf16[128,1024]{1,0:T(8,128)(2,1)S(1)}, u32[]{:S(2)}, u32[]{:S(2)}) collective-permute-start(bf16[128,1024]{1,0:T(8,128)(2,1)S(1)} %get-tuple-element.27), channel_id=1, source_target_pairs={{0,16},{8,24},{16,0},{24,8},{32,48},{40,56},{48,32},{56,40},{64,80... | collective-permute-start | bytes 786440 | tf_op jit(solution)/shard_map/ppermute | solution.py:31
  9.1 5.9 %collective-permute-start.1 = (bf16[64,1024]{1,0:T(8,128)(2,1)S(1)}, bf16[64,1024]{1,0:T(8,128)(2,1)S(1)}, u32[]{:S(2)}, u32[]{:S(2)}) collective-permute-start(bf16[64,1024]{1,0:T(8,128)(2,1)S(1)} %get-tuple-element.26.own_ref), channel_id=1, source_target_pairs={{0,32},{8,40},{16,48},{24,56},{32,0},{40,8},{48,16},{56,24},{64,96... | collective-permute-start | bytes 393224 | tf_op jit(solution)/shard_map/ppermute | solution.py:31
  15.0 1.9 %collective-permute-start.2 = (bf16[64,1024]{1,0:T(8,128)(2,1)S(1)}, bf16[64,1024]{1,0:T(8,128)(2,1)S(1)}, u32[]{:S(2)}, u32[]{:S(2)}) collective-permute-start(bf16[64,1024]{1,0:T(8,128)(2,1)S(1)} %get-tuple-element.26.own_ref), channel_id=1, source_target_pairs={{0,48},{8,56},{16,32},{24,40},{32,16},{40,24},{48,0},{56,8},{64,11... | collective-permute-start | bytes 393224 | tf_op jit(solution)/shard_map/ppermute | solution.py:31
  17.0 7.7 %collective-permute-done.1.b_ref = bf16[64,1024]{1,0:T(8,128)(2,1)S(1)} collective-permute-done((bf16[64,1024]{1,0:T(8,128)(2,1)S(1)}, bf16[64,1024]{1,0:T(8,128)(2,1)S(1)}, u32[]{:S(2)}, u32[]{:S(2)}) %collective-permute-start.1) | collective-permute-done | bytes 131104 | tf_op jit(solution)/shard_map/ppermute | solution.py:31
  24.6 5.6 %collective-permute-done.2.c_ref = bf16[64,1024]{1,0:T(8,128)(2,1)S(1)} collective-permute-done((bf16[64,1024]{1,0:T(8,128)(2,1)S(1)}, bf16[64,1024]{1,0:T(8,128)(2,1)S(1)}, u32[]{:S(2)}, u32[]{:S(2)}) %collective-permute-start.2) | collective-permute-done | bytes 131104 | tf_op jit(solution)/shard_map/ppermute | solution.py:31
  30.3 0.0 collective-permute-done.a_ref
  30.3 1.2 %shard_map.37 = (bf16[256,1024]{1,0:T(8,128)(2,1)}, bf16[128,1024]{1,0:T(8,128)(2,1)S(1)}, bf16[64,1024]{1,0:T(8,128)(2,1)S(1)}) custom-call(bf16[64,1024]{1,0:T(8,128)(2,1)S(1)} %get-tuple-element.26.own_ref, bf16[128,1024]{1,0:T(8,128)(2,1)S(1)} %collective-permute-done.a_ref, bf16[64,1024]{1,0:T(8,128)(2,1)S(1)} %collective-permute-done.1.b_ref, ...), custom_call_target="tpu_custom_call" | custom-call | flops 100000000 | bytes 1048576 | tf_op jit(solution)/shard_map/pallas_call | solution.py:100
  31.5 4.3 %collective-permute-start.3 = (bf16[128,1024]{1,0:T(8,128)(2,1)S(1)}, bf16[128,1024]{1,0:T(8,128)(2,1)S(1)}, u32[]{:S(2)}, u32[]{:S(2)}) collective-permute-start(bf16[128,1024]{1,0:T(8,128)(2,1)S(1)} %get-tuple-element.28), channel_id=1, source_target_pairs={{0,64},{8,72},{16,80},{24,88},{32,96},{40,104},{48,112},{56,120},{... | collective-permute-start | bytes 786440 | tf_op jit(solution)/shard_map/ppermute | solution.py:31
  35.7 1.9 %collective-permute-start.10 = (bf16[512,1024]{1,0:T(8,128)(2,1)}, bf16[512,1024]{1,0:T(8,128)(2,1)}, u32[]{:S(2)}, u32[]{:S(2)}) collective-permute-start(bf16[512,1024]{1,0:T(8,128)(2,1)} %get-tuple-element.34), channel_id=1, source_target_pairs={{0,8},{8,0},{16,24},{24,16},{32,40},{40,32},{48,56},{56,48},{64,72... | collective-permute-start | bytes 3145736 | tf_op jit(solution)/shard_map/ppermute | solution.py:31
  37.7 2.4 %collective-permute-done.3.three_ref = bf16[128,1024]{1,0:T(8,128)(2,1)S(1)} collective-permute-done((bf16[128,1024]{1,0:T(8,128)(2,1)S(1)}, bf16[128,1024]{1,0:T(8,128)(2,1)S(1)}, u32[]{:S(2)}, u32[]{:S(2)}) %collective-permute-start.3) | collective-permute-done | bytes 262176 | tf_op jit(solution)/shard_map/ppermute | solution.py:31
  40.1 0.3 shard_map.38
  40.4 10.6 %collective-permute-start.4 = (bf16[64,1024]{1,0:T(8,128)(2,1)S(1)}, bf16[64,1024]{1,0:T(8,128)(2,1)S(1)}, u32[]{:S(2)}, u32[]{:S(2)}) collective-permute-start(bf16[64,1024]{1,0:T(8,128)(2,1)S(1)} %get-tuple-element.30), channel_id=1, source_target_pairs={{0,320},{8,328},{16,336},{24,344},{32,352},{40,360},{48,368},{56,3... | collective-permute-start | bytes 393224 | tf_op jit(solution)/shard_map/ppermute | solution.py:31
  51.0 1.9 %collective-permute-start.5 = (bf16[64,1024]{1,0:T(8,128)(2,1)S(1)}, bf16[64,1024]{1,0:T(8,128)(2,1)S(1)}, u32[]{:S(2)}, u32[]{:S(2)}) collective-permute-start(bf16[64,1024]{1,0:T(8,128)(2,1)S(1)} %get-tuple-element.30), channel_id=1, source_target_pairs={{0,384},{8,392},{16,400},{24,408},{32,416},{40,424},{48,432},{56,4... | collective-permute-start | bytes 393224 | tf_op jit(solution)/shard_map/ppermute | solution.py:31
  52.9 4.3 %collective-permute-start.6 = (bf16[128,1024]{1,0:T(8,128)(2,1)S(1)}, bf16[128,1024]{1,0:T(8,128)(2,1)S(1)}, u32[]{:S(2)}, u32[]{:S(2)}) collective-permute-start(bf16[128,1024]{1,0:T(8,128)(2,1)S(1)} %get-tuple-element.31), channel_id=1, source_target_pairs={{0,128},{8,136},{16,144},{24,152},{32,160},{40,168},{48,176},{56,1... | collective-permute-start | bytes 786440 | tf_op jit(solution)/shard_map/ppermute | solution.py:31
  57.2 0.7 collective-permute-done.4
  58.0 2.1 %collective-permute-done.5 = bf16[64,1024]{1,0:T(8,128)(2,1)S(1)} collective-permute-done((bf16[64,1024]{1,0:T(8,128)(2,1)S(1)}, bf16[64,1024]{1,0:T(8,128)(2,1)S(1)}, u32[]{:S(2)}, u32[]{:S(2)}) %collective-permute-start.5) | collective-permute-done | bytes 131104 | tf_op jit(solution)/shard_map/ppermute | solution.py:31
  60.1 7.5 %collective-permute-done.6 = bf16[128,1024]{1,0:T(8,128)(2,1)S(1)} collective-permute-done((bf16[128,1024]{1,0:T(8,128)(2,1)S(1)}, bf16[128,1024]{1,0:T(8,128)(2,1)S(1)}, u32[]{:S(2)}, u32[]{:S(2)}) %collective-permute-start.6) | collective-permute-done | bytes 262176 | tf_op jit(solution)/shard_map/ppermute | solution.py:31
  67.5 1.9 %collective-permute-start.7 = (bf16[384,1024]{1,0:T(8,128)(2,1)S(1)}, bf16[384,1024]{1,0:T(8,128)(2,1)}, u32[]{:S(2)}, u32[]{:S(2)}) collective-permute-start(bf16[384,1024]{1,0:T(8,128)(2,1)S(1)} %constant_dynamic-update-slice_fusion.refs_2_), channel_id=1, source_target_pairs={{0,8},{8,0},{16,24},{24,16},{32,40},{40,32},{48,56},{56,48},{64,72... | collective-permute-start | bytes 2359304 | tf_op jit(solution)/shard_map/ppermute | solution.py:31
  69.5 0.7 collective-permute-start.9
  70.2 5.5 %collective-permute-start.8 = (bf16[256,1024]{1,0:T(8,128)(2,1)}, bf16[256,1024]{1,0:T(8,128)(2,1)}, u32[]{:S(2)}, u32[]{:S(2)}) collective-permute-start(bf16[256,1024]{1,0:T(8,128)(2,1)} %get-tuple-element.32.refs_3_), channel_id=1, source_target_pairs={{0,8},{8,0},{16,24},{24,16},{32,40},{40,32},{48,56},{56,48},{64,72... | collective-permute-start | bytes 1572872 | tf_op jit(solution)/shard_map/ppermute | solution.py:31
  75.7 0.0 copy-done
  75.7 0.0 copy-done.2
  75.7 0.0 copy-start.4
  75.7 1.2 %copy-done.4 = bf16[1024,512]{1,0:T(8,128)(2,1)S(1)} copy-done((bf16[1024,512]{1,0:T(8,128)(2,1)S(1)}, bf16[1024,512]{1,0:T(8,128)(2,1)}, u32[]{:S(2)}) %copy-start.4) | copy-done | bytes 1048600
  76.9 24.5 %shard_map.39 = (f32[4,128,1024]{2,1,0:T(8,128)S(1)}, f32[4,1,1024]{2,1,0:T(1,128)S(1)}, f32[4,1,1024]{2,1,0:T(1,128)S(1)}) custom-call(f32[1]{0:T(128)} %bitcast.refs_0_, bf16[1024,512]{1,0:T(8,128)(2,1)S(1)} %copy-done, bf16[1024,512]{1,0:T(8,128)(2,1)S(1)} %copy-done.2, bf16[1024,512]{1,0:T(8,128)(2,1)S(1)} %copy-done.4), custom_call_target="tpu_custom_call" | custom-call | flops 2147483648 | bytes 5242880 | tf_op jit(solution)/shard_map/pallas_call | solution.py:222
  101.4 0.0 collective-permute-done.10.refs_2_
  101.4 5.7 %shard_map.40 = (f32[4,128,1024]{2,1,0:T(8,128)S(1)}, f32[4,1,1024]{2,1,0:T(1,128)S(1)}, f32[4,1,1024]{2,1,0:T(1,128)S(1)}) custom-call(f32[1]{0:T(128)} %bitcast.refs_0_, bf16[1024,512]{1,0:T(8,128)(2,1)S(1)} %copy-done, bf16[512,1024]{1,0:T(8,128)(2,1)} %collective-permute-done.10.refs_2_, bf16[256,1024]{1,0:T(8,128)(2,1)} %get-tuple-element.32.refs_3_, ...), custom_call_target="tpu_custom_call" | custom-call | flops 1610612736 | bytes 4718592 | tf_op jit(solution)/shard_map/pallas_call | solution.py:222
  107.0 0.0 collective-permute-done.9.refs_3_
  107.1 0.0 collective-permute-done.8.refs_2_
  107.1 4.7 %shard_map.41 = (f32[4,128,1024]{2,1,0:T(8,128)S(1)}, f32[4,1,1024]{2,1,0:T(1,128)S(1)}, f32[4,1,1024]{2,1,0:T(1,128)S(1)}) custom-call(f32[1]{0:T(128)} %bitcast.refs_0_, bf16[1024,512]{1,0:T(8,128)(2,1)S(1)} %copy-done, bf16[256,1024]{1,0:T(8,128)(2,1)} %collective-permute-done.8.refs_2_, bf16[256,1024]{1,0:T(8,128)(2,1)S(1)} %collective-permute-done.9.refs_3_, ...), custom_call_target="tpu_custom_call" | custom-call | flops 1073741824 | bytes 4194304 | tf_op jit(solution)/shard_map/pallas_call | solution.py:222
  111.8 2.4 %shard_map.42 = (f32[4,128,1024]{2,1,0:T(8,128)S(1)}, f32[4,1,1024]{2,1,0:T(1,128)S(1)}, f32[4,1,1024]{2,1,0:T(1,128)S(1)}) custom-call(f32[1]{0:T(128)} %bitcast.refs_0_, bf16[1024,512]{1,0:T(8,128)(2,1)S(1)} %copy-done, bf16[384,1024]{1,0:T(8,128)(2,1)S(1)} %constant_dynamic-update-slice_fusion.refs_2_, f32[4,128,1024]{2,1,0:T(8,128)S(1)} %get-tuple-element.41.refs_3_, ...), custom_call_target="tpu_custom_call" | custom-call | flops 805306368 | bytes 3932160 | tf_op jit(solution)/shard_map/pallas_call | solution.py:222
  114.2 0.0 collective-permute-done.7.refs_2_
  114.2 4.8 %shard_map.43 = bf16[1024,512]{1,0:T(8,128)(2,1)} custom-call(f32[1]{0:T(128)} %bitcast.refs_0_, bf16[1024,512]{1,0:T(8,128)(2,1)S(1)} %copy-done, bf16[384,1024]{1,0:T(8,128)(2,1)} %collective-permute-done.7.refs_2_, f32[4,128,1024]{2,1,0:T(8,128)S(1)} %get-tuple-element.44.refs_3_, f32[4,1,1024]{2,1,0:T(1,128)S(1)} %get-tuple-element.45.refs_4_, ...), custom_call_target="tpu_custom_call" | custom-call | flops 805306368 | bytes 3932160 | tf_op jit(solution)/shard_map/pallas_call | solution.py:222
  (4 shorter events, 0.1 us)
Async XLA Ops:
  0.0 1.2 %copy-start.1 = (bf16[1024,512]{1,0:T(8,128)(2,1)S(1)}, bf16[1024,512]{1,0:T(8,128)(2,1)}, u32[]{:S(2)}) copy-start(bf16[1024,512]{1,0:T(8,128)(2,1)} %refs_2_.1) | copy-start | bytes 3145732
  1.2 1.2 %copy-start.3 = (bf16[1024,512]{1,0:T(8,128)(2,1)S(1)}, bf16[1024,512]{1,0:T(8,128)(2,1)}, u32[]{:S(2)}) copy-start(bf16[1024,512]{1,0:T(8,128)(2,1)} %refs_3_.1) | copy-start | bytes 3145732
  2.5 73.2 %copy-start = (bf16[1024,512]{1,0:T(8,128)(2,1)S(1)}, bf16[1024,512]{1,0:T(8,128)(2,1)}, u32[]{:S(2)}) copy-start(bf16[1024,512]{1,0:T(8,128)(2,1)} %refs_1_.9) | copy-start | bytes 3145732
  2.5 73.2 %copy-start.2 = (bf16[1024,512]{1,0:T(8,128)(2,1)S(1)}, bf16[1024,512]{1,0:T(8,128)(2,1)}, u32[]{:S(2)}) copy-start(bf16[1024,512]{1,0:T(8,128)(2,1)} %refs_2_.1) | copy-start | bytes 3145732
  4.6 25.7 %collective-permute-start = (bf16[128,1024]{1,0:T(8,128)(2,1)S(1)}, bf16[128,1024]{1,0:T(8,128)(2,1)S(1)}, u32[]{:S(2)}, u32[]{:S(2)}) collective-permute-start(bf16[128,1024]{1,0:T(8,128)(2,1)S(1)} %get-tuple-element.27), channel_id=1, source_target_pairs={{0,16},{8,24},{16,0},{24,8},{32,48},{40,56},{48,32},{56,40},{64,80... | collective-permute-start | bytes 786440 | tf_op jit(solution)/shard_map/ppermute | solution.py:31
  9.1 15.5 %collective-permute-start.1 = (bf16[64,1024]{1,0:T(8,128)(2,1)S(1)}, bf16[64,1024]{1,0:T(8,128)(2,1)S(1)}, u32[]{:S(2)}, u32[]{:S(2)}) collective-permute-start(bf16[64,1024]{1,0:T(8,128)(2,1)S(1)} %get-tuple-element.26.own_ref), channel_id=1, source_target_pairs={{0,32},{8,40},{16,48},{24,56},{32,0},{40,8},{48,16},{56,24},{64,96... | collective-permute-start | bytes 393224 | tf_op jit(solution)/shard_map/ppermute | solution.py:31
  15.0 15.2 %collective-permute-start.2 = (bf16[64,1024]{1,0:T(8,128)(2,1)S(1)}, bf16[64,1024]{1,0:T(8,128)(2,1)S(1)}, u32[]{:S(2)}, u32[]{:S(2)}) collective-permute-start(bf16[64,1024]{1,0:T(8,128)(2,1)S(1)} %get-tuple-element.26.own_ref), channel_id=1, source_target_pairs={{0,48},{8,56},{16,32},{24,40},{32,16},{40,24},{48,0},{56,8},{64,11... | collective-permute-start | bytes 393224 | tf_op jit(solution)/shard_map/ppermute | solution.py:31
  31.5 8.6 %collective-permute-start.3 = (bf16[128,1024]{1,0:T(8,128)(2,1)S(1)}, bf16[128,1024]{1,0:T(8,128)(2,1)S(1)}, u32[]{:S(2)}, u32[]{:S(2)}) collective-permute-start(bf16[128,1024]{1,0:T(8,128)(2,1)S(1)} %get-tuple-element.28), channel_id=1, source_target_pairs={{0,64},{8,72},{16,80},{24,88},{32,96},{40,104},{48,112},{56,120},{... | collective-permute-start | bytes 786440 | tf_op jit(solution)/shard_map/ppermute | solution.py:31
  35.7 65.6 %collective-permute-start.10 = (bf16[512,1024]{1,0:T(8,128)(2,1)}, bf16[512,1024]{1,0:T(8,128)(2,1)}, u32[]{:S(2)}, u32[]{:S(2)}) collective-permute-start(bf16[512,1024]{1,0:T(8,128)(2,1)} %get-tuple-element.34), channel_id=1, source_target_pairs={{0,8},{8,0},{16,24},{24,16},{32,40},{40,32},{48,56},{56,48},{64,72... | collective-permute-start | bytes 3145736 | tf_op jit(solution)/shard_map/ppermute | solution.py:31
  40.4 17.6 %collective-permute-start.4 = (bf16[64,1024]{1,0:T(8,128)(2,1)S(1)}, bf16[64,1024]{1,0:T(8,128)(2,1)S(1)}, u32[]{:S(2)}, u32[]{:S(2)}) collective-permute-start(bf16[64,1024]{1,0:T(8,128)(2,1)S(1)} %get-tuple-element.30), channel_id=1, source_target_pairs={{0,320},{8,328},{16,336},{24,344},{32,352},{40,360},{48,368},{56,3... | collective-permute-start | bytes 393224 | tf_op jit(solution)/shard_map/ppermute | solution.py:31
  51.0 9.1 %collective-permute-start.5 = (bf16[64,1024]{1,0:T(8,128)(2,1)S(1)}, bf16[64,1024]{1,0:T(8,128)(2,1)S(1)}, u32[]{:S(2)}, u32[]{:S(2)}) collective-permute-start(bf16[64,1024]{1,0:T(8,128)(2,1)S(1)} %get-tuple-element.30), channel_id=1, source_target_pairs={{0,384},{8,392},{16,400},{24,408},{32,416},{40,424},{48,432},{56,4... | collective-permute-start | bytes 393224 | tf_op jit(solution)/shard_map/ppermute | solution.py:31
  52.9 14.6 %collective-permute-start.6 = (bf16[128,1024]{1,0:T(8,128)(2,1)S(1)}, bf16[128,1024]{1,0:T(8,128)(2,1)S(1)}, u32[]{:S(2)}, u32[]{:S(2)}) collective-permute-start(bf16[128,1024]{1,0:T(8,128)(2,1)S(1)} %get-tuple-element.31), channel_id=1, source_target_pairs={{0,128},{8,136},{16,144},{24,152},{32,160},{40,168},{48,176},{56,1... | collective-permute-start | bytes 786440 | tf_op jit(solution)/shard_map/ppermute | solution.py:31
  67.5 46.7 %collective-permute-start.7 = (bf16[384,1024]{1,0:T(8,128)(2,1)S(1)}, bf16[384,1024]{1,0:T(8,128)(2,1)}, u32[]{:S(2)}, u32[]{:S(2)}) collective-permute-start(bf16[384,1024]{1,0:T(8,128)(2,1)S(1)} %constant_dynamic-update-slice_fusion.refs_2_), channel_id=1, source_target_pairs={{0,8},{8,0},{16,24},{24,16},{32,40},{40,32},{48,56},{56,48},{64,72... | collective-permute-start | bytes 2359304 | tf_op jit(solution)/shard_map/ppermute | solution.py:31
  69.5 37.6 %collective-permute-start.9 = (bf16[256,1024]{1,0:T(8,128)(2,1)}, bf16[256,1024]{1,0:T(8,128)(2,1)S(1)}, u32[]{:S(2)}, u32[]{:S(2)}) collective-permute-start(bf16[256,1024]{1,0:T(8,128)(2,1)} %get-tuple-element.33), channel_id=1, source_target_pairs={{8,16},{16,8},{24,32},{32,24},{40,48},{48,40},{56,64},{64,56},{72,... | collective-permute-start | bytes 1572872 | tf_op jit(solution)/shard_map/ppermute | solution.py:31
  70.2 36.9 %collective-permute-start.8 = (bf16[256,1024]{1,0:T(8,128)(2,1)}, bf16[256,1024]{1,0:T(8,128)(2,1)}, u32[]{:S(2)}, u32[]{:S(2)}) collective-permute-start(bf16[256,1024]{1,0:T(8,128)(2,1)} %get-tuple-element.32.refs_3_), channel_id=1, source_target_pairs={{0,8},{8,0},{16,24},{24,16},{32,40},{40,32},{48,56},{56,48},{64,72... | collective-permute-start | bytes 1572872 | tf_op jit(solution)/shard_map/ppermute | solution.py:31
  75.7 1.2 %copy-start.4 = (bf16[1024,512]{1,0:T(8,128)(2,1)S(1)}, bf16[1024,512]{1,0:T(8,128)(2,1)}, u32[]{:S(2)}) copy-start(bf16[1024,512]{1,0:T(8,128)(2,1)} %refs_3_.1) | copy-start | bytes 3145732

commit v3 on v2

--- a/solution.py
+++ b/solution.py
@@ -17,6 +17,7 @@
 N_CTX = 64
 SCALE_LOG2 = (HD**-0.5) * 1.4426950408889634
 Q_TILE = 128
+BLOCK = 256
 TOTAL_LIMIT = 2.0**100
 VMEM_LIMIT = 24 * 2**20
 
@@ -64,31 +65,46 @@
     return (total / jnp.float32(group**0.5)).astype(jnp.bfloat16)
 
 
-def first_kernel(core_ref, k_ref, v_ref, near_ref, far_ref, one_ref, two_ref):
+def first_kernel(core_ref, k_hbm, v_hbm, near_ref, far_ref, one_ref, two_ref, buf, sems):
     core = core_ref[0]
-    by4 = pooling_matrix(256, 4)
-    by2 = pooling_matrix(256, 2)
-    for side, ref in enumerate((k_ref, v_ref)):
-        cols = pl.ds(side * WIDTH, WIDTH)
-        for part in range(4):
-            near_ref[pl.ds(part * 64, 64), cols] = pool(ref[pl.ds(part * 256, 256), :], 4, by4)
-        one = pool(near_ref[pl.ds(0, 256), cols], 2, by2)
-        one_ref[:, cols] = one
-        two_ref[:, cols] = pool(one, 2, by2[:64, :128])
-        last = pl.multiple_of((1 - core) * (TOK - EDGE), EDGE)
-        near_ref[pl.ds(POOL, EDGE), cols] = ref[pl.ds(last, EDGE), :]
-        first = pl.multiple_of(core * (TOK - EDGE), EDGE)
-        far_ref[:, cols] = ref[pl.ds(first, EDGE), :]
+    by4 = pooling_matrix(BLOCK, 4)
+    by2 = pooling_matrix(BLOCK // 4, 2)
+    copies = []
+    for part in range(TOK // BLOCK):
+        rows = pl.ds(part * BLOCK, BLOCK)
+        for side, ref in enumerate((k_hbm, v_hbm)):
+            there = buf.at[rows, pl.ds(side * WIDTH, WIDTH)]
+            copies.append(pltpu.make_async_copy(ref.at[rows, :], there, sems.at[2 * part + side]))
+    for copy in copies:
+        copy.start()
+    for part in range(TOK // BLOCK):
+        for side in range(2):
+            copies[2 * part + side].wait()
+            cols = pl.ds(side * WIDTH, WIDTH)
+            zero = pool(buf[pl.ds(part * BLOCK, BLOCK), cols], 4, by4)
+            one = pool(zero, 2, by2)
+            near_ref[pl.ds(part * (BLOCK // 4), BLOCK // 4), cols] = zero
+            one_ref[pl.ds(part * (BLOCK // 8), BLOCK // 8), cols] = one
+            two = pool(one, 2, by2[: BLOCK // 16, : BLOCK // 8])
+            two_ref[pl.ds(part * (BLOCK // 16), BLOCK // 16), cols] = two
+    last = pl.multiple_of((1 - core) * (TOK - EDGE), EDGE)
+    near_ref[pl.ds(POOL, EDGE), :] = buf[pl.ds(last, EDGE), :]
+    first = pl.multiple_of(core * (TOK - EDGE), EDGE)
+    far_ref[...] = buf[pl.ds(first, EDGE), :]
 
 
 def first_pools(core, keys, values):
-    shape = lambda rows: jax.ShapeDtypeStruct((rows, 2 * WIDTH), jnp.bfloat16)
-    vmem = pl.BlockSpec(memory_space=pltpu.VMEM)
+    counts = (POOL + EDGE, EDGE, POOL // 2, POOL // 4)
+    hbm = pl.BlockSpec(memory_space=pltpu.HBM)
     return pl.pallas_call(
         first_kernel,
-        in_specs=[pl.BlockSpec(memory_space=pltpu.SMEM), vmem, vmem],
-        out_specs=[vmem] * 4,
-        out_shape=[shape(512), shape(256), shape(128), shape(64)],
+        in_specs=[pl.BlockSpec(memory_space=pltpu.SMEM), hbm, hbm],
+        out_specs=[pl.BlockSpec(memory_space=pltpu.VMEM)] * 4,
+        out_shape=[jax.ShapeDtypeStruct((r, 2 * WIDTH), jnp.bfloat16) for r in counts],
+        scratch_shapes=[
+            pltpu.VMEM((TOK, 2 * WIDTH), jnp.bfloat16),
+            pltpu.SemaphoreType.DMA((2 * TOK // BLOCK,)),
+        ],
         compiler_params=pltpu.CompilerParams(vmem_limit_bytes=VMEM_LIMIT),
         cost_estimate=pl.CostEstimate(flops=10**8, bytes_accessed=4 * 2**20, transcendentals=0),
         name="first_pools",
@@ -119,28 +135,50 @@
     four_ref[...] = pool(three, 2, by2[:64, :128])
 
 
-def pair_kernel(four_ref, three_ref, fours_ref, fives_ref):
+def pair_kernel(near_ref, planes_ref, four_ref, three_ref, fours_ref, fives_ref, chip_ref):
     by2 = pooling_matrix(128, 2)
-    fours = jnp.concatenate([four_ref[...], pool(three_ref[...], 2, by2)], axis=0)
+    three = three_ref[...]
+    fours = jnp.concatenate([four_ref[...], pool(three, 2, by2)], axis=0)
     fours_ref[...] = fours
     fives_ref[...] = pool(fours, 2, by2)
+    chip_ref[pl.ds(0, 512), :] = near_ref[...]
+    chip_ref[pl.ds(512, 256), :] = planes_ref[...]
+    chip_ref[pl.ds(768, 128), :] = three
 
 
 def times(a, b, dims):
     return lax.dot_general(a, b, (dims, ((), ())), preferred_element_type=jnp.float32)
 
 
-def attend_kernel(plan, carried, final, *refs):
+def attend_kernel(plan, carried, final, fetched, *refs):
     refs = list(refs)
     bias = refs.pop(0)[0]
     q_ref = refs.pop(0)
     arrays = [refs.pop(0) for _ in range(1 + max(max(p[0], p[1]) for p in plan))]
     if carried:
         acc_in, m_in, l_in = refs.pop(0), refs.pop(0), refs.pop(0)
+    if fetched:
+        sems = refs.pop()
+        held = [refs.pop(-2), refs.pop()]
+
+        def fetch(at, h):
+            lanes = pl.ds(pl.multiple_of(h * HD, HD), HD)
+            there = held[at].at[:, lanes]
+            return pltpu.make_async_copy(arrays[at].at[:, lanes], there, sems.at[at, h])
+
+        for h in range(HEADS_DEV):
+            for at in range(2):
+                fetch(at, h).start()
 
     def one_head(h, _):
         def lanes(first):
             return pl.ds(pl.multiple_of(first + h * HD, HD), HD)
+
+        sources = arrays
+        if fetched:
+            for at in range(2):
+                fetch(at, h).wait()
+            sources = held
 
         def put(rows, acc, peak, total):
             if final:
@@ -153,7 +191,8 @@
         pieces = []
         for k_at, v_at, first, count, v_lane, masked in plan:
             rows = pl.ds(first, count)
-            pieces.append((arrays[k_at][rows, lanes(0)], arrays[v_at][rows, lanes(v_lane)].T, masked))
+            k, v = sources[k_at][rows, lanes(0)], sources[v_at][rows, lanes(v_lane)]
+            pieces.append((k, v.T, masked))
 
         query = q_ref[:, lanes(0)]
         acc, total = 0.0, 0.0
@@ -207,10 +246,15 @@
     lax.fori_loop(0, HEADS_DEV, one_head, 0)
 
 
-def attend(bias, queries, arrays, plan, state, final):
+def attend(bias, queries, arrays, plan, state, final, fetched=False):
     vmem = pl.BlockSpec(memory_space=pltpu.VMEM)
     operands = [bias, queries, *arrays, *state]
     count = sum(piece[3] for piece in plan)
+    around, scratch = [vmem] * len(arrays), []
+    if fetched:
+        around = [pl.BlockSpec(memory_space=pltpu.HBM)] * len(arrays)
+        scratch = [pltpu.VMEM(array.shape, array.dtype) for array in arrays]
+        scratch.append(pltpu.SemaphoreType.DMA((len(arrays), HEADS_DEV)))
     if final:
         out_specs = vmem
         out_shape = jax.ShapeDtypeStruct((TOK, WIDTH), jnp.bfloat16)
@@ -220,8 +264,9 @@
             jax.ShapeDtypeStruct((HEADS_DEV, rows, TOK), jnp.float32) for rows in (HD, 1, 1)
         ]
     return pl.pallas_call(
-        functools.partial(attend_kernel, plan, bool(state), final),
-        in_specs=[pl.BlockSpec(memory_space=pltpu.SMEM)] + [vmem] * (len(operands) - 1),
+        functools.partial(attend_kernel, plan, bool(state), final, fetched),
+        in_specs=[pl.BlockSpec(memory_space=pltpu.SMEM), vmem, *around, *[vmem] * len(state)],
+        scratch_shapes=scratch,
         out_specs=out_specs,
         out_shape=out_shape,
         compiler_params=pltpu.CompilerParams(vmem_limit_bytes=VMEM_LIMIT),
@@ -239,31 +284,33 @@
     outer = (position == 0) | (position == N_CTX - 1)
     bias = jnp.where(outer, jnp.float32(-1e30), jnp.float32(0)).reshape(1)
 
+    keys = pltpu.with_memory_space_constraint(keys, pltpu.HBM)
+    values = pltpu.with_memory_space_constraint(values, pltpu.HBM)
     near, far, one, two = first_pools(core, keys, values)
+    got1 = swap(one, along_y(1))
     got2 = swap(two, along_y(2))
-    got1 = swap(one, along_y(1))
     got3 = swap(two, along_y(3))
-    near_got = swap(near, other_core)
-    own = (0, 1, 0, TOK, 0, False)
-    state = attend(bias, queries, [keys, values], (own,), (), False)
+    plan = ((0, 1, 0, TOK, 0, False),)
+    state = attend(bias, queries, [keys, values], plan, (), False, fetched=True)
 
     planes, three, four = small_call(plane_kernel, (256, 128, 64), two, got1, got2, got3)
     three_got = swap(three, along_z(1))
     far_got = swap(far, beside)
-    planes_got = swap(planes, other_core)
-    plan = ((0, 0, 0, 512, WIDTH, False), (1, 1, 0, 256, WIDTH, False))
-    state = attend(bias, queries, [near_got, planes], plan, state, False)
-
-    fours, fives = small_call(pair_kernel, (128, 64), four, three_got)
+    plan = ((0, 0, 0, 256, WIDTH, False),)
+    state = attend(bias, queries, [planes], plan, state, False)
+
+    fours, fives, chip = small_call(pair_kernel, (128, 64, 896), near, planes, four, three_got)
+    fours2 = swap(fours, along_z(2))
     fives5 = swap(fives, along_z(5))
-    fours2 = swap(fours, along_z(2))
     fives6 = swap(fives, along_z(6))
-    plan = ((0, 0, 0, 256, WIDTH, False), (1, 1, 0, 256, WIDTH, True))
-    state = attend(bias, queries, [planes_got, far_got], plan, state, False)
-
-    upper = jnp.concatenate([three_got, fives5, fives6, fours2], axis=0)
+    chip_got = swap(chip, other_core)
+    plan = ((0, 0, 0, 896, WIDTH, False),)
+    plan += ((1, 1, 0, 128, WIDTH, False), (2, 2, 0, 256, WIDTH, True))
+    state = attend(bias, queries, [chip_got, three_got, far_got], plan, state, False)
+
+    upper = jnp.concatenate([fours2, fives5, fives6], axis=0)
     upper_got = swap(upper, other_core)
-    plan = ((0, 0, 0, 384, WIDTH, False),)
+    plan = ((0, 0, 0, 256, WIDTH, False),)
     state = attend(bias, queries, [upper], plan, state, False)
     return attend(bias, queries, [upper_got], plan, state, True)
 

time: 120 us -> 127 us (1.058)
  waiting for transfers between devices: 26 us -> 34.6 us
  local copies, waits for them, and re-layouts: 3.73 us -> 0.95 us
  Pallas kernels: 45.7 us -> 48.2 us
    ppermute x11 -> x10, waiting for transfers between devices: 26 us -> 34.6 us  [swap(): return lax.ppermute(value, 'ctx', pairs)]
    unnamed x13 -> x4, local copies, waits for them, and re-layouts: 3.71 us -> 0.94 us
    pallas_call x1, Pallas kernels: 2.13 us -> 4.39 us  [first_pools(): pl.pallas_call(first_kernel, in_specs=[pl.BlockSpec(memory_space=pltpu.SM...]
    ppermute x11 -> x10, starting transfers between devices: 43.4 us -> 42.3 us  [swap(): return lax.ppermute(value, 'ctx', pairs)]
  transfers between devices with their start and end apart: 11 -> 10, of which waited for: 6 -> 5; matrix products, arithmetic and copies ran while one was open for 0% -> 1% of each run, Pallas kernels for 32% -> 30%
where the time goes in v3:
time: 127 us; the launch traced here: 126 us
  Pallas kernels  48.2 us (38%)
  starting transfers between devices  42.3 us (33%)
  waiting for transfers between devices  34.6 us (27%)
    ppermute x10, starting transfers between devices, swap(): return lax.ppermute(value, 'ctx', pairs)  42.3 us
    pallas_call x5, Pallas kernels, attend(): pl.pallas_call(functools.partial(attend_kernel, plan, bool(state), final,...  41.6 us
    ppermute x10, waiting for transfers between devices, swap(): return lax.ppermute(value, 'ctx', pairs)  34.6 us
    pallas_call x1, Pallas kernels, first_pools(): pl.pallas_call(first_kernel, in_specs=[pl.BlockSpec(memory_space=pltpu.SM...  4.39 us
  transfers between devices with their start and end apart: 10, of which 5 were waited for; matrix products, arithmetic and copies ran while one was open for 1% of the time, Pallas kernels for 30%

profile of v3, /device:TPU:6, one launch (start us, length us, event | category | flops | bytes accessed | tf_op | source)
XLA Modules:
  0.0 126.2 jit_solution(12512970773967870545)
XLA Ops:
  0.0 4.4 %first_pools.1 = (bf16[512,1024]{1,0:T(8,128)(2,1)S(1)}, bf16[256,1024]{1,0:T(8,128)(2,1)S(1)}, bf16[128,1024]{1,0:T(8,128)(2,1)S(1)}, bf16[64,1024]{1,0:T(8,128)(2,1)S(1)}) custom-call(s32[1]{0:T(128)} %bitcast.1.core_ref, bf16[1024,512]{1,0:T(8,128)(2,1)} %refs_2_.1, bf16[1024,512]{1,0:T(8,128)(2,1)} %refs_3_.1), custom_call_target="tpu_custom_call" | custom-call | flops 100000000 | bytes 4194304 | tf_op jit(solution)/shard_map/first_pools/pallas_call | solution.py:99
  4.4 0.0 copy-start
  4.4 4.6 %collective-permute-start = (bf16[128,1024]{1,0:T(8,128)(2,1)S(1)}, bf16[128,1024]{1,0:T(8,128)(2,1)S(1)}, u32[]{:S(2)}, u32[]{:S(2)}) collective-permute-start(bf16[128,1024]{1,0:T(8,128)(2,1)S(1)} %get-tuple-element.29), channel_id=1, source_target_pairs={{0,16},{8,24},{16,0},{24,8},{32,48},{40,56},{48,32},{56,40},{64,80... | collective-permute-start | bytes 786440 | tf_op jit(solution)/shard_map/ppermute | solution.py:32
  9.0 5.9 %collective-permute-start.1 = (bf16[64,1024]{1,0:T(8,128)(2,1)S(1)}, bf16[64,1024]{1,0:T(8,128)(2,1)S(1)}, u32[]{:S(2)}, u32[]{:S(2)}) collective-permute-start(bf16[64,1024]{1,0:T(8,128)(2,1)S(1)} %get-tuple-element.28.own_ref), channel_id=1, source_target_pairs={{0,32},{8,40},{16,48},{24,56},{32,0},{40,8},{48,16},{56,24},{64,96... | collective-permute-start | bytes 393224 | tf_op jit(solution)/shard_map/ppermute | solution.py:32
  15.0 1.9 %collective-permute-start.2 = (bf16[64,1024]{1,0:T(8,128)(2,1)S(1)}, bf16[64,1024]{1,0:T(8,128)(2,1)S(1)}, u32[]{:S(2)}, u32[]{:S(2)}) collective-permute-start(bf16[64,1024]{1,0:T(8,128)(2,1)S(1)} %get-tuple-element.28.own_ref), channel_id=1, source_target_pairs={{0,48},{8,56},{16,32},{24,40},{32,16},{40,24},{48,0},{56,8},{64,11... | collective-permute-start | bytes 393224 | tf_op jit(solution)/shard_map/ppermute | solution.py:32
  16.9 7.7 %collective-permute-done.1.b_ref = bf16[64,1024]{1,0:T(8,128)(2,1)S(1)} collective-permute-done((bf16[64,1024]{1,0:T(8,128)(2,1)S(1)}, bf16[64,1024]{1,0:T(8,128)(2,1)S(1)}, u32[]{:S(2)}, u32[]{:S(2)}) %collective-permute-start.1) | collective-permute-done | bytes 131104 | tf_op jit(solution)/shard_map/ppermute | solution.py:32
  24.6 5.6 %collective-permute-done.2.c_ref = bf16[64,1024]{1,0:T(8,128)(2,1)S(1)} collective-permute-done((bf16[64,1024]{1,0:T(8,128)(2,1)S(1)}, bf16[64,1024]{1,0:T(8,128)(2,1)S(1)}, u32[]{:S(2)}, u32[]{:S(2)}) %collective-permute-start.2) | collective-permute-done | bytes 131104 | tf_op jit(solution)/shard_map/ppermute | solution.py:32
  30.2 0.0 collective-permute-done.a_ref
  30.2 0.5 shard_map.37
  30.8 4.3 %collective-permute-start.3 = (bf16[128,1024]{1,0:T(8,128)(2,1)S(1)}, bf16[128,1024]{1,0:T(8,128)(2,1)S(1)}, u32[]{:S(2)}, u32[]{:S(2)}) collective-permute-start(bf16[128,1024]{1,0:T(8,128)(2,1)S(1)} %get-tuple-element.32), channel_id=1, source_target_pairs={{0,64},{8,72},{16,80},{24,88},{32,96},{40,104},{48,112},{56,120},{... | collective-permute-start | bytes 786440 | tf_op jit(solution)/shard_map/ppermute | solution.py:32
  35.1 4.3 %collective-permute-done.3.three_ref.refs_3_ = bf16[128,1024]{1,0:T(8,128)(2,1)S(1)} collective-permute-done((bf16[128,1024]{1,0:T(8,128)(2,1)S(1)}, bf16[128,1024]{1,0:T(8,128)(2,1)S(1)}, u32[]{:S(2)}, u32[]{:S(2)}) %collective-permute-start.3) | collective-permute-done | bytes 262176 | tf_op jit(solution)/shard_map/ppermute | solution.py:32
  39.4 1.6 %shard_map.38 = (bf16[128,1024]{1,0:T(8,128)(2,1)S(1)}, bf16[64,1024]{1,0:T(8,128)(2,1)S(1)}, bf16[896,1024]{1,0:T(8,128)(2,1)}) custom-call(bf16[512,1024]{1,0:T(8,128)(2,1)S(1)} %get-tuple-element.27.near_ref, bf16[256,1024]{1,0:T(8,128)(2,1)S(1)} %get-tuple-element.30.planes_ref.refs_2_, bf16[64,1024]{1,0:T(8,128)(2,1)S(1)} %get-tuple-element.31.four_ref, ...), custom_call_target="tpu_custom_call" | custom-call | flops 100000000 | bytes 1048576 | tf_op jit(solution)/shard_map/pallas_call | solution.py:116
  41.0 1.9 %collective-permute-start.8 = (bf16[896,1024]{1,0:T(8,128)(2,1)}, bf16[896,1024]{1,0:T(8,128)(2,1)}, u32[]{:S(2)}, u32[]{:S(2)}) collective-permute-start(bf16[896,1024]{1,0:T(8,128)(2,1)} %get-tuple-element.35), channel_id=1, source_target_pairs={{0,8},{8,0},{16,24},{24,16},{32,40},{40,32},{48,56},{56,48},{64,72... | collective-permute-start | bytes 5505032 | tf_op jit(solution)/shard_map/ppermute | solution.py:32
  42.9 6.1 %collective-permute-start.4 = (bf16[128,1024]{1,0:T(8,128)(2,1)S(1)}, bf16[128,1024]{1,0:T(8,128)(2,1)S(1)}, u32[]{:S(2)}, u32[]{:S(2)}) collective-permute-start(bf16[128,1024]{1,0:T(8,128)(2,1)S(1)} %get-tuple-element.33), channel_id=1, source_target_pairs={{0,128},{8,136},{16,144},{24,152},{32,160},{40,168},{48,176},{56,1... | collective-permute-start | bytes 786440 | tf_op jit(solution)/shard_map/ppermute | solution.py:32
  49.0 8.8 %collective-permute-start.5 = (bf16[64,1024]{1,0:T(8,128)(2,1)S(1)}, bf16[64,1024]{1,0:T(8,128)(2,1)}, u32[]{:S(2)}, u32[]{:S(2)}) collective-permute-start(bf16[64,1024]{1,0:T(8,128)(2,1)S(1)} %get-tuple-element.34), channel_id=1, source_target_pairs={{0,320},{8,328},{16,336},{24,344},{32,352},{40,360},{48,368},{56,3... | collective-permute-start | bytes 393224 | tf_op jit(solution)/shard_map/ppermute | solution.py:32
  57.8 0.7 collective-permute-start.9
  58.5 5.6 %collective-permute-start.6 = (bf16[64,1024]{1,0:T(8,128)(2,1)S(1)}, bf16[64,1024]{1,0:T(8,128)(2,1)S(1)}, u32[]{:S(2)}, u32[]{:S(2)}) collective-permute-start(bf16[64,1024]{1,0:T(8,128)(2,1)S(1)} %get-tuple-element.34), channel_id=1, source_target_pairs={{0,384},{8,392},{16,400},{24,408},{32,416},{40,424},{48,432},{56,4... | collective-permute-start | bytes 393224 | tf_op jit(solution)/shard_map/ppermute | solution.py:32
  64.1 0.5 collective-permute-done.4
  64.6 16.4 %collective-permute-done.5 = bf16[64,1024]{1,0:T(8,128)(2,1)} collective-permute-done((bf16[64,1024]{1,0:T(8,128)(2,1)S(1)}, bf16[64,1024]{1,0:T(8,128)(2,1)}, u32[]{:S(2)}, u32[]{:S(2)}) %collective-permute-start.5) | collective-permute-done | bytes 131104 | tf_op jit(solution)/shard_map/ppermute | solution.py:32
  81.0 0.9 constant_dynamic-update-slice_fusion.1
  81.9 0.0 collective-permute-done.6
  82.0 2.5 %collective-permute-start.7 = (bf16[256,1024]{1,0:T(8,128)(2,1)S(1)}, bf16[256,1024]{1,0:T(8,128)(2,1)S(1)}, u32[]{:S(2)}, u32[]{:S(2)}) collective-permute-start(bf16[256,1024]{1,0:T(8,128)(2,1)S(1)} %constant_dynamic-update-slice_fusion.refs_2_), channel_id=1, source_target_pairs={{0,8},{8,0},{16,24},{24,16},{32,40},{40,32},{48,56},{56,48},{64,72... | collective-permute-start | bytes 1572872 | tf_op jit(solution)/shard_map/ppermute | solution.py:32
  84.5 0.0 copy-done
  84.5 25.5 %shard_map.39 = (f32[4,128,1024]{2,1,0:T(8,128)S(1)}, f32[4,1,1024]{2,1,0:T(1,128)S(1)}, f32[4,1,1024]{2,1,0:T(1,128)S(1)}) custom-call(f32[1]{0:T(128)} %bitcast.refs_0_, bf16[1024,512]{1,0:T(8,128)(2,1)S(1)} %copy-done, bf16[1024,512]{1,0:T(8,128)(2,1)} %refs_2_.1, bf16[1024,512]{1,0:T(8,128)(2,1)} %refs_3_.1), custom_call_target="tpu_custom_call" | custom-call | flops 2147483648 | bytes 5242880 | tf_op jit(solution)/shard_map/pallas_call | solution.py:266
  110.0 2.1 %shard_map.40 = (f32[4,128,1024]{2,1,0:T(8,128)S(1)}, f32[4,1,1024]{2,1,0:T(1,128)S(1)}, f32[4,1,1024]{2,1,0:T(1,128)S(1)}) custom-call(f32[1]{0:T(128)} %bitcast.refs_0_, bf16[1024,512]{1,0:T(8,128)(2,1)S(1)} %copy-done, bf16[256,1024]{1,0:T(8,128)(2,1)S(1)} %get-tuple-element.30.planes_ref.refs_2_, f32[4,128,1024]{2,1,0:T(8,128)S(1)} %get-tuple-element.37.refs_3_, ...), custom_call_target="tpu_custom_call" | custom-call | flops 536870912 | bytes 3670016 | tf_op jit(solution)/shard_map/pallas_call | solution.py:266
  112.1 0.0 collective-permute-done.9.refs_4_
  112.2 0.0 collective-permute-done.8.refs_2_
  112.2 8.5 %shard_map.41 = (f32[4,128,1024]{2,1,0:T(8,128)S(1)}, f32[4,1,1024]{2,1,0:T(1,128)S(1)}, f32[4,1,1024]{2,1,0:T(1,128)S(1)}) custom-call(f32[1]{0:T(128)} %bitcast.refs_0_, bf16[1024,512]{1,0:T(8,128)(2,1)S(1)} %copy-done, bf16[896,1024]{1,0:T(8,128)(2,1)} %collective-permute-done.8.refs_2_, bf16[128,1024]{1,0:T(8,128)(2,1)S(1)} %collective-permute-done.3.three_ref.refs_3_, ...), custom_call_target="tpu_custom_call" | custom-call | flops 2684354560 | bytes 5767168 | tf_op jit(solution)/shard_map/pallas_call | solution.py:266
  120.7 2.1 %shard_map.42 = (f32[4,128,1024]{2,1,0:T(8,128)S(1)}, f32[4,1,1024]{2,1,0:T(1,128)S(1)}, f32[4,1,1024]{2,1,0:T(1,128)S(1)}) custom-call(f32[1]{0:T(128)} %bitcast.refs_0_, bf16[1024,512]{1,0:T(8,128)(2,1)S(1)} %copy-done, bf16[256,1024]{1,0:T(8,128)(2,1)S(1)} %constant_dynamic-update-slice_fusion.refs_2_, f32[4,128,1024]{2,1,0:T(8,128)S(1)} %get-tuple-element.43.refs_3_, ...), custom_call_target="tpu_custom_call" | custom-call | flops 536870912 | bytes 3670016 | tf_op jit(solution)/shard_map/pallas_call | solution.py:266
  122.8 0.0 collective-permute-done.7.refs_2_
  122.8 3.4 %shard_map.43 = bf16[1024,512]{1,0:T(8,128)(2,1)} custom-call(f32[1]{0:T(128)} %bitcast.refs_0_, bf16[1024,512]{1,0:T(8,128)(2,1)S(1)} %copy-done, bf16[256,1024]{1,0:T(8,128)(2,1)S(1)} %collective-permute-done.7.refs_2_, f32[4,128,1024]{2,1,0:T(8,128)S(1)} %get-tuple-element.46.refs_3_, f32[4,1,1024]{2,1,0:T(1,128)S(1)} %get-tuple-element.47.refs_4_, ...), custom_call_target="tpu_custom_call" | custom-call | flops 536870912 | bytes 3670016 | tf_op jit(solution)/shard_map/pallas_call | solution.py:266
  (2 shorter events, 0.0 us)
Async XLA Ops:
  4.4 80.1 %copy-start = (bf16[1024,512]{1,0:T(8,128)(2,1)S(1)}, bf16[1024,512]{1,0:T(8,128)(2,1)}, u32[]{:S(2)}) copy-start(bf16[1024,512]{1,0:T(8,128)(2,1)} %refs_1_.9) | copy-start | bytes 3145732
  4.4 25.8 %collective-permute-start = (bf16[128,1024]{1,0:T(8,128)(2,1)S(1)}, bf16[128,1024]{1,0:T(8,128)(2,1)S(1)}, u32[]{:S(2)}, u32[]{:S(2)}) collective-permute-start(bf16[128,1024]{1,0:T(8,128)(2,1)S(1)} %get-tuple-element.29), channel_id=1, source_target_pairs={{0,16},{8,24},{16,0},{24,8},{32,48},{40,56},{48,32},{56,40},{64,80... | collective-permute-start | bytes 786440 | tf_op jit(solution)/shard_map/ppermute | solution.py:32
  9.0 15.6 %collective-permute-start.1 = (bf16[64,1024]{1,0:T(8,128)(2,1)S(1)}, bf16[64,1024]{1,0:T(8,128)(2,1)S(1)}, u32[]{:S(2)}, u32[]{:S(2)}) collective-permute-start(bf16[64,1024]{1,0:T(8,128)(2,1)S(1)} %get-tuple-element.28.own_ref), channel_id=1, source_target_pairs={{0,32},{8,40},{16,48},{24,56},{32,0},{40,8},{48,16},{56,24},{64,96... | collective-permute-start | bytes 393224 | tf_op jit(solution)/shard_map/ppermute | solution.py:32
  15.0 15.2 %collective-permute-start.2 = (bf16[64,1024]{1,0:T(8,128)(2,1)S(1)}, bf16[64,1024]{1,0:T(8,128)(2,1)S(1)}, u32[]{:S(2)}, u32[]{:S(2)}) collective-permute-start(bf16[64,1024]{1,0:T(8,128)(2,1)S(1)} %get-tuple-element.28.own_ref), channel_id=1, source_target_pairs={{0,48},{8,56},{16,32},{24,40},{32,16},{40,24},{48,0},{56,8},{64,11... | collective-permute-start | bytes 393224 | tf_op jit(solution)/shard_map/ppermute | solution.py:32
  30.8 8.6 %collective-permute-start.3 = (bf16[128,1024]{1,0:T(8,128)(2,1)S(1)}, bf16[128,1024]{1,0:T(8,128)(2,1)S(1)}, u32[]{:S(2)}, u32[]{:S(2)}) collective-permute-start(bf16[128,1024]{1,0:T(8,128)(2,1)S(1)} %get-tuple-element.32), channel_id=1, source_target_pairs={{0,64},{8,72},{16,80},{24,88},{32,96},{40,104},{48,112},{56,120},{... | collective-permute-start | bytes 786440 | tf_op jit(solution)/shard_map/ppermute | solution.py:32
  41.0 71.2 %collective-permute-start.8 = (bf16[896,1024]{1,0:T(8,128)(2,1)}, bf16[896,1024]{1,0:T(8,128)(2,1)}, u32[]{:S(2)}, u32[]{:S(2)}) collective-permute-start(bf16[896,1024]{1,0:T(8,128)(2,1)} %get-tuple-element.35), channel_id=1, source_target_pairs={{0,8},{8,0},{16,24},{24,16},{32,40},{40,32},{48,56},{56,48},{64,72... | collective-permute-start | bytes 5505032 | tf_op jit(solution)/shard_map/ppermute | solution.py:32
  42.9 21.7 %collective-permute-start.4 = (bf16[128,1024]{1,0:T(8,128)(2,1)S(1)}, bf16[128,1024]{1,0:T(8,128)(2,1)S(1)}, u32[]{:S(2)}, u32[]{:S(2)}) collective-permute-start(bf16[128,1024]{1,0:T(8,128)(2,1)S(1)} %get-tuple-element.33), channel_id=1, source_target_pairs={{0,128},{8,136},{16,144},{24,152},{32,160},{40,168},{48,176},{56,1... | collective-permute-start | bytes 786440 | tf_op jit(solution)/shard_map/ppermute | solution.py:32
  49.0 32.0 %collective-permute-start.5 = (bf16[64,1024]{1,0:T(8,128)(2,1)S(1)}, bf16[64,1024]{1,0:T(8,128)(2,1)}, u32[]{:S(2)}, u32[]{:S(2)}) collective-permute-start(bf16[64,1024]{1,0:T(8,128)(2,1)S(1)} %get-tuple-element.34), channel_id=1, source_target_pairs={{0,320},{8,328},{16,336},{24,344},{32,352},{40,360},{48,368},{56,3... | collective-permute-start | bytes 393224 | tf_op jit(solution)/shard_map/ppermute | solution.py:32
  57.8 54.4 %collective-permute-start.9 = (bf16[256,1024]{1,0:T(8,128)(2,1)S(1)}, bf16[256,1024]{1,0:T(8,128)(2,1)S(1)}, u32[]{:S(2)}, u32[]{:S(2)}) collective-permute-start(bf16[256,1024]{1,0:T(8,128)(2,1)S(1)} %get-tuple-element.36), channel_id=1, source_target_pairs={{8,16},{16,8},{24,32},{32,24},{40,48},{48,40},{56,64},{64,56},{72,... | collective-permute-start | bytes 1572872 | tf_op jit(solution)/shard_map/ppermute | solution.py:32
  58.5 23.4 %collective-permute-start.6 = (bf16[64,1024]{1,0:T(8,128)(2,1)S(1)}, bf16[64,1024]{1,0:T(8,128)(2,1)S(1)}, u32[]{:S(2)}, u32[]{:S(2)}) collective-permute-start(bf16[64,1024]{1,0:T(8,128)(2,1)S(1)} %get-tuple-element.34), channel_id=1, source_target_pairs={{0,384},{8,392},{16,400},{24,408},{32,416},{40,424},{48,432},{56,4... | collective-permute-start | bytes 393224 | tf_op jit(solution)/shard_map/ppermute | solution.py:32
  82.0 40.8 %collective-permute-start.7 = (bf16[256,1024]{1,0:T(8,128)(2,1)S(1)}, bf16[256,1024]{1,0:T(8,128)(2,1)S(1)}, u32[]{:S(2)}, u32[]{:S(2)}) collective-permute-start(bf16[256,1024]{1,0:T(8,128)(2,1)S(1)} %constant_dynamic-update-slice_fusion.refs_2_), channel_id=1, source_target_pairs={{0,8},{8,0},{16,24},{24,16},{32,40},{40,32},{48,56},{56,48},{64,72... | collective-permute-start | bytes 1572872 | tf_op jit(solution)/shard_map/ppermute | solution.py:32

commit v4 on v3

--- a/solution.py
+++ b/solution.py
@@ -44,8 +44,8 @@
     return lambda z, y, core: index_of(z, y ^ bits, core)
 
 
-def along_z(bits):
-    return lambda z, y, core: index_of(z ^ bits, y, core)
+def along_z(first, second):
+    return lambda z, y, core: index_of(z ^ (second if core else first), y, core)
 
 
 def beside(z, y, core):
@@ -68,7 +68,7 @@
 def first_kernel(core_ref, k_hbm, v_hbm, near_ref, far_ref, one_ref, two_ref, buf, sems):
     core = core_ref[0]
     by4 = pooling_matrix(BLOCK, 4)
-    by2 = pooling_matrix(BLOCK // 4, 2)
+    by2 = pooling_matrix(POOL, 2)
     copies = []
     for part in range(TOK // BLOCK):
         rows = pl.ds(part * BLOCK, BLOCK)
@@ -82,11 +82,10 @@
             copies[2 * part + side].wait()
             cols = pl.ds(side * WIDTH, WIDTH)
             zero = pool(buf[pl.ds(part * BLOCK, BLOCK), cols], 4, by4)
-            one = pool(zero, 2, by2)
             near_ref[pl.ds(part * (BLOCK // 4), BLOCK // 4), cols] = zero
-            one_ref[pl.ds(part * (BLOCK // 8), BLOCK // 8), cols] = one
-            two = pool(one, 2, by2[: BLOCK // 16, : BLOCK // 8])
-            two_ref[pl.ds(part * (BLOCK // 16), BLOCK // 16), cols] = two
+    one = pool(near_ref[pl.ds(0, POOL), :], 2, by2)
+    one_ref[...] = one
+    two_ref[...] = pool(one, 2, by2[: POOL // 4, : POOL // 2])
     last = pl.multiple_of((1 - core) * (TOK - EDGE), EDGE)
     near_ref[pl.ds(POOL, EDGE), :] = buf[pl.ds(last, EDGE), :]
     first = pl.multiple_of(core * (TOK - EDGE), EDGE)
@@ -123,27 +122,27 @@
     )(*operands)
 
 
-def plane_kernel(own_ref, a_ref, b_ref, c_ref, got_ref, three_ref, four_ref):
+def plane_kernel(own_ref, a_ref, b_ref, c_ref, got_ref, three_ref):
     by2 = pooling_matrix(256, 2)
     a, b, c = a_ref[...], b_ref[...], c_ref[...]
+    own = own_ref[...]
     got_ref[pl.ds(0, 128), :] = a
     got_ref[pl.ds(128, 64), :] = b
     got_ref[pl.ds(192, 64), :] = c
-    rows = jnp.concatenate([own_ref[...], pool(a, 2, by2[:64, :128]), b, c], axis=0)
-    three = pool(rows, 2, by2)
-    three_ref[...] = three
-    four_ref[...] = pool(three, 2, by2[:64, :128])
-
-
-def pair_kernel(near_ref, planes_ref, four_ref, three_ref, fours_ref, fives_ref, chip_ref):
-    by2 = pooling_matrix(128, 2)
-    three = three_ref[...]
-    fours = jnp.concatenate([four_ref[...], pool(three, 2, by2)], axis=0)
+    got_ref[pl.ds(256, 64), :] = own
+    rows = jnp.concatenate([pool(a, 2, by2[:64, :128]), b, c, own], axis=0)
+    three_ref[...] = pool(rows, 2, by2)
+
+
+def wide_kernel(three_ref, got_ref, fours_ref, fives_ref):
+    by2 = pooling_matrix(256, 2)
+    rows = jnp.concatenate(
+        [pool(got_ref[pl.ds(0, 128), :], 2, by2[:64, :128]), got_ref[pl.ds(128, 192), :]], axis=0
+    )
+    threes = jnp.concatenate([three_ref[...], pool(rows, 2, by2)], axis=0)
+    fours = pool(threes, 2, by2)
     fours_ref[...] = fours
-    fives_ref[...] = pool(fours, 2, by2)
-    chip_ref[pl.ds(0, 512), :] = near_ref[...]
-    chip_ref[pl.ds(512, 256), :] = planes_ref[...]
-    chip_ref[pl.ds(768, 128), :] = three
+    fives_ref[...] = pool(fours, 2, by2[:64, :128])
 
 
 def times(a, b, dims):
@@ -290,28 +289,27 @@
     got1 = swap(one, along_y(1))
     got2 = swap(two, along_y(2))
     got3 = swap(two, along_y(3))
+    near_got = swap(near, other_core)
     plan = ((0, 1, 0, TOK, 0, False),)
     state = attend(bias, queries, [keys, values], plan, (), False, fetched=True)
 
-    planes, three, four = small_call(plane_kernel, (256, 128, 64), two, got1, got2, got3)
-    three_got = swap(three, along_z(1))
+    planes, three = small_call(plane_kernel, (320, 128), two, got1, got2, got3)
+    planes_got = swap(planes, other_core)
+    three_got = swap(three, along_z(1, 1))
+    fours, fives = small_call(wide_kernel, (128, 64), three, planes_got)
+    fours_got = swap(fours, along_z(2, 3))
     far_got = swap(far, beside)
-    plan = ((0, 0, 0, 256, WIDTH, False),)
-    state = attend(bias, queries, [planes], plan, state, False)
-
-    fours, fives, chip = small_call(pair_kernel, (128, 64, 896), near, planes, four, three_got)
-    fours2 = swap(fours, along_z(2))
-    fives5 = swap(fives, along_z(5))
-    fives6 = swap(fives, along_z(6))
-    chip_got = swap(chip, other_core)
-    plan = ((0, 0, 0, 896, WIDTH, False),)
-    plan += ((1, 1, 0, 128, WIDTH, False), (2, 2, 0, 256, WIDTH, True))
-    state = attend(bias, queries, [chip_got, three_got, far_got], plan, state, False)
-
-    upper = jnp.concatenate([fours2, fives5, fives6], axis=0)
+    fives_c = swap(fives, along_z(5, 4))
+    fives_d = swap(fives, along_z(6, 7))
+    plan = ((0, 0, 0, 512, WIDTH, False), (1, 1, 0, 256, WIDTH, False))
+    plan += ((2, 2, 0, 256, WIDTH, False),)
+    state = attend(bias, queries, [near_got, planes, planes_got], plan, state, False)
+
+    upper = jnp.concatenate([three_got, fours_got, fives_c, fives_d], axis=0)
     upper_got = swap(upper, other_core)
-    plan = ((0, 0, 0, 256, WIDTH, False),)
-    state = attend(bias, queries, [upper], plan, state, False)
+    plan = ((0, 0, 0, 384, WIDTH, False), (1, 1, 0, 256, WIDTH, True))
+    state = attend(bias, queries, [upper, far_got], plan, state, False)
+    plan = ((0, 0, 0, 384, WIDTH, False),)
     return attend(bias, queries, [upper_got], plan, state, True)
 
 

time: 127 us -> 112 us (0.88)
  the two profiles are of different devices: /device:TPU:6 before, /device:TPU:86 now
where the time goes in v4:
time: 112 us; the launch traced here: 111 us
  Pallas kernels  46.1 us (41%)
  starting transfers between devices  44.1 us (39%)
  waiting for transfers between devices  21 us (19%)
    ppermute x11, starting transfers between devices, swap(): return lax.ppermute(value, 'ctx', pairs)  44.1 us
    pallas_call x4, Pallas kernels, attend(): pl.pallas_call(functools.partial(attend_kernel, plan, bool(state), final,...  41.2 us
    ppermute x11, waiting for transfers between devices, swap(): return lax.ppermute(value, 'ctx', pairs)  21 us
    pallas_call x1, Pallas kernels, first_pools(): pl.pallas_call(first_kernel, in_specs=[pl.BlockSpec(memory_space=pltpu.SM...  3.74 us
  transfers between devices with their start and end apart: 11, of which 6 were waited for; matrix products, arithmetic and copies ran while one was open for 0% of the time, Pallas kernels for 34%

profile of v4, /device:TPU:86, one launch (start us, length us, event | category | flops | bytes accessed | tf_op | source)
XLA Modules:
  0.0 111.5 jit_solution(16756561384389547524)
XLA Ops:
  0.0 3.7 %first_pools.1 = (bf16[512,1024]{1,0:T(8,128)(2,1)}, bf16[256,1024]{1,0:T(8,128)(2,1)}, bf16[128,1024]{1,0:T(8,128)(2,1)S(1)}, bf16[64,1024]{1,0:T(8,128)(2,1)S(1)}) custom-call(s32[1]{0:T(128)} %bitcast.1.core_ref, bf16[1024,512]{1,0:T(8,128)(2,1)} %refs_2_.1, bf16[1024,512]{1,0:T(8,128)(2,1)} %refs_3_.1), custom_call_target="tpu_custom_call" | custom-call | flops 100000000 | bytes 4194304 | tf_op jit(solution)/shard_map/first_pools/pallas_call | solution.py:98
  3.8 0.0 copy-start
  3.8 2.4 %collective-permute-start = (bf16[128,1024]{1,0:T(8,128)(2,1)S(1)}, bf16[128,1024]{1,0:T(8,128)(2,1)S(1)}, u32[]{:S(2)}, u32[]{:S(2)}) collective-permute-start(bf16[128,1024]{1,0:T(8,128)(2,1)S(1)} %get-tuple-element.23), channel_id=1, source_target_pairs={{0,16},{8,24},{16,0},{24,8},{32,48},{40,56},{48,32},{56,40},{64,80... | collective-permute-start | bytes 786440 | tf_op jit(solution)/shard_map/ppermute | solution.py:32
  6.1 7.7 %collective-permute-start.1 = (bf16[64,1024]{1,0:T(8,128)(2,1)S(1)}, bf16[64,1024]{1,0:T(8,128)(2,1)S(1)}, u32[]{:S(2)}, u32[]{:S(2)}) collective-permute-start(bf16[64,1024]{1,0:T(8,128)(2,1)S(1)} %get-tuple-element.22.own_ref), channel_id=1, source_target_pairs={{0,32},{8,40},{16,48},{24,56},{32,0},{40,8},{48,16},{56,24},{64,96... | collective-permute-start | bytes 393224 | tf_op jit(solution)/shard_map/ppermute | solution.py:32
  13.9 2.2 %collective-permute-start.2 = (bf16[64,1024]{1,0:T(8,128)(2,1)S(1)}, bf16[64,1024]{1,0:T(8,128)(2,1)S(1)}, u32[]{:S(2)}, u32[]{:S(2)}) collective-permute-start(bf16[64,1024]{1,0:T(8,128)(2,1)S(1)} %get-tuple-element.22.own_ref), channel_id=1, source_target_pairs={{0,48},{8,56},{16,32},{24,40},{32,16},{40,24},{48,0},{56,8},{64,11... | collective-permute-start | bytes 393224 | tf_op jit(solution)/shard_map/ppermute | solution.py:32
  16.1 9.3 %collective-permute-done.1.b_ref = bf16[64,1024]{1,0:T(8,128)(2,1)S(1)} collective-permute-done((bf16[64,1024]{1,0:T(8,128)(2,1)S(1)}, bf16[64,1024]{1,0:T(8,128)(2,1)S(1)}, u32[]{:S(2)}, u32[]{:S(2)}) %collective-permute-start.1) | collective-permute-done | bytes 131104 | tf_op jit(solution)/shard_map/ppermute | solution.py:32
  25.4 2.1 %collective-permute-done.2.c_ref = bf16[64,1024]{1,0:T(8,128)(2,1)S(1)} collective-permute-done((bf16[64,1024]{1,0:T(8,128)(2,1)S(1)}, bf16[64,1024]{1,0:T(8,128)(2,1)S(1)}, u32[]{:S(2)}, u32[]{:S(2)}) %collective-permute-start.2) | collective-permute-done | bytes 131104 | tf_op jit(solution)/shard_map/ppermute | solution.py:32
  27.5 0.0 collective-permute-done.a_ref
  27.5 0.4 shard_map.37
  27.9 0.0 copy-start.1
  27.9 1.9 %collective-permute-start.4 = (bf16[320,1024]{1,0:T(8,128)(2,1)S(1)}, bf16[320,1024]{1,0:T(8,128)(2,1)S(1)}, u32[]{:S(2)}, u32[]{:S(2)}) collective-permute-start(bf16[320,1024]{1,0:T(8,128)(2,1)S(1)} %get-tuple-element.25.refs_3_), channel_id=1, source_target_pairs={{0,8},{8,0},{16,24},{24,16},{32,40},{40,32},{48,56},{56,48},{64,72... | collective-permute-start | bytes 1966088 | tf_op jit(solution)/shard_map/ppermute | solution.py:32
  29.9 1.9 %collective-permute-start.3 = (bf16[128,1024]{1,0:T(8,128)(2,1)S(1)}, bf16[128,1024]{1,0:T(8,128)(2,1)S(1)}, u32[]{:S(2)}, u32[]{:S(2)}) collective-permute-start(bf16[128,1024]{1,0:T(8,128)(2,1)S(1)} %get-tuple-element.24.three_ref), channel_id=1, source_target_pairs={{0,64},{8,72},{16,80},{24,88},{32,96},{40,104},{48,112},{56,120},{... | collective-permute-start | bytes 786440 | tf_op jit(solution)/shard_map/ppermute | solution.py:32
  31.8 0.1 collective-permute-done.4.got_ref.refs_4_
  31.9 0.7 shard_map.38
  32.6 6.1 %collective-permute-start.5 = (bf16[128,1024]{1,0:T(8,128)(2,1)S(1)}, bf16[128,1024]{1,0:T(8,128)(2,1)S(1)}, u32[]{:S(2)}, u32[]{:S(2)}) collective-permute-start(bf16[128,1024]{1,0:T(8,128)(2,1)S(1)} %get-tuple-element.26), channel_id=1, source_target_pairs={{0,128},{8,200},{16,144},{24,216},{32,160},{40,232},{48,176},{56,2... | collective-permute-start | bytes 786440 | tf_op jit(solution)/shard_map/ppermute | solution.py:32
  38.7 2.3 %collective-permute-start.10 = (bf16[512,1024]{1,0:T(8,128)(2,1)}, bf16[512,1024]{1,0:T(8,128)(2,1)}, u32[]{:S(2)}, u32[]{:S(2)}) collective-permute-start(bf16[512,1024]{1,0:T(8,128)(2,1)} %get-tuple-element.29), channel_id=1, source_target_pairs={{0,8},{8,0},{16,24},{24,16},{32,40},{40,32},{48,56},{56,48},{64,72... | collective-permute-start | bytes 3145736 | tf_op jit(solution)/shard_map/ppermute | solution.py:32
  41.0 8.3 %collective-permute-start.6 = (bf16[64,1024]{1,0:T(8,128)(2,1)S(1)}, bf16[64,1024]{1,0:T(8,128)(2,1)S(1)}, u32[]{:S(2)}, u32[]{:S(2)}) collective-permute-start(bf16[64,1024]{1,0:T(8,128)(2,1)S(1)} %get-tuple-element.27), channel_id=1, source_target_pairs={{0,320},{8,264},{16,336},{24,280},{32,352},{40,296},{48,368},{56,3... | collective-permute-start | bytes 393224 | tf_op jit(solution)/shard_map/ppermute | solution.py:32
  49.3 0.0 collective-permute-done.3
  49.3 2.7 %collective-permute-start.7 = (bf16[64,1024]{1,0:T(8,128)(2,1)S(1)}, bf16[64,1024]{1,0:T(8,128)(2,1)S(1)}, u32[]{:S(2)}, u32[]{:S(2)}) collective-permute-start(bf16[64,1024]{1,0:T(8,128)(2,1)S(1)} %get-tuple-element.27), channel_id=1, source_target_pairs={{0,384},{8,456},{16,400},{24,472},{32,416},{40,488},{48,432},{56,5... | collective-permute-start | bytes 393224 | tf_op jit(solution)/shard_map/ppermute | solution.py:32
  52.1 2.9 %collective-permute-done.5 = bf16[128,1024]{1,0:T(8,128)(2,1)S(1)} collective-permute-done((bf16[128,1024]{1,0:T(8,128)(2,1)S(1)}, bf16[128,1024]{1,0:T(8,128)(2,1)S(1)}, u32[]{:S(2)}, u32[]{:S(2)}) %collective-permute-start.5) | collective-permute-done | bytes 262176 | tf_op jit(solution)/shard_map/ppermute | solution.py:32
  55.0 1.4 %collective-permute-done.6 = bf16[64,1024]{1,0:T(8,128)(2,1)S(1)} collective-permute-done((bf16[64,1024]{1,0:T(8,128)(2,1)S(1)}, bf16[64,1024]{1,0:T(8,128)(2,1)S(1)}, u32[]{:S(2)}, u32[]{:S(2)}) %collective-permute-start.6) | collective-permute-done | bytes 131104 | tf_op jit(solution)/shard_map/ppermute | solution.py:32
  56.4 5.2 %collective-permute-done.7 = bf16[64,1024]{1,0:T(8,128)(2,1)S(1)} collective-permute-done((bf16[64,1024]{1,0:T(8,128)(2,1)S(1)}, bf16[64,1024]{1,0:T(8,128)(2,1)S(1)}, u32[]{:S(2)}, u32[]{:S(2)}) %collective-permute-start.7) | collective-permute-done | bytes 131104 | tf_op jit(solution)/shard_map/ppermute | solution.py:32
  61.6 0.0 copy-done.1
  61.6 3.9 %collective-permute-start.8 = (bf16[384,1024]{1,0:T(8,128)(2,1)S(1)}, bf16[384,1024]{1,0:T(8,128)(2,1)S(1)}, u32[]{:S(2)}, u32[]{:S(2)}) collective-permute-start(bf16[384,1024]{1,0:T(8,128)(2,1)S(1)} %constant_dynamic-update-slice_fusion.refs_2_), channel_id=1, source_target_pairs={{0,8},{8,0},{16,24},{24,16},{32,40},{40,32},{48,56},{56,48},{64,72... | collective-permute-start | bytes 2359304 | tf_op jit(solution)/shard_map/ppermute | solution.py:32
  65.6 4.6 %collective-permute-start.9 = (bf16[256,1024]{1,0:T(8,128)(2,1)}, bf16[256,1024]{1,0:T(8,128)(2,1)}, u32[]{:S(2)}, u32[]{:S(2)}) collective-permute-start(bf16[256,1024]{1,0:T(8,128)(2,1)} %get-tuple-element.28), channel_id=1, source_target_pairs={{8,16},{16,8},{24,32},{32,24},{40,48},{48,40},{56,64},{64,56},{72,... | collective-permute-start | bytes 1572872 | tf_op jit(solution)/shard_map/ppermute | solution.py:32
  70.2 0.0 copy-done
  70.2 0.0 copy-start.2
  70.2 25.6 %shard_map.39 = (f32[4,128,1024]{2,1,0:T(8,128)S(1)}, f32[4,1,1024]{2,1,0:T(1,128)S(1)}, f32[4,1,1024]{2,1,0:T(1,128)S(1)}) custom-call(f32[1]{0:T(128)} %bitcast.refs_0_, bf16[1024,512]{1,0:T(8,128)(2,1)S(1)} %copy-done, bf16[1024,512]{1,0:T(8,128)(2,1)} %refs_2_.1, bf16[1024,512]{1,0:T(8,128)(2,1)} %refs_3_.1), custom_call_target="tpu_custom_call" | custom-call | flops 2147483648 | bytes 5242880 | tf_op jit(solution)/shard_map/pallas_call | solution.py:265
  95.8 0.0 collective-permute-done.10.refs_2_
  95.8 0.0 copy-done.2
  95.8 7.0 %shard_map.40 = (f32[4,128,1024]{2,1,0:T(8,128)S(1)}, f32[4,1,1024]{2,1,0:T(1,128)S(1)}, f32[4,1,1024]{2,1,0:T(1,128)S(1)}) custom-call(f32[1]{0:T(128)} %bitcast.refs_0_, bf16[1024,512]{1,0:T(8,128)(2,1)S(1)} %copy-done, bf16[512,1024]{1,0:T(8,128)(2,1)} %collective-permute-done.10.refs_2_, bf16[320,1024]{1,0:T(8,128)(2,1)S(1)} %copy-done.2, ...), custom_call_target="tpu_custom_call" | custom-call | flops 2147483648 | bytes 5242880 | tf_op jit(solution)/shard_map/pallas_call | solution.py:265
  102.8 0.0 collective-permute-done.9.refs_3_
  102.8 5.0 %shard_map.41 = (f32[4,128,1024]{2,1,0:T(8,128)S(1)}, f32[4,1,1024]{2,1,0:T(1,128)S(1)}, f32[4,1,1024]{2,1,0:T(1,128)S(1)}) custom-call(f32[1]{0:T(128)} %bitcast.refs_0_, bf16[1024,512]{1,0:T(8,128)(2,1)S(1)} %copy-done, bf16[384,1024]{1,0:T(8,128)(2,1)S(1)} %constant_dynamic-update-slice_fusion.refs_2_, bf16[256,1024]{1,0:T(8,128)(2,1)} %collective-permute-done.9.refs_3_, ...), custom_call_target="tpu_custom_call" | custom-call | flops 1342177280 | bytes 4456448 | tf_op jit(solution)/shard_map/pallas_call | solution.py:265
  107.8 0.0 collective-permute-done.8.refs_2_
  107.8 3.7 %shard_map.42 = bf16[1024,512]{1,0:T(8,128)(2,1)} custom-call(f32[1]{0:T(128)} %bitcast.refs_0_, bf16[1024,512]{1,0:T(8,128)(2,1)S(1)} %copy-done, bf16[384,1024]{1,0:T(8,128)(2,1)S(1)} %collective-permute-done.8.refs_2_, f32[4,128,1024]{2,1,0:T(8,128)S(1)} %get-tuple-element.36.refs_3_, f32[4,1,1024]{2,1,0:T(1,128)S(1)} %get-tuple-element.37.refs_4_, ...), custom_call_target="tpu_custom_call" | custom-call | flops 805306368 | bytes 3932160 | tf_op jit(solution)/shard_map/pallas_call | solution.py:265
  (4 shorter events, 0.1 us)
Async XLA Ops:
  3.8 66.4 %copy-start = (bf16[1024,512]{1,0:T(8,128)(2,1)S(1)}, bf16[1024,512]{1,0:T(8,128)(2,1)}, u32[]{:S(2)}) copy-start(bf16[1024,512]{1,0:T(8,128)(2,1)} %refs_1_.7) | copy-start | bytes 3145732
  3.8 23.8 %collective-permute-start = (bf16[128,1024]{1,0:T(8,128)(2,1)S(1)}, bf16[128,1024]{1,0:T(8,128)(2,1)S(1)}, u32[]{:S(2)}, u32[]{:S(2)}) collective-permute-start(bf16[128,1024]{1,0:T(8,128)(2,1)S(1)} %get-tuple-element.23), channel_id=1, source_target_pairs={{0,16},{8,24},{16,0},{24,8},{32,48},{40,56},{48,32},{56,40},{64,80... | collective-permute-start | bytes 786440 | tf_op jit(solution)/shard_map/ppermute | solution.py:32
  6.1 19.3 %collective-permute-start.1 = (bf16[64,1024]{1,0:T(8,128)(2,1)S(1)}, bf16[64,1024]{1,0:T(8,128)(2,1)S(1)}, u32[]{:S(2)}, u32[]{:S(2)}) collective-permute-start(bf16[64,1024]{1,0:T(8,128)(2,1)S(1)} %get-tuple-element.22.own_ref), channel_id=1, source_target_pairs={{0,32},{8,40},{16,48},{24,56},{32,0},{40,8},{48,16},{56,24},{64,96... | collective-permute-start | bytes 393224 | tf_op jit(solution)/shard_map/ppermute | solution.py:32
  13.9 13.6 %collective-permute-start.2 = (bf16[64,1024]{1,0:T(8,128)(2,1)S(1)}, bf16[64,1024]{1,0:T(8,128)(2,1)S(1)}, u32[]{:S(2)}, u32[]{:S(2)}) collective-permute-start(bf16[64,1024]{1,0:T(8,128)(2,1)S(1)} %get-tuple-element.22.own_ref), channel_id=1, source_target_pairs={{0,48},{8,56},{16,32},{24,40},{32,16},{40,24},{48,0},{56,8},{64,11... | collective-permute-start | bytes 393224 | tf_op jit(solution)/shard_map/ppermute | solution.py:32
  27.9 33.7 %copy-start.1 = (bf16[320,1024]{1,0:T(8,128)(2,1)}, bf16[320,1024]{1,0:T(8,128)(2,1)S(1)}, u32[]{:S(2)}) copy-start(bf16[320,1024]{1,0:T(8,128)(2,1)S(1)} %get-tuple-element.25.refs_3_) | copy-start | bytes 1966084
  27.9 4.0 %collective-permute-start.4 = (bf16[320,1024]{1,0:T(8,128)(2,1)S(1)}, bf16[320,1024]{1,0:T(8,128)(2,1)S(1)}, u32[]{:S(2)}, u32[]{:S(2)}) collective-permute-start(bf16[320,1024]{1,0:T(8,128)(2,1)S(1)} %get-tuple-element.25.refs_3_), channel_id=1, source_target_pairs={{0,8},{8,0},{16,24},{24,16},{32,40},{40,32},{48,56},{56,48},{64,72... | collective-permute-start | bytes 1966088 | tf_op jit(solution)/shard_map/ppermute | solution.py:32
  29.9 19.4 %collective-permute-start.3 = (bf16[128,1024]{1,0:T(8,128)(2,1)S(1)}, bf16[128,1024]{1,0:T(8,128)(2,1)S(1)}, u32[]{:S(2)}, u32[]{:S(2)}) collective-permute-start(bf16[128,1024]{1,0:T(8,128)(2,1)S(1)} %get-tuple-element.24.three_ref), channel_id=1, source_target_pairs={{0,64},{8,72},{16,80},{24,88},{32,96},{40,104},{48,112},{56,120},{... | collective-permute-start | bytes 786440 | tf_op jit(solution)/shard_map/ppermute | solution.py:32
  32.6 22.3 %collective-permute-start.5 = (bf16[128,1024]{1,0:T(8,128)(2,1)S(1)}, bf16[128,1024]{1,0:T(8,128)(2,1)S(1)}, u32[]{:S(2)}, u32[]{:S(2)}) collective-permute-start(bf16[128,1024]{1,0:T(8,128)(2,1)S(1)} %get-tuple-element.26), channel_id=1, source_target_pairs={{0,128},{8,200},{16,144},{24,216},{32,160},{40,232},{48,176},{56,2... | collective-permute-start | bytes 786440 | tf_op jit(solution)/shard_map/ppermute | solution.py:32
  38.7 57.1 %collective-permute-start.10 = (bf16[512,1024]{1,0:T(8,128)(2,1)}, bf16[512,1024]{1,0:T(8,128)(2,1)}, u32[]{:S(2)}, u32[]{:S(2)}) collective-permute-start(bf16[512,1024]{1,0:T(8,128)(2,1)} %get-tuple-element.29), channel_id=1, source_target_pairs={{0,8},{8,0},{16,24},{24,16},{32,40},{40,32},{48,56},{56,48},{64,72... | collective-permute-start | bytes 3145736 | tf_op jit(solution)/shard_map/ppermute | solution.py:32
  41.0 15.4 %collective-permute-start.6 = (bf16[64,1024]{1,0:T(8,128)(2,1)S(1)}, bf16[64,1024]{1,0:T(8,128)(2,1)S(1)}, u32[]{:S(2)}, u32[]{:S(2)}) collective-permute-start(bf16[64,1024]{1,0:T(8,128)(2,1)S(1)} %get-tuple-element.27), channel_id=1, source_target_pairs={{0,320},{8,264},{16,336},{24,280},{32,352},{40,296},{48,368},{56,3... | collective-permute-start | bytes 393224 | tf_op jit(solution)/shard_map/ppermute | solution.py:32
  49.3 12.2 %collective-permute-start.7 = (bf16[64,1024]{1,0:T(8,128)(2,1)S(1)}, bf16[64,1024]{1,0:T(8,128)(2,1)S(1)}, u32[]{:S(2)}, u32[]{:S(2)}) collective-permute-start(bf16[64,1024]{1,0:T(8,128)(2,1)S(1)} %get-tuple-element.27), channel_id=1, source_target_pairs={{0,384},{8,456},{16,400},{24,472},{32,416},{40,488},{48,432},{56,5... | collective-permute-start | bytes 393224 | tf_op jit(solution)/shard_map/ppermute | solution.py:32
  61.6 46.2 %collective-permute-start.8 = (bf16[384,1024]{1,0:T(8,128)(2,1)S(1)}, bf16[384,1024]{1,0:T(8,128)(2,1)S(1)}, u32[]{:S(2)}, u32[]{:S(2)}) collective-permute-start(bf16[384,1024]{1,0:T(8,128)(2,1)S(1)} %constant_dynamic-update-slice_fusion.refs_2_), channel_id=1, source_target_pairs={{0,8},{8,0},{16,24},{24,16},{32,40},{40,32},{48,56},{56,48},{64,72... | collective-permute-start | bytes 2359304 | tf_op jit(solution)/shard_map/ppermute | solution.py:32
  65.6 37.3 %collective-permute-start.9 = (bf16[256,1024]{1,0:T(8,128)(2,1)}, bf16[256,1024]{1,0:T(8,128)(2,1)}, u32[]{:S(2)}, u32[]{:S(2)}) collective-permute-start(bf16[256,1024]{1,0:T(8,128)(2,1)} %get-tuple-element.28), channel_id=1, source_target_pairs={{8,16},{16,8},{24,32},{32,24},{40,48},{48,40},{56,64},{64,56},{72,... | collective-permute-start | bytes 1572872 | tf_op jit(solution)/shard_map/ppermute | solution.py:32
  70.2 25.6 %copy-start.2 = (bf16[320,1024]{1,0:T(8,128)(2,1)S(1)}, bf16[320,1024]{1,0:T(8,128)(2,1)}, u32[]{:S(2)}) copy-start(bf16[320,1024]{1,0:T(8,128)(2,1)} %copy-done.1) | copy-start | bytes 1966084

commit v5 on v4

--- a/solution.py
+++ b/solution.py
@@ -17,6 +17,7 @@
 N_CTX = 64
 SCALE_LOG2 = (HD**-0.5) * 1.4426950408889634
 Q_TILE = 128
+STRIP = 1024
 BLOCK = 256
 TOTAL_LIMIT = 2.0**100
 VMEM_LIMIT = 24 * 2**20
@@ -40,8 +41,8 @@
     return index_of(z, y, 1 - core)
 
 
-def along_y(bits):
-    return lambda z, y, core: index_of(z, y ^ bits, core)
+def along_y(first, second):
+    return lambda z, y, core: index_of(z, y ^ (second if core else first), core)
 
 
 def along_z(first, second):
@@ -65,7 +66,7 @@
     return (total / jnp.float32(group**0.5)).astype(jnp.bfloat16)
 
 
-def first_kernel(core_ref, k_hbm, v_hbm, near_ref, far_ref, one_ref, two_ref, buf, sems):
+def first_kernel(core_ref, k_hbm, v_hbm, near_ref, far_hbm, one_ref, two_ref, buf, sems, far_sem):
     core = core_ref[0]
     by4 = pooling_matrix(BLOCK, 4)
     by2 = pooling_matrix(POOL, 2)
@@ -83,26 +84,34 @@
             cols = pl.ds(side * WIDTH, WIDTH)
             zero = pool(buf[pl.ds(part * BLOCK, BLOCK), cols], 4, by4)
             near_ref[pl.ds(part * (BLOCK // 4), BLOCK // 4), cols] = zero
+    first = pl.multiple_of(core * (TOK - EDGE), EDGE)
+    far = pltpu.make_async_copy(buf.at[pl.ds(first, EDGE), :], far_hbm, far_sem)
+    far.start()
     one = pool(near_ref[pl.ds(0, POOL), :], 2, by2)
     one_ref[...] = one
-    two_ref[...] = pool(one, 2, by2[: POOL // 4, : POOL // 2])
+    two = pool(one, 2, by2[: POOL // 4, : POOL // 2])
+    two_ref[...] = two
+    near_ref[pl.ds(POOL + EDGE, POOL // 4), :] = two
     last = pl.multiple_of((1 - core) * (TOK - EDGE), EDGE)
     near_ref[pl.ds(POOL, EDGE), :] = buf[pl.ds(last, EDGE), :]
-    first = pl.multiple_of(core * (TOK - EDGE), EDGE)
-    far_ref[...] = buf[pl.ds(first, EDGE), :]
+    far.wait()
 
 
 def first_pools(core, keys, values):
-    counts = (POOL + EDGE, EDGE, POOL // 2, POOL // 4)
-    hbm = pl.BlockSpec(memory_space=pltpu.HBM)
+    counts = (POOL + EDGE + POOL // 4, EDGE, POOL // 2, POOL // 4)
+    hbm, vmem = (pl.BlockSpec(memory_space=m) for m in (pltpu.HBM, pltpu.VMEM))
     return pl.pallas_call(
         first_kernel,
         in_specs=[pl.BlockSpec(memory_space=pltpu.SMEM), hbm, hbm],
-        out_specs=[pl.BlockSpec(memory_space=pltpu.VMEM)] * 4,
-        out_shape=[jax.ShapeDtypeStruct((r, 2 * WIDTH), jnp.bfloat16) for r in counts],
+        out_specs=[vmem, hbm, vmem, vmem],
+        out_shape=[
+            (pltpu.HBM if r == EDGE else jax.ShapeDtypeStruct)((r, 2 * WIDTH), jnp.bfloat16)
+            for r in counts
+        ],
         scratch_shapes=[
             pltpu.VMEM((TOK, 2 * WIDTH), jnp.bfloat16),
             pltpu.SemaphoreType.DMA((2 * TOK // BLOCK,)),
+            pltpu.SemaphoreType.DMA,
         ],
         compiler_params=pltpu.CompilerParams(vmem_limit_bytes=VMEM_LIMIT),
         cost_estimate=pl.CostEstimate(flops=10**8, bytes_accessed=4 * 2**20, transcendentals=0),
@@ -122,25 +131,28 @@
     )(*operands)
 
 
-def plane_kernel(own_ref, a_ref, b_ref, c_ref, got_ref, three_ref):
+def both_kernel(two_ref, near_ref, both_ref):
+    both_ref[pl.ds(0, 64), :] = two_ref[...]
+    both_ref[pl.ds(64, 64), :] = near_ref[pl.ds(512, 64), :]
+
+
+def threes(two, one_got, twos_got, by2):
+    rows = jnp.concatenate([pool(one_got, 2, by2[:64, :128]), twos_got, two], axis=0)
+    return pool(rows, 2, by2)
+
+
+def plane_kernel(two_ref, one_ref, twos_ref, got_ref, three_ref):
+    one, twos = one_ref[...], twos_ref[...]
+    got_ref[pl.ds(0, 128), :] = one
+    got_ref[pl.ds(128, 128), :] = twos
+    three_ref[...] = threes(two_ref[...], one, twos, pooling_matrix(256, 2))
+
+
+def wide_kernel(three_ref, got_ref, near_ref, fours_ref, fives_ref):
     by2 = pooling_matrix(256, 2)
-    a, b, c = a_ref[...], b_ref[...], c_ref[...]
-    own = own_ref[...]
-    got_ref[pl.ds(0, 128), :] = a
-    got_ref[pl.ds(128, 64), :] = b
-    got_ref[pl.ds(192, 64), :] = c
-    got_ref[pl.ds(256, 64), :] = own
-    rows = jnp.concatenate([pool(a, 2, by2[:64, :128]), b, c, own], axis=0)
-    three_ref[...] = pool(rows, 2, by2)
-
-
-def wide_kernel(three_ref, got_ref, fours_ref, fives_ref):
-    by2 = pooling_matrix(256, 2)
-    rows = jnp.concatenate(
-        [pool(got_ref[pl.ds(0, 128), :], 2, by2[:64, :128]), got_ref[pl.ds(128, 192), :]], axis=0
-    )
-    threes = jnp.concatenate([three_ref[...], pool(rows, 2, by2)], axis=0)
-    fours = pool(threes, 2, by2)
+    got = got_ref[pl.ds(0, 128), :], got_ref[pl.ds(128, 128), :]
+    other = threes(near_ref[pl.ds(512, 64), :], *got, by2)
+    fours = pool(jnp.concatenate([three_ref[...], other], axis=0), 2, by2)
     fours_ref[...] = fours
     fives_ref[...] = pool(fours, 2, by2[:64, :128])
 
@@ -169,80 +181,87 @@
             for at in range(2):
                 fetch(at, h).start()
 
-    def one_head(h, _):
-        def lanes(first):
-            return pl.ds(pl.multiple_of(first + h * HD, HD), HD)
-
-        sources = arrays
+    sources = held if fetched else arrays
+
+    def lanes(first, h):
+        if isinstance(h, int):
+            return pl.ds(first + h * HD, HD)
+        return pl.ds(pl.multiple_of(first + h * HD, HD), HD)
+
+    def pieces_of(h):
+        pieces = []
+        for k_at, v_at, first, count, v_lane, masked in plan:
+            rows = pl.ds(first, count)
+            k, v = sources[k_at][rows, lanes(0, h)], sources[v_at][rows, lanes(v_lane, h)]
+            pieces.append((k, v.T, masked))
+        return pieces
+
+    def put(h, rows, acc, peak, total):
+        if final:
+            refs[0][rows, lanes(0, h)] = (acc * (1.0 / total)).astype(jnp.bfloat16).T
+        else:
+            refs[0][h, :, rows] = acc
+            refs[1][h, :, rows] = peak
+            refs[2][h, :, rows] = total
+
+    def add(v, s, peak, total, acc):
+        p = jnp.exp2((s - peak) * SCALE_LOG2)
+        total = total + jnp.sum(p, axis=0, keepdims=True)
+        return total, acc + times(v, p.astype(jnp.bfloat16), ((1,), (0,)))
+
+    largest = []
+    for h in range(HEADS_DEV):
         if fetched:
             for at in range(2):
                 fetch(at, h).wait()
-            sources = held
-
-        def put(rows, acc, peak, total):
-            if final:
-                refs[0][rows, lanes(0)] = (acc * (1.0 / total)).astype(jnp.bfloat16).T
+        pieces = pieces_of(h)
+        for first in range(0, TOK, STRIP):
+            rows = pl.ds(first, STRIP)
+            query = q_ref[rows, lanes(0, h)]
+            acc, total = 0.0, 0.0
+            if carried:
+                acc, peak, total = acc_in[h, :, rows], m_in[h, :, rows], l_in[h, :, rows]
+                parts = pieces
             else:
-                refs[0][h, :, rows] = acc
-                refs[1][h, :, rows] = peak
-                refs[2][h, :, rows] = total
-
-        pieces = []
-        for k_at, v_at, first, count, v_lane, masked in plan:
-            rows = pl.ds(first, count)
-            k, v = sources[k_at][rows, lanes(0)], sources[v_at][rows, lanes(v_lane)]
-            pieces.append((k, v.T, masked))
-
-        query = q_ref[:, lanes(0)]
-        acc, total = 0.0, 0.0
-        if carried:
-            acc, peak, total = acc_in[h], m_in[h], l_in[h]
-            parts = pieces
-        else:
-            (k, v, masked), *rest = pieces
-            parts = [(k[:256], v[:, :256], masked), (k[256:], v[:, 256:], masked), *rest]
-            peak = None
-        for k, v, masked in parts:
-            s = times(k, query, ((1,), (1,)))
-            if masked:
-                s = s + bias
-            if peak is None:
-                peak = jnp.max(s, axis=0, keepdims=True)
-            p = jnp.exp2((s - peak) * SCALE_LOG2)
-            total = total + jnp.sum(p, axis=0, keepdims=True)
-            acc = acc + times(v, p.astype(jnp.bfloat16), ((1,), (0,)))
-        put(pl.ds(0, TOK), acc, peak, total)
-
-        @pl.when(jnp.logical_not(jnp.max(total) < TOTAL_LIMIT))
-        def _():
-            def one_tile(tile, _):
-                rows = pl.ds(pl.multiple_of(tile * Q_TILE, Q_TILE), Q_TILE)
-                query = q_ref[rows, lanes(0)]
-                scores = []
-                for k, _, masked in pieces:
-                    s = times(k, query, ((1,), (1,)))
-                    scores.append(s + bias if masked else s)
-                peaks = [jnp.max(s, axis=0, keepdims=True) for s in scores]
-                acc, total = 0.0, 0.0
-                if carried:
-                    before = m_in[h, :, rows]
-                    peaks.append(before)
-                peak = functools.reduce(jnp.maximum, peaks)
-                if carried:
-                    fade = jnp.exp2((before - peak) * SCALE_LOG2)
-                    acc, total = acc_in[h, :, rows] * fade, l_in[h, :, rows] * fade
-                for s, (_, v, _) in zip(scores, pieces):
-                    p = jnp.exp2((s - peak) * SCALE_LOG2)
-                    total = total + jnp.sum(p, axis=0, keepdims=True)
-                    acc = acc + times(v, p.astype(jnp.bfloat16), ((1,), (0,)))
-                put(rows, acc, peak, total)
-                return 0
-
-            lax.fori_loop(0, TOK // Q_TILE, one_tile, 0)
-
-        return 0
-
-    lax.fori_loop(0, HEADS_DEV, one_head, 0)
+                (k, v, masked), *rest = pieces
+                parts = [(k[:256], v[:, :256], masked), (k[256:], v[:, 256:], masked), *rest]
+                peak = None
+            for k, v, masked in parts:
+                s = times(k, query, ((1,), (1,)))
+                if masked:
+                    s = s + bias
+                if peak is None:
+                    peak = jnp.max(s, axis=0, keepdims=True)
+                total, acc = add(v, s, peak, total, acc)
+            put(h, rows, acc, peak, total)
+            largest.append(jnp.max(total, axis=1, keepdims=True))
+
+    @pl.when(jnp.logical_not(jnp.max(functools.reduce(jnp.maximum, largest)) < TOTAL_LIMIT))
+    def _():
+        def one_tile(index, _):
+            h = index // (TOK // Q_TILE)
+            rows = pl.ds(pl.multiple_of(index % (TOK // Q_TILE) * Q_TILE, Q_TILE), Q_TILE)
+            query = q_ref[rows, lanes(0, h)]
+            pieces = pieces_of(h)
+            scores = []
+            for k, _, masked in pieces:
+                s = times(k, query, ((1,), (1,)))
+                scores.append(s + bias if masked else s)
+            peaks = [jnp.max(s, axis=0, keepdims=True) for s in scores]
+            acc, total = 0.0, 0.0
+            if carried:
+                before = m_in[h, :, rows]
+                peaks.append(before)
+            peak = functools.reduce(jnp.maximum, peaks)
+            if carried:
+                fade = jnp.exp2((before - peak) * SCALE_LOG2)
+                acc, total = acc_in[h, :, rows] * fade, l_in[h, :, rows] * fade
+            for s, (k, v, _) in zip(scores, pieces):
+                total, acc = add(v, s, peak, total, acc)
+            put(h, rows, acc, peak, total)
+            return 0
+
+        lax.fori_loop(0, HEADS_DEV * (TOK // Q_TILE), one_tile, 0)
 
 
 def attend(bias, queries, arrays, plan, state, final, fetched=False):
@@ -286,17 +305,17 @@
     keys = pltpu.with_memory_space_constraint(keys, pltpu.HBM)
     values = pltpu.with_memory_space_constraint(values, pltpu.HBM)
     near, far, one, two = first_pools(core, keys, values)
-    got1 = swap(one, along_y(1))
-    got2 = swap(two, along_y(2))
-    got3 = swap(two, along_y(3))
     near_got = swap(near, other_core)
+    one_got = swap(one, along_y(1, 1))
+    (both,) = small_call(both_kernel, (128,), two, near_got)
+    twos_got = swap(both, along_y(2, 3))
     plan = ((0, 1, 0, TOK, 0, False),)
     state = attend(bias, queries, [keys, values], plan, (), False, fetched=True)
 
-    planes, three = small_call(plane_kernel, (320, 128), two, got1, got2, got3)
+    planes, three = small_call(plane_kernel, (256, 128), two, one_got, twos_got)
     planes_got = swap(planes, other_core)
     three_got = swap(three, along_z(1, 1))
-    fours, fives = small_call(wide_kernel, (128, 64), three, planes_got)
+    fours, fives = small_call(wide_kernel, (128, 64), three, planes_got, near_got)
     fours_got = swap(fours, along_z(2, 3))
     far_got = swap(far, beside)
     fives_c = swap(fives, along_z(5, 4))

time: 112 us -> 112 us (level)
  the two profiles are of different devices: /device:TPU:86 before, /device:TPU:33 now
where the time goes in v5:
time: 112 us
  starting transfers between devices  46.3 us (41%)
  Pallas kernels  42.8 us (38%)
  waiting for transfers between devices  19.6 us (18%)
  local copies, waits for them, and re-layouts  2.79 us (2%)
    ppermute x10, starting transfers between devices, swap(): return lax.ppermute(value, 'ctx', pairs)  46.3 us
    pallas_call x4, Pallas kernels, attend(): pl.pallas_call(functools.partial(attend_kernel, plan, bool(state), final,...  38.7 us
    ppermute x10, waiting for transfers between devices, swap(): return lax.ppermute(value, 'ctx', pairs)  19.6 us
    pallas_call x1, Pallas kernels, first_pools(): pl.pallas_call(first_kernel, in_specs=[pl.BlockSpec(memory_space=pltpu.SM...  3.02 us
  transfers between devices with their start and end apart: 10, of which 4 were waited for; matrix products, arithmetic and copies ran while one was open for 2% of the time, Pallas kernels for 33%

profile of v5, /device:TPU:33, one launch (start us, length us, event | category | flops | bytes accessed | tf_op | source)
XLA Modules:
  0.0 111.7 jit_solution(4065105986734520932)
XLA Ops:
  0.0 3.0 %first_pools.1 = (bf16[576,1024]{1,0:T(8,128)(2,1)S(1)}, bf16[256,1024]{1,0:T(8,128)(2,1)}, bf16[128,1024]{1,0:T(8,128)(2,1)S(1)}, bf16[64,1024]{1,0:T(8,128)(2,1)S(1)}) custom-call(s32[1]{0:T(128)} %bitcast.1.core_ref, bf16[1024,512]{1,0:T(8,128)(2,1)} %refs_2_.1, bf16[1024,512]{1,0:T(8,128)(2,1)} %refs_3_.1), custom_call_target="tpu_custom_call" | custom-call | flops 100000000 | bytes 4194304 | tf_op jit(solution)/shard_map/first_pools/pallas_call | solution.py:103
  3.0 2.6 %collective-permute-start.1 = (bf16[576,1024]{1,0:T(8,128)(2,1)S(1)}, bf16[576,1024]{1,0:T(8,128)(2,1)S(1)}, u32[]{:S(2)}, u32[]{:S(2)}) collective-permute-start(bf16[576,1024]{1,0:T(8,128)(2,1)S(1)} %get-tuple-element.24), channel_id=1, source_target_pairs={{0,8},{8,0},{16,24},{24,16},{32,40},{40,32},{48,56},{56,48},{64,72... | collective-permute-start | bytes 3538952 | tf_op jit(solution)/shard_map/ppermute | solution.py:33
  5.6 2.4 %collective-permute-start = (bf16[128,1024]{1,0:T(8,128)(2,1)S(1)}, bf16[128,1024]{1,0:T(8,128)(2,1)S(1)}, u32[]{:S(2)}, u32[]{:S(2)}) collective-permute-start(bf16[128,1024]{1,0:T(8,128)(2,1)S(1)} %get-tuple-element.23), channel_id=1, source_target_pairs={{0,16},{8,24},{16,0},{24,8},{32,48},{40,56},{48,32},{56,40},{64,80... | collective-permute-start | bytes 786440 | tf_op jit(solution)/shard_map/ppermute | solution.py:33
  8.0 0.0 collective-permute-done.1.near_ref.refs_2_
  8.1 0.0 copy-start
  8.1 7.0 %collective-permute-start.2 = (bf16[128,1024]{1,0:T(8,128)(2,1)S(1)}, bf16[128,1024]{1,0:T(8,128)(2,1)S(1)}, u32[]{:S(2)}, u32[]{:S(2)}) collective-permute-start(bf16[128,1024]{1,0:T(8,128)(2,1)S(1)} %shard_map.37), channel_id=1, source_target_pairs={{0,32},{8,56},{16,48},{24,40},{32,0},{40,24},{48,16},{56,8},{64,96... | collective-permute-start | bytes 786440 | tf_op jit(solution)/shard_map/ppermute | solution.py:33
  15.1 10.6 %collective-permute-done.one_ref = bf16[128,1024]{1,0:T(8,128)(2,1)S(1)} collective-permute-done((bf16[128,1024]{1,0:T(8,128)(2,1)S(1)}, bf16[128,1024]{1,0:T(8,128)(2,1)S(1)}, u32[]{:S(2)}, u32[]{:S(2)}) %collective-permute-start) | collective-permute-done | bytes 262176 | tf_op jit(solution)/shard_map/ppermute | solution.py:33
  25.7 1.0 collective-permute-done.2.twos_ref
  26.7 0.4 shard_map.38
  27.1 0.0 copy-start.1
  27.1 1.9 %collective-permute-start.4 = (bf16[256,1024]{1,0:T(8,128)(2,1)S(1)}, bf16[256,1024]{1,0:T(8,128)(2,1)S(1)}, u32[]{:S(2)}, u32[]{:S(2)}) collective-permute-start(bf16[256,1024]{1,0:T(8,128)(2,1)S(1)} %get-tuple-element.26.refs_3_), channel_id=1, source_target_pairs={{0,8},{8,0},{16,24},{24,16},{32,40},{40,32},{48,56},{56,48},{64,72... | collective-permute-start | bytes 1572872 | tf_op jit(solution)/shard_map/ppermute | solution.py:33
  29.0 4.4 %collective-permute-start.3 = (bf16[128,1024]{1,0:T(8,128)(2,1)S(1)}, bf16[128,1024]{1,0:T(8,128)(2,1)S(1)}, u32[]{:S(2)}, u32[]{:S(2)}) collective-permute-start(bf16[128,1024]{1,0:T(8,128)(2,1)S(1)} %get-tuple-element.25.three_ref), channel_id=1, source_target_pairs={{0,64},{8,72},{16,80},{24,88},{32,96},{40,104},{48,112},{56,120},{... | collective-permute-start | bytes 786440 | tf_op jit(solution)/shard_map/ppermute | solution.py:33
  33.4 0.0 collective-permute-done.4.got_ref.refs_4_
  33.4 0.7 shard_map.39
  34.1 5.5 %collective-permute-start.5 = (bf16[128,1024]{1,0:T(8,128)(2,1)S(1)}, bf16[128,1024]{1,0:T(8,128)(2,1)S(1)}, u32[]{:S(2)}, u32[]{:S(2)}) collective-permute-start(bf16[128,1024]{1,0:T(8,128)(2,1)S(1)} %get-tuple-element.27), channel_id=1, source_target_pairs={{0,128},{8,200},{16,144},{24,216},{32,160},{40,232},{48,176},{56,2... | collective-permute-start | bytes 786440 | tf_op jit(solution)/shard_map/ppermute | solution.py:33
  39.7 8.2 %collective-permute-start.6 = (bf16[64,1024]{1,0:T(8,128)(2,1)S(1)}, bf16[64,1024]{1,0:T(8,128)(2,1)S(1)}, u32[]{:S(2)}, u32[]{:S(2)}) collective-permute-start(bf16[64,1024]{1,0:T(8,128)(2,1)S(1)} %get-tuple-element.28), channel_id=1, source_target_pairs={{0,320},{8,264},{16,336},{24,280},{32,352},{40,296},{48,368},{56,3... | collective-permute-start | bytes 393224 | tf_op jit(solution)/shard_map/ppermute | solution.py:33
  47.9 0.0 collective-permute-done.3
  47.9 0.7 constant_dynamic-update-slice_fusion.3
  48.7 1.9 %collective-permute-start.7 = (bf16[64,1024]{1,0:T(8,128)(2,1)S(1)}, bf16[64,1024]{1,0:T(8,128)(2,1)S(1)}, u32[]{:S(2)}, u32[]{:S(2)}) collective-permute-start(bf16[64,1024]{1,0:T(8,128)(2,1)S(1)} %get-tuple-element.28), channel_id=1, source_target_pairs={{0,384},{8,456},{16,400},{24,472},{32,416},{40,488},{48,432},{56,5... | collective-permute-start | bytes 393224 | tf_op jit(solution)/shard_map/ppermute | solution.py:33
  50.6 0.0 collective-permute-done.5
  50.6 0.7 constant_dynamic-update-slice_fusion.2
  51.3 7.8 %collective-permute-done.6 = bf16[64,1024]{1,0:T(8,128)(2,1)S(1)} collective-permute-done((bf16[64,1024]{1,0:T(8,128)(2,1)S(1)}, bf16[64,1024]{1,0:T(8,128)(2,1)S(1)}, u32[]{:S(2)}, u32[]{:S(2)}) %collective-permute-start.6) | collective-permute-done | bytes 131104 | tf_op jit(solution)/shard_map/ppermute | solution.py:33
  59.1 0.7 constant_dynamic-update-slice_fusion.1
  59.7 0.2 collective-permute-done.7
  59.9 0.0 copy-done.1
  59.9 0.7 constant_dynamic-update-slice_fusion.refs_2_
  60.6 6.2 %collective-permute-start.8 = (bf16[384,1024]{1,0:T(8,128)(2,1)}, bf16[384,1024]{1,0:T(8,128)(2,1)S(1)}, u32[]{:S(2)}, u32[]{:S(2)}) collective-permute-start(bf16[384,1024]{1,0:T(8,128)(2,1)} %constant_dynamic-update-slice_fusion.refs_2_), channel_id=1, source_target_pairs={{0,8},{8,0},{16,24},{24,16},{32,40},{40,32},{48,56},{56,48},{64,72... | collective-permute-start | bytes 2359304 | tf_op jit(solution)/shard_map/ppermute | solution.py:33
  66.8 6.1 %collective-permute-start.9 = (bf16[256,1024]{1,0:T(8,128)(2,1)}, bf16[256,1024]{1,0:T(8,128)(2,1)}, u32[]{:S(2)}, u32[]{:S(2)}) collective-permute-start(bf16[256,1024]{1,0:T(8,128)(2,1)} %get-tuple-element.29), channel_id=1, source_target_pairs={{8,16},{16,8},{24,32},{32,24},{40,48},{48,40},{56,64},{64,56},{72,... | collective-permute-start | bytes 1572872 | tf_op jit(solution)/shard_map/ppermute | solution.py:33
  72.9 0.0 copy-done
  73.0 0.0 copy-start.2
  73.0 25.7 %shard_map.40 = (f32[4,128,1024]{2,1,0:T(8,128)S(1)}, f32[4,1,1024]{2,1,0:T(1,128)S(1)}, f32[4,1,1024]{2,1,0:T(1,128)S(1)}) custom-call(f32[1]{0:T(128)} %bitcast.refs_0_, bf16[1024,512]{1,0:T(8,128)(2,1)S(1)} %copy-done, bf16[1024,512]{1,0:T(8,128)(2,1)} %refs_2_.1, bf16[1024,512]{1,0:T(8,128)(2,1)} %refs_3_.1), custom_call_target="tpu_custom_call" | custom-call | flops 2147483648 | bytes 5242880 | tf_op jit(solution)/shard_map/pallas_call | solution.py:284
  98.6 0.0 copy-done.2
  98.7 5.4 %shard_map.41 = (f32[4,128,1024]{2,1,0:T(8,128)S(1)}, f32[4,1,1024]{2,1,0:T(1,128)S(1)}, f32[4,1,1024]{2,1,0:T(1,128)S(1)}) custom-call(f32[1]{0:T(128)} %bitcast.refs_0_, bf16[1024,512]{1,0:T(8,128)(2,1)S(1)} %copy-done, bf16[576,1024]{1,0:T(8,128)(2,1)S(1)} %collective-permute-done.1.near_ref.refs_2_, bf16[256,1024]{1,0:T(8,128)(2,1)S(1)} %copy-done.2, ...), custom_call_target="tpu_custom_call" | custom-call | flops 2147483648 | bytes 5242880 | tf_op jit(solution)/shard_map/pallas_call | solution.py:284
  104.0 0.0 collective-permute-done.9.refs_3_
  104.0 4.7 %shard_map.42 = (f32[4,128,1024]{2,1,0:T(8,128)S(1)}, f32[4,1,1024]{2,1,0:T(1,128)S(1)}, f32[4,1,1024]{2,1,0:T(1,128)S(1)}) custom-call(f32[1]{0:T(128)} %bitcast.refs_0_, bf16[1024,512]{1,0:T(8,128)(2,1)S(1)} %copy-done, bf16[384,1024]{1,0:T(8,128)(2,1)} %constant_dynamic-update-slice_fusion.refs_2_, bf16[256,1024]{1,0:T(8,128)(2,1)} %collective-permute-done.9.refs_3_, ...), custom_call_target="tpu_custom_call" | custom-call | flops 1342177280 | bytes 4456448 | tf_op jit(solution)/shard_map/pallas_call | solution.py:284
  108.8 0.0 collective-permute-done.8.refs_2_
  108.8 2.9 %shard_map.43 = bf16[1024,512]{1,0:T(8,128)(2,1)} custom-call(f32[1]{0:T(128)} %bitcast.refs_0_, bf16[1024,512]{1,0:T(8,128)(2,1)S(1)} %copy-done, bf16[384,1024]{1,0:T(8,128)(2,1)S(1)} %collective-permute-done.8.refs_2_, f32[4,128,1024]{2,1,0:T(8,128)S(1)} %get-tuple-element.36.refs_3_, f32[4,1,1024]{2,1,0:T(1,128)S(1)} %get-tuple-element.37.refs_4_, ...), custom_call_target="tpu_custom_call" | custom-call | flops 805306368 | bytes 3932160 | tf_op jit(solution)/shard_map/pallas_call | solution.py:284
  (1 shorter events, 0.0 us)
Async XLA Ops:
  3.0 5.0 %collective-permute-start.1 = (bf16[576,1024]{1,0:T(8,128)(2,1)S(1)}, bf16[576,1024]{1,0:T(8,128)(2,1)S(1)}, u32[]{:S(2)}, u32[]{:S(2)}) collective-permute-start(bf16[576,1024]{1,0:T(8,128)(2,1)S(1)} %get-tuple-element.24), channel_id=1, source_target_pairs={{0,8},{8,0},{16,24},{24,16},{32,40},{40,32},{48,56},{56,48},{64,72... | collective-permute-start | bytes 3538952 | tf_op jit(solution)/shard_map/ppermute | solution.py:33
  5.6 20.1 %collective-permute-start = (bf16[128,1024]{1,0:T(8,128)(2,1)S(1)}, bf16[128,1024]{1,0:T(8,128)(2,1)S(1)}, u32[]{:S(2)}, u32[]{:S(2)}) collective-permute-start(bf16[128,1024]{1,0:T(8,128)(2,1)S(1)} %get-tuple-element.23), channel_id=1, source_target_pairs={{0,16},{8,24},{16,0},{24,8},{32,48},{40,56},{48,32},{56,40},{64,80... | collective-permute-start | bytes 786440 | tf_op jit(solution)/shard_map/ppermute | solution.py:33
  8.1 64.9 %copy-start = (bf16[1024,512]{1,0:T(8,128)(2,1)S(1)}, bf16[1024,512]{1,0:T(8,128)(2,1)}, u32[]{:S(2)}) copy-start(bf16[1024,512]{1,0:T(8,128)(2,1)} %refs_1_.7) | copy-start | bytes 3145732
  8.1 18.6 %collective-permute-start.2 = (bf16[128,1024]{1,0:T(8,128)(2,1)S(1)}, bf16[128,1024]{1,0:T(8,128)(2,1)S(1)}, u32[]{:S(2)}, u32[]{:S(2)}) collective-permute-start(bf16[128,1024]{1,0:T(8,128)(2,1)S(1)} %shard_map.37), channel_id=1, source_target_pairs={{0,32},{8,56},{16,48},{24,40},{32,0},{40,24},{48,16},{56,8},{64,96... | collective-permute-start | bytes 786440 | tf_op jit(solution)/shard_map/ppermute | solution.py:33
  27.1 32.8 %copy-start.1 = (bf16[256,1024]{1,0:T(8,128)(2,1)}, bf16[256,1024]{1,0:T(8,128)(2,1)S(1)}, u32[]{:S(2)}) copy-start(bf16[256,1024]{1,0:T(8,128)(2,1)S(1)} %get-tuple-element.26.refs_3_) | copy-start | bytes 1572868
  27.1 6.3 %collective-permute-start.4 = (bf16[256,1024]{1,0:T(8,128)(2,1)S(1)}, bf16[256,1024]{1,0:T(8,128)(2,1)S(1)}, u32[]{:S(2)}, u32[]{:S(2)}) collective-permute-start(bf16[256,1024]{1,0:T(8,128)(2,1)S(1)} %get-tuple-element.26.refs_3_), channel_id=1, source_target_pairs={{0,8},{8,0},{16,24},{24,16},{32,40},{40,32},{48,56},{56,48},{64,72... | collective-permute-start | bytes 1572872 | tf_op jit(solution)/shard_map/ppermute | solution.py:33
  29.0 18.9 %collective-permute-start.3 = (bf16[128,1024]{1,0:T(8,128)(2,1)S(1)}, bf16[128,1024]{1,0:T(8,128)(2,1)S(1)}, u32[]{:S(2)}, u32[]{:S(2)}) collective-permute-start(bf16[128,1024]{1,0:T(8,128)(2,1)S(1)} %get-tuple-element.25.three_ref), channel_id=1, source_target_pairs={{0,64},{8,72},{16,80},{24,88},{32,96},{40,104},{48,112},{56,120},{... | collective-permute-start | bytes 786440 | tf_op jit(solution)/shard_map/ppermute | solution.py:33
  34.1 16.4 %collective-permute-start.5 = (bf16[128,1024]{1,0:T(8,128)(2,1)S(1)}, bf16[128,1024]{1,0:T(8,128)(2,1)S(1)}, u32[]{:S(2)}, u32[]{:S(2)}) collective-permute-start(bf16[128,1024]{1,0:T(8,128)(2,1)S(1)} %get-tuple-element.27), channel_id=1, source_target_pairs={{0,128},{8,200},{16,144},{24,216},{32,160},{40,232},{48,176},{56,2... | collective-permute-start | bytes 786440 | tf_op jit(solution)/shard_map/ppermute | solution.py:33
  39.7 19.4 %collective-permute-start.6 = (bf16[64,1024]{1,0:T(8,128)(2,1)S(1)}, bf16[64,1024]{1,0:T(8,128)(2,1)S(1)}, u32[]{:S(2)}, u32[]{:S(2)}) collective-permute-start(bf16[64,1024]{1,0:T(8,128)(2,1)S(1)} %get-tuple-element.28), channel_id=1, source_target_pairs={{0,320},{8,264},{16,336},{24,280},{32,352},{40,296},{48,368},{56,3... | collective-permute-start | bytes 393224 | tf_op jit(solution)/shard_map/ppermute | solution.py:33
  48.7 11.3 %collective-permute-start.7 = (bf16[64,1024]{1,0:T(8,128)(2,1)S(1)}, bf16[64,1024]{1,0:T(8,128)(2,1)S(1)}, u32[]{:S(2)}, u32[]{:S(2)}) collective-permute-start(bf16[64,1024]{1,0:T(8,128)(2,1)S(1)} %get-tuple-element.28), channel_id=1, source_target_pairs={{0,384},{8,456},{16,400},{24,472},{32,416},{40,488},{48,432},{56,5... | collective-permute-start | bytes 393224 | tf_op jit(solution)/shard_map/ppermute | solution.py:33
  60.6 48.2 %collective-permute-start.8 = (bf16[384,1024]{1,0:T(8,128)(2,1)}, bf16[384,1024]{1,0:T(8,128)(2,1)S(1)}, u32[]{:S(2)}, u32[]{:S(2)}) collective-permute-start(bf16[384,1024]{1,0:T(8,128)(2,1)} %constant_dynamic-update-slice_fusion.refs_2_), channel_id=1, source_target_pairs={{0,8},{8,0},{16,24},{24,16},{32,40},{40,32},{48,56},{56,48},{64,72... | collective-permute-start | bytes 2359304 | tf_op jit(solution)/shard_map/ppermute | solution.py:33
  66.8 37.2 %collective-permute-start.9 = (bf16[256,1024]{1,0:T(8,128)(2,1)}, bf16[256,1024]{1,0:T(8,128)(2,1)}, u32[]{:S(2)}, u32[]{:S(2)}) collective-permute-start(bf16[256,1024]{1,0:T(8,128)(2,1)} %get-tuple-element.29), channel_id=1, source_target_pairs={{8,16},{16,8},{24,32},{32,24},{40,48},{48,40},{56,64},{64,56},{72,... | collective-permute-start | bytes 1572872 | tf_op jit(solution)/shard_map/ppermute | solution.py:33
  73.0 25.7 %copy-start.2 = (bf16[256,1024]{1,0:T(8,128)(2,1)S(1)}, bf16[256,1024]{1,0:T(8,128)(2,1)}, u32[]{:S(2)}) copy-start(bf16[256,1024]{1,0:T(8,128)(2,1)} %copy-done.1) | copy-start | bytes 1572868

commit v6 on v5

--- a/solution.py
+++ b/solution.py
@@ -305,31 +305,32 @@
     keys = pltpu.with_memory_space_constraint(keys, pltpu.HBM)
     values = pltpu.with_memory_space_constraint(values, pltpu.HBM)
     near, far, one, two = first_pools(core, keys, values)
+    one_got = swap(one, along_y(1, 1))
     near_got = swap(near, other_core)
-    one_got = swap(one, along_y(1, 1))
     (both,) = small_call(both_kernel, (128,), two, near_got)
     twos_got = swap(both, along_y(2, 3))
     plan = ((0, 1, 0, TOK, 0, False),)
     state = attend(bias, queries, [keys, values], plan, (), False, fetched=True)
+    plan = ((0, 0, 0, 512, WIDTH, False),)
+    state = attend(bias, queries, [near_got], plan, state, False)
 
     planes, three = small_call(plane_kernel, (256, 128), two, one_got, twos_got)
     planes_got = swap(planes, other_core)
     three_got = swap(three, along_z(1, 1))
     fours, fives = small_call(wide_kernel, (128, 64), three, planes_got, near_got)
     fours_got = swap(fours, along_z(2, 3))
-    far_got = swap(far, beside)
     fives_c = swap(fives, along_z(5, 4))
     fives_d = swap(fives, along_z(6, 7))
-    plan = ((0, 0, 0, 512, WIDTH, False), (1, 1, 0, 256, WIDTH, False))
-    plan += ((2, 2, 0, 256, WIDTH, False),)
-    state = attend(bias, queries, [near_got, planes, planes_got], plan, state, False)
+    far_got = swap(far, beside)
+    plan = ((0, 0, 0, 256, WIDTH, False), (1, 1, 0, 256, WIDTH, False))
+    state = attend(bias, queries, [planes, planes_got], plan, state, False)
 
     upper = jnp.concatenate([three_got, fours_got, fives_c, fives_d], axis=0)
     upper_got = swap(upper, other_core)
-    plan = ((0, 0, 0, 384, WIDTH, False), (1, 1, 0, 256, WIDTH, True))
-    state = attend(bias, queries, [upper, far_got], plan, state, False)
     plan = ((0, 0, 0, 384, WIDTH, False),)
-    return attend(bias, queries, [upper_got], plan, state, True)
+    state = attend(bias, queries, [upper], plan, state, False)
+    plan += ((1, 1, 0, 256, WIDTH, True),)
+    return attend(bias, queries, [upper_got, far_got], plan, state, True)
 
 
 def solution(mesh):

time: 112 us -> 111 us (level)
  the two profiles are of different devices: /device:TPU:33 before, /device:TPU:39 now
where the time goes in v6:
time: 111 us
  Pallas kernels  43 us (39%)
  starting transfers between devices  41.5 us (37%)
  waiting for transfers between devices  25.8 us (23%)
    ppermute x10, starting transfers between devices, swap(): return lax.ppermute(value, 'ctx', pairs)  41.5 us
    pallas_call x5, Pallas kernels, attend(): pl.pallas_call(functools.partial(attend_kernel, plan, bool(state), final,...  38.9 us
    ppermute x10, waiting for transfers between devices, swap(): return lax.ppermute(value, 'ctx', pairs)  25.8 us
    pallas_call x1, Pallas kernels, first_pools(): pl.pallas_call(first_kernel, in_specs=[pl.BlockSpec(memory_space=pltpu.SM...  3 us
  transfers between devices with their start and end apart: 10, of which 4 were waited for; matrix products, arithmetic and copies ran while one was open for 0% of the time, Pallas kernels for 31%

profile of v6, /device:TPU:39, one launch (start us, length us, event | category | flops | bytes accessed | tf_op | source)
XLA Modules:
  0.0 110.6 jit_solution(5955145311710679719)
XLA Ops:
  0.0 3.0 %first_pools.1 = (bf16[576,1024]{1,0:T(8,128)(2,1)S(1)}, bf16[256,1024]{1,0:T(8,128)(2,1)}, bf16[128,1024]{1,0:T(8,128)(2,1)S(1)}, bf16[64,1024]{1,0:T(8,128)(2,1)S(1)}) custom-call(s32[1]{0:T(128)} %bitcast.1.core_ref, bf16[1024,512]{1,0:T(8,128)(2,1)} %refs_2_.1, bf16[1024,512]{1,0:T(8,128)(2,1)} %refs_3_.1), custom_call_target="tpu_custom_call" | custom-call | flops 100000000 | bytes 4194304 | tf_op jit(solution)/shard_map/first_pools/pallas_call | solution.py:103
  3.0 2.6 %collective-permute-start.1 = (bf16[576,1024]{1,0:T(8,128)(2,1)S(1)}, bf16[576,1024]{1,0:T(8,128)(2,1)S(1)}, u32[]{:S(2)}, u32[]{:S(2)}) collective-permute-start(bf16[576,1024]{1,0:T(8,128)(2,1)S(1)} %get-tuple-element.27), channel_id=1, source_target_pairs={{0,8},{8,0},{16,24},{24,16},{32,40},{40,32},{48,56},{56,48},{64,72... | collective-permute-start | bytes 3538952 | tf_op jit(solution)/shard_map/ppermute | solution.py:33
  5.6 2.4 %collective-permute-start = (bf16[128,1024]{1,0:T(8,128)(2,1)S(1)}, bf16[128,1024]{1,0:T(8,128)(2,1)S(1)}, u32[]{:S(2)}, u32[]{:S(2)}) collective-permute-start(bf16[128,1024]{1,0:T(8,128)(2,1)S(1)} %get-tuple-element.26), channel_id=1, source_target_pairs={{0,16},{8,24},{16,0},{24,8},{32,48},{40,56},{48,32},{56,40},{64,80... | collective-permute-start | bytes 786440 | tf_op jit(solution)/shard_map/ppermute | solution.py:33
  8.0 0.0 collective-permute-done.1.near_ref.refs_2_
  8.1 0.0 copy-start
  8.1 2.1 %collective-permute-start.2 = (bf16[128,1024]{1,0:T(8,128)(2,1)S(1)}, bf16[128,1024]{1,0:T(8,128)(2,1)S(1)}, u32[]{:S(2)}, u32[]{:S(2)}) collective-permute-start(bf16[128,1024]{1,0:T(8,128)(2,1)S(1)} %shard_map.37), channel_id=1, source_target_pairs={{0,32},{8,56},{16,48},{24,40},{32,0},{40,24},{48,16},{56,8},{64,96... | collective-permute-start | bytes 786440 | tf_op jit(solution)/shard_map/ppermute | solution.py:33
  10.2 16.2 %collective-permute-done.one_ref = bf16[128,1024]{1,0:T(8,128)(2,1)S(1)} collective-permute-done((bf16[128,1024]{1,0:T(8,128)(2,1)S(1)}, bf16[128,1024]{1,0:T(8,128)(2,1)S(1)}, u32[]{:S(2)}, u32[]{:S(2)}) %collective-permute-start) | collective-permute-done | bytes 262176 | tf_op jit(solution)/shard_map/ppermute | solution.py:33
  26.4 0.5 collective-permute-done.2.twos_ref
  26.9 0.4 shard_map.38
  27.3 0.0 copy-start.1
  27.3 2.1 %collective-permute-start.4 = (bf16[256,1024]{1,0:T(8,128)(2,1)S(1)}, bf16[256,1024]{1,0:T(8,128)(2,1)S(1)}, u32[]{:S(2)}, u32[]{:S(2)}) collective-permute-start(bf16[256,1024]{1,0:T(8,128)(2,1)S(1)} %get-tuple-element.29.refs_2_), channel_id=1, source_target_pairs={{0,8},{8,0},{16,24},{24,16},{32,40},{40,32},{48,56},{56,48},{64,72... | collective-permute-start | bytes 1572872 | tf_op jit(solution)/shard_map/ppermute | solution.py:33
  29.4 4.0 %collective-permute-start.3 = (bf16[128,1024]{1,0:T(8,128)(2,1)S(1)}, bf16[128,1024]{1,0:T(8,128)(2,1)S(1)}, u32[]{:S(2)}, u32[]{:S(2)}) collective-permute-start(bf16[128,1024]{1,0:T(8,128)(2,1)S(1)} %get-tuple-element.28.three_ref), channel_id=1, source_target_pairs={{0,64},{8,72},{16,80},{24,88},{32,96},{40,104},{48,112},{56,120},{... | collective-permute-start | bytes 786440 | tf_op jit(solution)/shard_map/ppermute | solution.py:33
  33.4 0.0 collective-permute-done.4.got_ref.refs_3_
  33.4 0.7 shard_map.39
  34.1 5.6 %collective-permute-start.5 = (bf16[128,1024]{1,0:T(8,128)(2,1)S(1)}, bf16[128,1024]{1,0:T(8,128)(2,1)S(1)}, u32[]{:S(2)}, u32[]{:S(2)}) collective-permute-start(bf16[128,1024]{1,0:T(8,128)(2,1)S(1)} %get-tuple-element.30), channel_id=1, source_target_pairs={{0,128},{8,200},{16,144},{24,216},{32,160},{40,232},{48,176},{56,2... | collective-permute-start | bytes 786440 | tf_op jit(solution)/shard_map/ppermute | solution.py:33
  39.7 8.2 %collective-permute-start.6 = (bf16[64,1024]{1,0:T(8,128)(2,1)S(1)}, bf16[64,1024]{1,0:T(8,128)(2,1)S(1)}, u32[]{:S(2)}, u32[]{:S(2)}) collective-permute-start(bf16[64,1024]{1,0:T(8,128)(2,1)S(1)} %get-tuple-element.31), channel_id=1, source_target_pairs={{0,320},{8,264},{16,336},{24,280},{32,352},{40,296},{48,368},{56,3... | collective-permute-start | bytes 393224 | tf_op jit(solution)/shard_map/ppermute | solution.py:33
  47.9 0.0 collective-permute-done.3
  47.9 1.9 %collective-permute-start.7 = (bf16[64,1024]{1,0:T(8,128)(2,1)S(1)}, bf16[64,1024]{1,0:T(8,128)(2,1)S(1)}, u32[]{:S(2)}, u32[]{:S(2)}) collective-permute-start(bf16[64,1024]{1,0:T(8,128)(2,1)S(1)} %get-tuple-element.31), channel_id=1, source_target_pairs={{0,384},{8,456},{16,400},{24,472},{32,416},{40,488},{48,432},{56,5... | collective-permute-start | bytes 393224 | tf_op jit(solution)/shard_map/ppermute | solution.py:33
  49.9 0.0 collective-permute-done.5
  49.9 8.8 %collective-permute-done.6 = bf16[64,1024]{1,0:T(8,128)(2,1)S(1)} collective-permute-done((bf16[64,1024]{1,0:T(8,128)(2,1)S(1)}, bf16[64,1024]{1,0:T(8,128)(2,1)S(1)}, u32[]{:S(2)}, u32[]{:S(2)}) %collective-permute-start.6) | collective-permute-done | bytes 131104 | tf_op jit(solution)/shard_map/ppermute | solution.py:33
  58.7 0.3 collective-permute-done.7
  59.0 0.0 copy-done.1
  59.1 6.5 %collective-permute-start.8 = (bf16[384,1024]{1,0:T(8,128)(2,1)S(1)}, bf16[384,1024]{1,0:T(8,128)(2,1)}, u32[]{:S(2)}, u32[]{:S(2)}) collective-permute-start(bf16[384,1024]{1,0:T(8,128)(2,1)S(1)} %constant_dynamic-update-slice_fusion.refs_2_), channel_id=1, source_target_pairs={{0,8},{8,0},{16,24},{24,16},{32,40},{40,32},{48,56},{56,48},{64,72... | collective-permute-start | bytes 2359304 | tf_op jit(solution)/shard_map/ppermute | solution.py:33
  65.5 6.1 %collective-permute-start.9 = (bf16[256,1024]{1,0:T(8,128)(2,1)}, bf16[256,1024]{1,0:T(8,128)(2,1)}, u32[]{:S(2)}, u32[]{:S(2)}) collective-permute-start(bf16[256,1024]{1,0:T(8,128)(2,1)} %get-tuple-element.32), channel_id=1, source_target_pairs={{8,16},{16,8},{24,32},{32,24},{40,48},{48,40},{56,64},{64,56},{72,... | collective-permute-start | bytes 1572872 | tf_op jit(solution)/shard_map/ppermute | solution.py:33
  71.7 0.0 copy-done
  71.7 25.6 %shard_map.40 = (f32[4,128,1024]{2,1,0:T(8,128)S(1)}, f32[4,1,1024]{2,1,0:T(1,128)S(1)}, f32[4,1,1024]{2,1,0:T(1,128)S(1)}) custom-call(f32[1]{0:T(128)} %bitcast.refs_0_, bf16[1024,512]{1,0:T(8,128)(2,1)S(1)} %copy-done, bf16[1024,512]{1,0:T(8,128)(2,1)} %refs_2_.1, bf16[1024,512]{1,0:T(8,128)(2,1)} %refs_3_.1), custom_call_target="tpu_custom_call" | custom-call | flops 2147483648 | bytes 5242880 | tf_op jit(solution)/shard_map/pallas_call | solution.py:284
  97.3 0.0 copy-start.2
  97.3 2.5 %shard_map.41 = (f32[4,128,1024]{2,1,0:T(8,128)S(1)}, f32[4,1,1024]{2,1,0:T(1,128)S(1)}, f32[4,1,1024]{2,1,0:T(1,128)S(1)}) custom-call(f32[1]{0:T(128)} %bitcast.refs_0_, bf16[1024,512]{1,0:T(8,128)(2,1)S(1)} %copy-done, bf16[576,1024]{1,0:T(8,128)(2,1)S(1)} %collective-permute-done.1.near_ref.refs_2_, f32[4,128,1024]{2,1,0:T(8,128)S(1)} %get-tuple-element.33.refs_3_, ...), custom_call_target="tpu_custom_call" | custom-call | flops 1073741824 | bytes 4194304 | tf_op jit(solution)/shard_map/pallas_call | solution.py:284
  99.9 0.0 copy-done.2
  99.9 3.1 %shard_map.42 = (f32[4,128,1024]{2,1,0:T(8,128)S(1)}, f32[4,1,1024]{2,1,0:T(1,128)S(1)}, f32[4,1,1024]{2,1,0:T(1,128)S(1)}) custom-call(f32[1]{0:T(128)} %bitcast.refs_0_, bf16[1024,512]{1,0:T(8,128)(2,1)S(1)} %copy-done, bf16[256,1024]{1,0:T(8,128)(2,1)S(1)} %copy-done.2, bf16[256,1024]{1,0:T(8,128)(2,1)S(1)} %collective-permute-done.4.got_ref.refs_3_, ...), custom_call_target="tpu_custom_call" | custom-call | flops 1073741824 | bytes 4194304 | tf_op jit(solution)/shard_map/pallas_call | solution.py:284
  102.9 1.9 %shard_map.43 = (f32[4,128,1024]{2,1,0:T(8,128)S(1)}, f32[4,1,1024]{2,1,0:T(1,128)S(1)}, f32[4,1,1024]{2,1,0:T(1,128)S(1)}) custom-call(f32[1]{0:T(128)} %bitcast.refs_0_, bf16[1024,512]{1,0:T(8,128)(2,1)S(1)} %copy-done, bf16[384,1024]{1,0:T(8,128)(2,1)S(1)} %constant_dynamic-update-slice_fusion.refs_2_, f32[4,128,1024]{2,1,0:T(8,128)S(1)} %get-tuple-element.39.refs_3_, ...), custom_call_target="tpu_custom_call" | custom-call | flops 805306368 | bytes 3932160 | tf_op jit(solution)/shard_map/pallas_call | solution.py:284
  104.8 0.0 collective-permute-done.9.refs_3_
  104.9 0.0 collective-permute-done.8.refs_2_
  104.9 5.8 %shard_map.44 = bf16[1024,512]{1,0:T(8,128)(2,1)} custom-call(f32[1]{0:T(128)} %bitcast.refs_0_, bf16[1024,512]{1,0:T(8,128)(2,1)S(1)} %copy-done, bf16[384,1024]{1,0:T(8,128)(2,1)} %collective-permute-done.8.refs_2_, bf16[256,1024]{1,0:T(8,128)(2,1)} %collective-permute-done.9.refs_3_, f32[4,128,1024]{2,1,0:T(8,128)S(1)} %get-tuple-element.42.refs_4_, ...), custom_call_target="tpu_custom_call" | custom-call | flops 1342177280 | bytes 4456448 | tf_op jit(solution)/shard_map/pallas_call | solution.py:284
  (5 shorter events, 0.1 us)
Async XLA Ops:
  3.0 5.0 %collective-permute-start.1 = (bf16[576,1024]{1,0:T(8,128)(2,1)S(1)}, bf16[576,1024]{1,0:T(8,128)(2,1)S(1)}, u32[]{:S(2)}, u32[]{:S(2)}) collective-permute-start(bf16[576,1024]{1,0:T(8,128)(2,1)S(1)} %get-tuple-element.27), channel_id=1, source_target_pairs={{0,8},{8,0},{16,24},{24,16},{32,40},{40,32},{48,56},{56,48},{64,72... | collective-permute-start | bytes 3538952 | tf_op jit(solution)/shard_map/ppermute | solution.py:33
  5.6 20.8 %collective-permute-start = (bf16[128,1024]{1,0:T(8,128)(2,1)S(1)}, bf16[128,1024]{1,0:T(8,128)(2,1)S(1)}, u32[]{:S(2)}, u32[]{:S(2)}) collective-permute-start(bf16[128,1024]{1,0:T(8,128)(2,1)S(1)} %get-tuple-element.26), channel_id=1, source_target_pairs={{0,16},{8,24},{16,0},{24,8},{32,48},{40,56},{48,32},{56,40},{64,80... | collective-permute-start | bytes 786440 | tf_op jit(solution)/shard_map/ppermute | solution.py:33
  8.1 63.6 %copy-start = (bf16[1024,512]{1,0:T(8,128)(2,1)S(1)}, bf16[1024,512]{1,0:T(8,128)(2,1)}, u32[]{:S(2)}) copy-start(bf16[1024,512]{1,0:T(8,128)(2,1)} %refs_1_.9) | copy-start | bytes 3145732
  8.1 18.8 %collective-permute-start.2 = (bf16[128,1024]{1,0:T(8,128)(2,1)S(1)}, bf16[128,1024]{1,0:T(8,128)(2,1)S(1)}, u32[]{:S(2)}, u32[]{:S(2)}) collective-permute-start(bf16[128,1024]{1,0:T(8,128)(2,1)S(1)} %shard_map.37), channel_id=1, source_target_pairs={{0,32},{8,56},{16,48},{24,40},{32,0},{40,24},{48,16},{56,8},{64,96... | collective-permute-start | bytes 786440 | tf_op jit(solution)/shard_map/ppermute | solution.py:33
  27.3 31.7 %copy-start.1 = (bf16[256,1024]{1,0:T(8,128)(2,1)}, bf16[256,1024]{1,0:T(8,128)(2,1)S(1)}, u32[]{:S(2)}) copy-start(bf16[256,1024]{1,0:T(8,128)(2,1)S(1)} %get-tuple-element.29.refs_2_) | copy-start | bytes 1572868
  27.3 6.1 %collective-permute-start.4 = (bf16[256,1024]{1,0:T(8,128)(2,1)S(1)}, bf16[256,1024]{1,0:T(8,128)(2,1)S(1)}, u32[]{:S(2)}, u32[]{:S(2)}) collective-permute-start(bf16[256,1024]{1,0:T(8,128)(2,1)S(1)} %get-tuple-element.29.refs_2_), channel_id=1, source_target_pairs={{0,8},{8,0},{16,24},{24,16},{32,40},{40,32},{48,56},{56,48},{64,72... | collective-permute-start | bytes 1572872 | tf_op jit(solution)/shard_map/ppermute | solution.py:33
  29.4 18.5 %collective-permute-start.3 = (bf16[128,1024]{1,0:T(8,128)(2,1)S(1)}, bf16[128,1024]{1,0:T(8,128)(2,1)S(1)}, u32[]{:S(2)}, u32[]{:S(2)}) collective-permute-start(bf16[128,1024]{1,0:T(8,128)(2,1)S(1)} %get-tuple-element.28.three_ref), channel_id=1, source_target_pairs={{0,64},{8,72},{16,80},{24,88},{32,96},{40,104},{48,112},{56,120},{... | collective-permute-start | bytes 786440 | tf_op jit(solution)/shard_map/ppermute | solution.py:33
  34.1 15.7 %collective-permute-start.5 = (bf16[128,1024]{1,0:T(8,128)(2,1)S(1)}, bf16[128,1024]{1,0:T(8,128)(2,1)S(1)}, u32[]{:S(2)}, u32[]{:S(2)}) collective-permute-start(bf16[128,1024]{1,0:T(8,128)(2,1)S(1)} %get-tuple-element.30), channel_id=1, source_target_pairs={{0,128},{8,200},{16,144},{24,216},{32,160},{40,232},{48,176},{56,2... | collective-permute-start | bytes 786440 | tf_op jit(solution)/shard_map/ppermute | solution.py:33
  39.7 19.0 %collective-permute-start.6 = (bf16[64,1024]{1,0:T(8,128)(2,1)S(1)}, bf16[64,1024]{1,0:T(8,128)(2,1)S(1)}, u32[]{:S(2)}, u32[]{:S(2)}) collective-permute-start(bf16[64,1024]{1,0:T(8,128)(2,1)S(1)} %get-tuple-element.31), channel_id=1, source_target_pairs={{0,320},{8,264},{16,336},{24,280},{32,352},{40,296},{48,368},{56,3... | collective-permute-start | bytes 393224 | tf_op jit(solution)/shard_map/ppermute | solution.py:33
  47.9 11.1 %collective-permute-start.7 = (bf16[64,1024]{1,0:T(8,128)(2,1)S(1)}, bf16[64,1024]{1,0:T(8,128)(2,1)S(1)}, u32[]{:S(2)}, u32[]{:S(2)}) collective-permute-start(bf16[64,1024]{1,0:T(8,128)(2,1)S(1)} %get-tuple-element.31), channel_id=1, source_target_pairs={{0,384},{8,456},{16,400},{24,472},{32,416},{40,488},{48,432},{56,5... | collective-permute-start | bytes 393224 | tf_op jit(solution)/shard_map/ppermute | solution.py:33
  59.1 45.8 %collective-permute-start.8 = (bf16[384,1024]{1,0:T(8,128)(2,1)S(1)}, bf16[384,1024]{1,0:T(8,128)(2,1)}, u32[]{:S(2)}, u32[]{:S(2)}) collective-permute-start(bf16[384,1024]{1,0:T(8,128)(2,1)S(1)} %constant_dynamic-update-slice_fusion.refs_2_), channel_id=1, source_target_pairs={{0,8},{8,0},{16,24},{24,16},{32,40},{40,32},{48,56},{56,48},{64,72... | collective-permute-start | bytes 2359304 | tf_op jit(solution)/shard_map/ppermute | solution.py:33
  65.5 39.3 %collective-permute-start.9 = (bf16[256,1024]{1,0:T(8,128)(2,1)}, bf16[256,1024]{1,0:T(8,128)(2,1)}, u32[]{:S(2)}, u32[]{:S(2)}) collective-permute-start(bf16[256,1024]{1,0:T(8,128)(2,1)} %get-tuple-element.32), channel_id=1, source_target_pairs={{8,16},{16,8},{24,32},{32,24},{40,48},{48,40},{56,64},{64,56},{72,... | collective-permute-start | bytes 1572872 | tf_op jit(solution)/shard_map/ppermute | solution.py:33
  97.3 2.5 %copy-start.2 = (bf16[256,1024]{1,0:T(8,128)(2,1)S(1)}, bf16[256,1024]{1,0:T(8,128)(2,1)}, u32[]{:S(2)}) copy-start(bf16[256,1024]{1,0:T(8,128)(2,1)} %copy-done.1) | copy-start | bytes 1572868

commit v7 on v6

--- a/solution.py
+++ b/solution.py
@@ -105,8 +105,7 @@
         in_specs=[pl.BlockSpec(memory_space=pltpu.SMEM), hbm, hbm],
         out_specs=[vmem, hbm, vmem, vmem],
         out_shape=[
-            (pltpu.HBM if r == EDGE else jax.ShapeDtypeStruct)((r, 2 * WIDTH), jnp.bfloat16)
-            for r in counts
+            (pltpu.HBM if r == EDGE else pltpu.VMEM)((r, 2 * WIDTH), jnp.bfloat16) for r in counts
         ],
         scratch_shapes=[
             pltpu.VMEM((TOK, 2 * WIDTH), jnp.bfloat16),
@@ -148,10 +147,10 @@
     three_ref[...] = threes(two_ref[...], one, twos, pooling_matrix(256, 2))
 
 
-def wide_kernel(three_ref, got_ref, near_ref, fours_ref, fives_ref):
+def wide_kernel(three_ref, got_ref, both_ref, fours_ref, fives_ref):
     by2 = pooling_matrix(256, 2)
     got = got_ref[pl.ds(0, 128), :], got_ref[pl.ds(128, 128), :]
-    other = threes(near_ref[pl.ds(512, 64), :], *got, by2)
+    other = threes(both_ref[pl.ds(64, 64), :], *got, by2)
     fours = pool(jnp.concatenate([three_ref[...], other], axis=0), 2, by2)
     fours_ref[...] = fours
     fives_ref[...] = pool(fours, 2, by2[:64, :128])
@@ -305,32 +304,32 @@
     keys = pltpu.with_memory_space_constraint(keys, pltpu.HBM)
     values = pltpu.with_memory_space_constraint(values, pltpu.HBM)
     near, far, one, two = first_pools(core, keys, values)
+    near_got = swap(near, other_core)
     one_got = swap(one, along_y(1, 1))
-    near_got = swap(near, other_core)
     (both,) = small_call(both_kernel, (128,), two, near_got)
     twos_got = swap(both, along_y(2, 3))
     plan = ((0, 1, 0, TOK, 0, False),)
     state = attend(bias, queries, [keys, values], plan, (), False, fetched=True)
     plan = ((0, 0, 0, 512, WIDTH, False),)
     state = attend(bias, queries, [near_got], plan, state, False)
+    far_got = swap(far, beside)
 
     planes, three = small_call(plane_kernel, (256, 128), two, one_got, twos_got)
     planes_got = swap(planes, other_core)
     three_got = swap(three, along_z(1, 1))
-    fours, fives = small_call(wide_kernel, (128, 64), three, planes_got, near_got)
+    fours, fives = small_call(wide_kernel, (128, 64), three, planes_got, both)
     fours_got = swap(fours, along_z(2, 3))
     fives_c = swap(fives, along_z(5, 4))
     fives_d = swap(fives, along_z(6, 7))
-    far_got = swap(far, beside)
     plan = ((0, 0, 0, 256, WIDTH, False), (1, 1, 0, 256, WIDTH, False))
-    state = attend(bias, queries, [planes, planes_got], plan, state, False)
+    plan += ((2, 2, 0, 256, WIDTH, True),)
+    state = attend(bias, queries, [planes, planes_got, far_got], plan, state, False)
 
     upper = jnp.concatenate([three_got, fours_got, fives_c, fives_d], axis=0)
     upper_got = swap(upper, other_core)
     plan = ((0, 0, 0, 384, WIDTH, False),)
     state = attend(bias, queries, [upper], plan, state, False)
-    plan += ((1, 1, 0, 256, WIDTH, True),)
-    return attend(bias, queries, [upper_got, far_got], plan, state, True)
+    return attend(bias, queries, [upper_got], plan, state, True)
 
 
 def solution(mesh):

time: 111 us -> 112 us (level)
  transfers between devices with their start and end apart: 10 -> 10, of which waited for: 4 -> 3; matrix products, arithmetic and copies ran while one was open for 0% -> 0% of each run, Pallas kernels for 31% -> 33%
where the time goes in v7:
time: 112 us
  Pallas kernels  43.9 us (39%)
  starting transfers between devices  41.8 us (37%)
  waiting for transfers between devices  25.5 us (23%)
    ppermute x10, starting transfers between devices, swap(): return lax.ppermute(value, 'ctx', pairs)  41.8 us
    pallas_call x5, Pallas kernels, attend(): pl.pallas_call(functools.partial(attend_kernel, plan, bool(state), final,...  39.8 us
    ppermute x10, waiting for transfers between devices, swap(): return lax.ppermute(value, 'ctx', pairs)  25.5 us
    pallas_call x1, Pallas kernels, first_pools(): pl.pallas_call(first_kernel, in_specs=[pl.BlockSpec(memory_space=pltpu.SM...  3 us
  transfers between devices with their start and end apart: 10, of which 3 were waited for; matrix products, arithmetic and copies ran while one was open for 0% of the time, Pallas kernels for 33%

profile of v7, /device:TPU:39, one launch (start us, length us, event | category | flops | bytes accessed | tf_op | source)
XLA Modules:
  0.0 111.5 jit_solution(3599788578064089658)
XLA Ops:
  0.0 3.0 %first_pools.1 = (bf16[576,1024]{1,0:T(8,128)(2,1)S(1)}, bf16[256,1024]{1,0:T(8,128)(2,1)}, bf16[128,1024]{1,0:T(8,128)(2,1)S(1)}, bf16[64,1024]{1,0:T(8,128)(2,1)S(1)}) custom-call(s32[1]{0:T(128)} %bitcast.1.core_ref, bf16[1024,512]{1,0:T(8,128)(2,1)} %refs_2_.1, bf16[1024,512]{1,0:T(8,128)(2,1)} %refs_3_.1), custom_call_target="tpu_custom_call" | custom-call | flops 100000000 | bytes 4194304 | tf_op jit(solution)/shard_map/first_pools/pallas_call | solution.py:103
  3.0 2.6 %collective-permute-start.1 = (bf16[576,1024]{1,0:T(8,128)(2,1)S(1)}, bf16[576,1024]{1,0:T(8,128)(2,1)S(1)}, u32[]{:S(2)}, u32[]{:S(2)}) collective-permute-start(bf16[576,1024]{1,0:T(8,128)(2,1)S(1)} %get-tuple-element.27), channel_id=1, source_target_pairs={{0,8},{8,0},{16,24},{24,16},{32,40},{40,32},{48,56},{56,48},{64,72... | collective-permute-start | bytes 3538952 | tf_op jit(solution)/shard_map/ppermute | solution.py:33
  5.6 2.4 %collective-permute-start = (bf16[128,1024]{1,0:T(8,128)(2,1)S(1)}, bf16[128,1024]{1,0:T(8,128)(2,1)S(1)}, u32[]{:S(2)}, u32[]{:S(2)}) collective-permute-start(bf16[128,1024]{1,0:T(8,128)(2,1)S(1)} %get-tuple-element.26), channel_id=1, source_target_pairs={{0,16},{8,24},{16,0},{24,8},{32,48},{40,56},{48,32},{56,40},{64,80... | collective-permute-start | bytes 786440 | tf_op jit(solution)/shard_map/ppermute | solution.py:33
  8.0 0.0 collective-permute-done.1.near_ref.refs_2_
  8.1 0.0 copy-start
  8.1 2.1 %collective-permute-start.2 = (bf16[128,1024]{1,0:T(8,128)(2,1)S(1)}, bf16[128,1024]{1,0:T(8,128)(2,1)S(1)}, u32[]{:S(2)}, u32[]{:S(2)}) collective-permute-start(bf16[128,1024]{1,0:T(8,128)(2,1)S(1)} %shard_map.37.both_ref), channel_id=1, source_target_pairs={{0,32},{8,56},{16,48},{24,40},{32,0},{40,24},{48,16},{56,8},{64,96... | collective-permute-start | bytes 786440 | tf_op jit(solution)/shard_map/ppermute | solution.py:33
  10.2 16.3 %collective-permute-done.one_ref = bf16[128,1024]{1,0:T(8,128)(2,1)S(1)} collective-permute-done((bf16[128,1024]{1,0:T(8,128)(2,1)S(1)}, bf16[128,1024]{1,0:T(8,128)(2,1)S(1)}, u32[]{:S(2)}, u32[]{:S(2)}) %collective-permute-start) | collective-permute-done | bytes 262176 | tf_op jit(solution)/shard_map/ppermute | solution.py:33
  26.4 0.5 collective-permute-done.2.twos_ref
  26.9 0.4 shard_map.38
  27.3 0.0 copy-start.1
  27.3 2.1 %collective-permute-start.4 = (bf16[256,1024]{1,0:T(8,128)(2,1)S(1)}, bf16[256,1024]{1,0:T(8,128)(2,1)S(1)}, u32[]{:S(2)}, u32[]{:S(2)}) collective-permute-start(bf16[256,1024]{1,0:T(8,128)(2,1)S(1)} %get-tuple-element.29.refs_2_), channel_id=1, source_target_pairs={{0,8},{8,0},{16,24},{24,16},{32,40},{40,32},{48,56},{56,48},{64,72... | collective-permute-start | bytes 1572872 | tf_op jit(solution)/shard_map/ppermute | solution.py:33
  29.4 4.0 %collective-permute-start.3 = (bf16[128,1024]{1,0:T(8,128)(2,1)S(1)}, bf16[128,1024]{1,0:T(8,128)(2,1)S(1)}, u32[]{:S(2)}, u32[]{:S(2)}) collective-permute-start(bf16[128,1024]{1,0:T(8,128)(2,1)S(1)} %get-tuple-element.28.three_ref), channel_id=1, source_target_pairs={{0,64},{8,72},{16,80},{24,88},{32,96},{40,104},{48,112},{56,120},{... | collective-permute-start | bytes 786440 | tf_op jit(solution)/shard_map/ppermute | solution.py:33
  33.5 0.0 collective-permute-done.4.got_ref.refs_3_
  33.5 0.7 shard_map.39
  34.2 5.6 %collective-permute-start.5 = (bf16[128,1024]{1,0:T(8,128)(2,1)S(1)}, bf16[128,1024]{1,0:T(8,128)(2,1)S(1)}, u32[]{:S(2)}, u32[]{:S(2)}) collective-permute-start(bf16[128,1024]{1,0:T(8,128)(2,1)S(1)} %get-tuple-element.30), channel_id=1, source_target_pairs={{0,128},{8,200},{16,144},{24,216},{32,160},{40,232},{48,176},{56,2... | collective-permute-start | bytes 786440 | tf_op jit(solution)/shard_map/ppermute | solution.py:33
  39.8 8.1 %collective-permute-start.6 = (bf16[64,1024]{1,0:T(8,128)(2,1)S(1)}, bf16[64,1024]{1,0:T(8,128)(2,1)S(1)}, u32[]{:S(2)}, u32[]{:S(2)}) collective-permute-start(bf16[64,1024]{1,0:T(8,128)(2,1)S(1)} %get-tuple-element.31), channel_id=1, source_target_pairs={{0,320},{8,264},{16,336},{24,280},{32,352},{40,296},{48,368},{56,3... | collective-permute-start | bytes 393224 | tf_op jit(solution)/shard_map/ppermute | solution.py:33
  47.9 0.0 copy-done.1
  47.9 0.0 collective-permute-done.3
  48.0 1.9 %collective-permute-start.7 = (bf16[64,1024]{1,0:T(8,128)(2,1)S(1)}, bf16[64,1024]{1,0:T(8,128)(2,1)S(1)}, u32[]{:S(2)}, u32[]{:S(2)}) collective-permute-start(bf16[64,1024]{1,0:T(8,128)(2,1)S(1)} %get-tuple-element.31), channel_id=1, source_target_pairs={{0,384},{8,456},{16,400},{24,472},{32,416},{40,488},{48,432},{56,5... | collective-permute-start | bytes 393224 | tf_op jit(solution)/shard_map/ppermute | solution.py:33
  49.9 0.0 collective-permute-done.5
  49.9 8.7 %collective-permute-done.6 = bf16[64,1024]{1,0:T(8,128)(2,1)S(1)} collective-permute-done((bf16[64,1024]{1,0:T(8,128)(2,1)S(1)}, bf16[64,1024]{1,0:T(8,128)(2,1)S(1)}, u32[]{:S(2)}, u32[]{:S(2)}) %collective-permute-start.6) | collective-permute-done | bytes 131104 | tf_op jit(solution)/shard_map/ppermute | solution.py:33
  58.7 0.0 collective-permute-done.7
  58.7 6.8 %collective-permute-start.8 = (bf16[384,1024]{1,0:T(8,128)(2,1)S(1)}, bf16[384,1024]{1,0:T(8,128)(2,1)}, u32[]{:S(2)}, u32[]{:S(2)}) collective-permute-start(bf16[384,1024]{1,0:T(8,128)(2,1)S(1)} %constant_dynamic-update-slice_fusion.refs_2_), channel_id=1, source_target_pairs={{0,8},{8,0},{16,24},{24,16},{32,40},{40,32},{48,56},{56,48},{64,72... | collective-permute-start | bytes 2359304 | tf_op jit(solution)/shard_map/ppermute | solution.py:33
  65.5 6.1 %collective-permute-start.9 = (bf16[256,1024]{1,0:T(8,128)(2,1)}, bf16[256,1024]{1,0:T(8,128)(2,1)}, u32[]{:S(2)}, u32[]{:S(2)}) collective-permute-start(bf16[256,1024]{1,0:T(8,128)(2,1)} %get-tuple-element.32), channel_id=1, source_target_pairs={{8,16},{16,8},{24,32},{32,24},{40,48},{48,40},{56,64},{64,56},{72,... | collective-permute-start | bytes 1572872 | tf_op jit(solution)/shard_map/ppermute | solution.py:33
  71.6 0.0 copy-done
  71.6 25.6 %shard_map.40 = (f32[4,128,1024]{2,1,0:T(8,128)S(1)}, f32[4,1,1024]{2,1,0:T(1,128)S(1)}, f32[4,1,1024]{2,1,0:T(1,128)S(1)}) custom-call(f32[1]{0:T(128)} %bitcast.refs_0_, bf16[1024,512]{1,0:T(8,128)(2,1)S(1)} %copy-done, bf16[1024,512]{1,0:T(8,128)(2,1)} %refs_2_.1, bf16[1024,512]{1,0:T(8,128)(2,1)} %refs_3_.1), custom_call_target="tpu_custom_call" | custom-call | flops 2147483648 | bytes 5242880 | tf_op jit(solution)/shard_map/pallas_call | solution.py:283
  97.3 0.0 copy-start.2
  97.3 2.5 %shard_map.41 = (f32[4,128,1024]{2,1,0:T(8,128)S(1)}, f32[4,1,1024]{2,1,0:T(1,128)S(1)}, f32[4,1,1024]{2,1,0:T(1,128)S(1)}) custom-call(f32[1]{0:T(128)} %bitcast.refs_0_, bf16[1024,512]{1,0:T(8,128)(2,1)S(1)} %copy-done, bf16[576,1024]{1,0:T(8,128)(2,1)S(1)} %collective-permute-done.1.near_ref.refs_2_, f32[4,128,1024]{2,1,0:T(8,128)S(1)} %get-tuple-element.33.refs_3_, ...), custom_call_target="tpu_custom_call" | custom-call | flops 1073741824 | bytes 4194304 | tf_op jit(solution)/shard_map/pallas_call | solution.py:283
  99.8 0.0 collective-permute-done.9.refs_4_
  99.8 0.0 copy-done.2
  99.8 5.7 %shard_map.42 = (f32[4,128,1024]{2,1,0:T(8,128)S(1)}, f32[4,1,1024]{2,1,0:T(1,128)S(1)}, f32[4,1,1024]{2,1,0:T(1,128)S(1)}) custom-call(f32[1]{0:T(128)} %bitcast.refs_0_, bf16[1024,512]{1,0:T(8,128)(2,1)S(1)} %copy-done, bf16[256,1024]{1,0:T(8,128)(2,1)S(1)} %copy-done.2, bf16[256,1024]{1,0:T(8,128)(2,1)S(1)} %collective-permute-done.4.got_ref.refs_3_, ...), custom_call_target="tpu_custom_call" | custom-call | flops 1610612736 | bytes 4718592 | tf_op jit(solution)/shard_map/pallas_call | solution.py:283
  105.6 1.9 %shard_map.43 = (f32[4,128,1024]{2,1,0:T(8,128)S(1)}, f32[4,1,1024]{2,1,0:T(1,128)S(1)}, f32[4,1,1024]{2,1,0:T(1,128)S(1)}) custom-call(f32[1]{0:T(128)} %bitcast.refs_0_, bf16[1024,512]{1,0:T(8,128)(2,1)S(1)} %copy-done, bf16[384,1024]{1,0:T(8,128)(2,1)S(1)} %constant_dynamic-update-slice_fusion.refs_2_, f32[4,128,1024]{2,1,0:T(8,128)S(1)} %get-tuple-element.39.refs_3_, ...), custom_call_target="tpu_custom_call" | custom-call | flops 805306368 | bytes 3932160 | tf_op jit(solution)/shard_map/pallas_call | solution.py:283
  107.5 0.0 collective-permute-done.8.refs_2_
  107.5 4.1 %shard_map.44 = bf16[1024,512]{1,0:T(8,128)(2,1)} custom-call(f32[1]{0:T(128)} %bitcast.refs_0_, bf16[1024,512]{1,0:T(8,128)(2,1)S(1)} %copy-done, bf16[384,1024]{1,0:T(8,128)(2,1)} %collective-permute-done.8.refs_2_, f32[4,128,1024]{2,1,0:T(8,128)S(1)} %get-tuple-element.42.refs_3_, f32[4,1,1024]{2,1,0:T(1,128)S(1)} %get-tuple-element.43.refs_4_, ...), custom_call_target="tpu_custom_call" | custom-call | flops 805306368 | bytes 3932160 | tf_op jit(solution)/shard_map/pallas_call | solution.py:283
  (5 shorter events, 0.1 us)
Async XLA Ops:
  3.0 5.0 %collective-permute-start.1 = (bf16[576,1024]{1,0:T(8,128)(2,1)S(1)}, bf16[576,1024]{1,0:T(8,128)(2,1)S(1)}, u32[]{:S(2)}, u32[]{:S(2)}) collective-permute-start(bf16[576,1024]{1,0:T(8,128)(2,1)S(1)} %get-tuple-element.27), channel_id=1, source_target_pairs={{0,8},{8,0},{16,24},{24,16},{32,40},{40,32},{48,56},{56,48},{64,72... | collective-permute-start | bytes 3538952 | tf_op jit(solution)/shard_map/ppermute | solution.py:33
  5.6 20.8 %collective-permute-start = (bf16[128,1024]{1,0:T(8,128)(2,1)S(1)}, bf16[128,1024]{1,0:T(8,128)(2,1)S(1)}, u32[]{:S(2)}, u32[]{:S(2)}) collective-permute-start(bf16[128,1024]{1,0:T(8,128)(2,1)S(1)} %get-tuple-element.26), channel_id=1, source_target_pairs={{0,16},{8,24},{16,0},{24,8},{32,48},{40,56},{48,32},{56,40},{64,80... | collective-permute-start | bytes 786440 | tf_op jit(solution)/shard_map/ppermute | solution.py:33
  8.1 63.6 %copy-start = (bf16[1024,512]{1,0:T(8,128)(2,1)S(1)}, bf16[1024,512]{1,0:T(8,128)(2,1)}, u32[]{:S(2)}) copy-start(bf16[1024,512]{1,0:T(8,128)(2,1)} %refs_1_.9) | copy-start | bytes 3145732
  8.1 18.8 %collective-permute-start.2 = (bf16[128,1024]{1,0:T(8,128)(2,1)S(1)}, bf16[128,1024]{1,0:T(8,128)(2,1)S(1)}, u32[]{:S(2)}, u32[]{:S(2)}) collective-permute-start(bf16[128,1024]{1,0:T(8,128)(2,1)S(1)} %shard_map.37.both_ref), channel_id=1, source_target_pairs={{0,32},{8,56},{16,48},{24,40},{32,0},{40,24},{48,16},{56,8},{64,96... | collective-permute-start | bytes 786440 | tf_op jit(solution)/shard_map/ppermute | solution.py:33
  27.3 20.6 %copy-start.1 = (bf16[256,1024]{1,0:T(8,128)(2,1)}, bf16[256,1024]{1,0:T(8,128)(2,1)S(1)}, u32[]{:S(2)}) copy-start(bf16[256,1024]{1,0:T(8,128)(2,1)S(1)} %get-tuple-element.29.refs_2_) | copy-start | bytes 1572868
  27.3 6.2 %collective-permute-start.4 = (bf16[256,1024]{1,0:T(8,128)(2,1)S(1)}, bf16[256,1024]{1,0:T(8,128)(2,1)S(1)}, u32[]{:S(2)}, u32[]{:S(2)}) collective-permute-start(bf16[256,1024]{1,0:T(8,128)(2,1)S(1)} %get-tuple-element.29.refs_2_), channel_id=1, source_target_pairs={{0,8},{8,0},{16,24},{24,16},{32,40},{40,32},{48,56},{56,48},{64,72... | collective-permute-start | bytes 1572872 | tf_op jit(solution)/shard_map/ppermute | solution.py:33
  29.4 18.5 %collective-permute-start.3 = (bf16[128,1024]{1,0:T(8,128)(2,1)S(1)}, bf16[128,1024]{1,0:T(8,128)(2,1)S(1)}, u32[]{:S(2)}, u32[]{:S(2)}) collective-permute-start(bf16[128,1024]{1,0:T(8,128)(2,1)S(1)} %get-tuple-element.28.three_ref), channel_id=1, source_target_pairs={{0,64},{8,72},{16,80},{24,88},{32,96},{40,104},{48,112},{56,120},{... | collective-permute-start | bytes 786440 | tf_op jit(solution)/shard_map/ppermute | solution.py:33
  34.2 15.7 %collective-permute-start.5 = (bf16[128,1024]{1,0:T(8,128)(2,1)S(1)}, bf16[128,1024]{1,0:T(8,128)(2,1)S(1)}, u32[]{:S(2)}, u32[]{:S(2)}) collective-permute-start(bf16[128,1024]{1,0:T(8,128)(2,1)S(1)} %get-tuple-element.30), channel_id=1, source_target_pairs={{0,128},{8,200},{16,144},{24,216},{32,160},{40,232},{48,176},{56,2... | collective-permute-start | bytes 786440 | tf_op jit(solution)/shard_map/ppermute | solution.py:33
  39.8 18.9 %collective-permute-start.6 = (bf16[64,1024]{1,0:T(8,128)(2,1)S(1)}, bf16[64,1024]{1,0:T(8,128)(2,1)S(1)}, u32[]{:S(2)}, u32[]{:S(2)}) collective-permute-start(bf16[64,1024]{1,0:T(8,128)(2,1)S(1)} %get-tuple-element.31), channel_id=1, source_target_pairs={{0,320},{8,264},{16,336},{24,280},{32,352},{40,296},{48,368},{56,3... | collective-permute-start | bytes 393224 | tf_op jit(solution)/shard_map/ppermute | solution.py:33
  48.0 10.7 %collective-permute-start.7 = (bf16[64,1024]{1,0:T(8,128)(2,1)S(1)}, bf16[64,1024]{1,0:T(8,128)(2,1)S(1)}, u32[]{:S(2)}, u32[]{:S(2)}) collective-permute-start(bf16[64,1024]{1,0:T(8,128)(2,1)S(1)} %get-tuple-element.31), channel_id=1, source_target_pairs={{0,384},{8,456},{16,400},{24,472},{32,416},{40,488},{48,432},{56,5... | collective-permute-start | bytes 393224 | tf_op jit(solution)/shard_map/ppermute | solution.py:33
  58.7 48.7 %collective-permute-start.8 = (bf16[384,1024]{1,0:T(8,128)(2,1)S(1)}, bf16[384,1024]{1,0:T(8,128)(2,1)}, u32[]{:S(2)}, u32[]{:S(2)}) collective-permute-start(bf16[384,1024]{1,0:T(8,128)(2,1)S(1)} %constant_dynamic-update-slice_fusion.refs_2_), channel_id=1, source_target_pairs={{0,8},{8,0},{16,24},{24,16},{32,40},{40,32},{48,56},{56,48},{64,72... | collective-permute-start | bytes 2359304 | tf_op jit(solution)/shard_map/ppermute | solution.py:33
  65.5 34.3 %collective-permute-start.9 = (bf16[256,1024]{1,0:T(8,128)(2,1)}, bf16[256,1024]{1,0:T(8,128)(2,1)}, u32[]{:S(2)}, u32[]{:S(2)}) collective-permute-start(bf16[256,1024]{1,0:T(8,128)(2,1)} %get-tuple-element.32), channel_id=1, source_target_pairs={{8,16},{16,8},{24,32},{32,24},{40,48},{48,40},{56,64},{64,56},{72,... | collective-permute-start | bytes 1572872 | tf_op jit(solution)/shard_map/ppermute | solution.py:33
  97.3 2.6 %copy-start.2 = (bf16[256,1024]{1,0:T(8,128)(2,1)S(1)}, bf16[256,1024]{1,0:T(8,128)(2,1)}, u32[]{:S(2)}) copy-start(bf16[256,1024]{1,0:T(8,128)(2,1)} %copy-done.1) | copy-start | bytes 1572868

commit v8 on v7

--- a/solution.py
+++ b/solution.py
@@ -89,16 +89,14 @@
     far.start()
     one = pool(near_ref[pl.ds(0, POOL), :], 2, by2)
     one_ref[...] = one
-    two = pool(one, 2, by2[: POOL // 4, : POOL // 2])
-    two_ref[...] = two
-    near_ref[pl.ds(POOL + EDGE, POOL // 4), :] = two
+    two_ref[...] = pool(one, 2, by2[: POOL // 4, : POOL // 2])
     last = pl.multiple_of((1 - core) * (TOK - EDGE), EDGE)
     near_ref[pl.ds(POOL, EDGE), :] = buf[pl.ds(last, EDGE), :]
     far.wait()
 
 
 def first_pools(core, keys, values):
-    counts = (POOL + EDGE + POOL // 4, EDGE, POOL // 2, POOL // 4)
+    counts = (POOL + EDGE, EDGE, POOL // 2, POOL // 4)
     hbm, vmem = (pl.BlockSpec(memory_space=m) for m in (pltpu.HBM, pltpu.VMEM))
     return pl.pallas_call(
         first_kernel,
@@ -132,7 +130,9 @@
 
 def both_kernel(two_ref, near_ref, both_ref):
     both_ref[pl.ds(0, 64), :] = two_ref[...]
-    both_ref[pl.ds(64, 64), :] = near_ref[pl.ds(512, 64), :]
+    by2 = pooling_matrix(POOL, 2)
+    one = pool(near_ref[pl.ds(0, POOL), :], 2, by2)
+    both_ref[pl.ds(64, 64), :] = pool(one, 2, by2[:64, :128])
 
 
 def threes(two, one_got, twos_got, by2):

time: 112 us -> 112 us (level)
  transfers between devices with their start and end apart: 10 -> 10, of which waited for: 3 -> 4; matrix products, arithmetic and copies ran while one was open for 0% -> 0% of each run, Pallas kernels for 33% -> 33%
where the time goes in v8:
time: 112 us
  Pallas kernels  44.5 us (40%)
  starting transfers between devices  41 us (37%)
  waiting for transfers between devices  26.2 us (23%)
    ppermute x10, starting transfers between devices, swap(): return lax.ppermute(value, 'ctx', pairs)  41 us
    pallas_call x5, Pallas kernels, attend(): pl.pallas_call(functools.partial(attend_kernel, plan, bool(state), final,...  39.8 us
    ppermute x10, waiting for transfers between devices, swap(): return lax.ppermute(value, 'ctx', pairs)  26.2 us
    pallas_call x1, Pallas kernels, first_pools(): pl.pallas_call(first_kernel, in_specs=[pl.BlockSpec(memory_space=pltpu.SM...  3.22 us
  transfers between devices with their start and end apart: 10, of which 4 were waited for; matrix products, arithmetic and copies ran while one was open for 0% of the time, Pallas kernels for 33%

profile of v8, /device:TPU:39, one launch (start us, length us, event | category | flops | bytes accessed | tf_op | source)
XLA Modules:
  0.0 112.0 jit_solution(31215119238914334)
XLA Ops:
  0.0 3.2 %first_pools.1 = (bf16[512,1024]{1,0:T(8,128)(2,1)S(1)}, bf16[256,1024]{1,0:T(8,128)(2,1)}, bf16[128,1024]{1,0:T(8,128)(2,1)S(1)}, bf16[64,1024]{1,0:T(8,128)(2,1)S(1)}) custom-call(s32[1]{0:T(128)} %bitcast.1.core_ref, bf16[1024,512]{1,0:T(8,128)(2,1)} %refs_2_.1, bf16[1024,512]{1,0:T(8,128)(2,1)} %refs_3_.1), custom_call_target="tpu_custom_call" | custom-call | flops 100000000 | bytes 4194304 | tf_op jit(solution)/shard_map/first_pools/pallas_call | solution.py:101
  3.2 2.6 %collective-permute-start.1 = (bf16[512,1024]{1,0:T(8,128)(2,1)S(1)}, bf16[512,1024]{1,0:T(8,128)(2,1)S(1)}, u32[]{:S(2)}, u32[]{:S(2)}) collective-permute-start(bf16[512,1024]{1,0:T(8,128)(2,1)S(1)} %get-tuple-element.27), channel_id=1, source_target_pairs={{0,8},{8,0},{16,24},{24,16},{32,40},{40,32},{48,56},{56,48},{64,72... | collective-permute-start | bytes 3145736 | tf_op jit(solution)/shard_map/ppermute | solution.py:33
  5.8 2.4 %collective-permute-start = (bf16[128,1024]{1,0:T(8,128)(2,1)S(1)}, bf16[128,1024]{1,0:T(8,128)(2,1)S(1)}, u32[]{:S(2)}, u32[]{:S(2)}) collective-permute-start(bf16[128,1024]{1,0:T(8,128)(2,1)S(1)} %get-tuple-element.26), channel_id=1, source_target_pairs={{0,16},{8,24},{16,0},{24,8},{32,48},{40,56},{48,32},{56,40},{64,80... | collective-permute-start | bytes 786440 | tf_op jit(solution)/shard_map/ppermute | solution.py:33
  8.2 0.0 collective-permute-done.1.near_ref.refs_2_
  8.3 0.0 copy-start
  8.3 0.4 shard_map.37.both_ref
  8.7 1.9 %collective-permute-start.2 = (bf16[128,1024]{1,0:T(8,128)(2,1)S(1)}, bf16[128,1024]{1,0:T(8,128)(2,1)S(1)}, u32[]{:S(2)}, u32[]{:S(2)}) collective-permute-start(bf16[128,1024]{1,0:T(8,128)(2,1)S(1)} %shard_map.37.both_ref), channel_id=1, source_target_pairs={{0,32},{8,56},{16,48},{24,40},{32,0},{40,24},{48,16},{56,8},{64,96... | collective-permute-start | bytes 786440 | tf_op jit(solution)/shard_map/ppermute | solution.py:33
  10.6 15.8 %collective-permute-done.one_ref = bf16[128,1024]{1,0:T(8,128)(2,1)S(1)} collective-permute-done((bf16[128,1024]{1,0:T(8,128)(2,1)S(1)}, bf16[128,1024]{1,0:T(8,128)(2,1)S(1)}, u32[]{:S(2)}, u32[]{:S(2)}) %collective-permute-start) | collective-permute-done | bytes 262176 | tf_op jit(solution)/shard_map/ppermute | solution.py:33
  26.4 1.2 %collective-permute-done.2.twos_ref = bf16[128,1024]{1,0:T(8,128)(2,1)S(1)} collective-permute-done((bf16[128,1024]{1,0:T(8,128)(2,1)S(1)}, bf16[128,1024]{1,0:T(8,128)(2,1)S(1)}, u32[]{:S(2)}, u32[]{:S(2)}) %collective-permute-start.2) | collective-permute-done | bytes 262176 | tf_op jit(solution)/shard_map/ppermute | solution.py:33
  27.6 0.4 shard_map.38
  27.9 0.0 copy-start.1
  28.0 1.9 %collective-permute-start.4 = (bf16[256,1024]{1,0:T(8,128)(2,1)S(1)}, bf16[256,1024]{1,0:T(8,128)(2,1)S(1)}, u32[]{:S(2)}, u32[]{:S(2)}) collective-permute-start(bf16[256,1024]{1,0:T(8,128)(2,1)S(1)} %get-tuple-element.29.refs_2_), channel_id=1, source_target_pairs={{0,8},{8,0},{16,24},{24,16},{32,40},{40,32},{48,56},{56,48},{64,72... | collective-permute-start | bytes 1572872 | tf_op jit(solution)/shard_map/ppermute | solution.py:33
  29.9 4.0 %collective-permute-start.3 = (bf16[128,1024]{1,0:T(8,128)(2,1)S(1)}, bf16[128,1024]{1,0:T(8,128)(2,1)S(1)}, u32[]{:S(2)}, u32[]{:S(2)}) collective-permute-start(bf16[128,1024]{1,0:T(8,128)(2,1)S(1)} %get-tuple-element.28.three_ref), channel_id=1, source_target_pairs={{0,64},{8,72},{16,80},{24,88},{32,96},{40,104},{48,112},{56,120},{... | collective-permute-start | bytes 786440 | tf_op jit(solution)/shard_map/ppermute | solution.py:33
  33.9 0.0 collective-permute-done.4.got_ref.refs_3_
  33.9 0.7 shard_map.39
  34.6 5.5 %collective-permute-start.5 = (bf16[128,1024]{1,0:T(8,128)(2,1)S(1)}, bf16[128,1024]{1,0:T(8,128)(2,1)S(1)}, u32[]{:S(2)}, u32[]{:S(2)}) collective-permute-start(bf16[128,1024]{1,0:T(8,128)(2,1)S(1)} %get-tuple-element.30), channel_id=1, source_target_pairs={{0,128},{8,200},{16,144},{24,216},{32,160},{40,232},{48,176},{56,2... | collective-permute-start | bytes 786440 | tf_op jit(solution)/shard_map/ppermute | solution.py:33
  40.2 8.2 %collective-permute-start.6 = (bf16[64,1024]{1,0:T(8,128)(2,1)S(1)}, bf16[64,1024]{1,0:T(8,128)(2,1)S(1)}, u32[]{:S(2)}, u32[]{:S(2)}) collective-permute-start(bf16[64,1024]{1,0:T(8,128)(2,1)S(1)} %get-tuple-element.31), channel_id=1, source_target_pairs={{0,320},{8,264},{16,336},{24,280},{32,352},{40,296},{48,368},{56,3... | collective-permute-start | bytes 393224 | tf_op jit(solution)/shard_map/ppermute | solution.py:33
  48.4 0.0 copy-done.1
  48.4 0.0 collective-permute-done.3
  48.4 1.9 %collective-permute-start.7 = (bf16[64,1024]{1,0:T(8,128)(2,1)S(1)}, bf16[64,1024]{1,0:T(8,128)(2,1)S(1)}, u32[]{:S(2)}, u32[]{:S(2)}) collective-permute-start(bf16[64,1024]{1,0:T(8,128)(2,1)S(1)} %get-tuple-element.31), channel_id=1, source_target_pairs={{0,384},{8,456},{16,400},{24,472},{32,416},{40,488},{48,432},{56,5... | collective-permute-start | bytes 393224 | tf_op jit(solution)/shard_map/ppermute | solution.py:33
  50.3 0.0 collective-permute-done.5
  50.4 8.8 %collective-permute-done.6 = bf16[64,1024]{1,0:T(8,128)(2,1)S(1)} collective-permute-done((bf16[64,1024]{1,0:T(8,128)(2,1)S(1)}, bf16[64,1024]{1,0:T(8,128)(2,1)S(1)}, u32[]{:S(2)}, u32[]{:S(2)}) %collective-permute-start.6) | collective-permute-done | bytes 131104 | tf_op jit(solution)/shard_map/ppermute | solution.py:33
  59.1 0.4 collective-permute-done.7
  59.6 6.4 %collective-permute-start.8 = (bf16[384,1024]{1,0:T(8,128)(2,1)S(1)}, bf16[384,1024]{1,0:T(8,128)(2,1)}, u32[]{:S(2)}, u32[]{:S(2)}) collective-permute-start(bf16[384,1024]{1,0:T(8,128)(2,1)S(1)} %constant_dynamic-update-slice_fusion.refs_2_), channel_id=1, source_target_pairs={{0,8},{8,0},{16,24},{24,16},{32,40},{40,32},{48,56},{56,48},{64,72... | collective-permute-start | bytes 2359304 | tf_op jit(solution)/shard_map/ppermute | solution.py:33
  66.0 6.1 %collective-permute-start.9 = (bf16[256,1024]{1,0:T(8,128)(2,1)}, bf16[256,1024]{1,0:T(8,128)(2,1)}, u32[]{:S(2)}, u32[]{:S(2)}) collective-permute-start(bf16[256,1024]{1,0:T(8,128)(2,1)} %get-tuple-element.32), channel_id=1, source_target_pairs={{8,16},{16,8},{24,32},{32,24},{40,48},{48,40},{56,64},{64,56},{72,... | collective-permute-start | bytes 1572872 | tf_op jit(solution)/shard_map/ppermute | solution.py:33
  72.1 0.0 copy-done
  72.1 25.6 %shard_map.40 = (f32[4,128,1024]{2,1,0:T(8,128)S(1)}, f32[4,1,1024]{2,1,0:T(1,128)S(1)}, f32[4,1,1024]{2,1,0:T(1,128)S(1)}) custom-call(f32[1]{0:T(128)} %bitcast.refs_0_, bf16[1024,512]{1,0:T(8,128)(2,1)S(1)} %copy-done, bf16[1024,512]{1,0:T(8,128)(2,1)} %refs_2_.1, bf16[1024,512]{1,0:T(8,128)(2,1)} %refs_3_.1), custom_call_target="tpu_custom_call" | custom-call | flops 2147483648 | bytes 5242880 | tf_op jit(solution)/shard_map/pallas_call | solution.py:283
  97.7 0.0 copy-start.2
  97.7 2.5 %shard_map.41 = (f32[4,128,1024]{2,1,0:T(8,128)S(1)}, f32[4,1,1024]{2,1,0:T(1,128)S(1)}, f32[4,1,1024]{2,1,0:T(1,128)S(1)}) custom-call(f32[1]{0:T(128)} %bitcast.refs_0_, bf16[1024,512]{1,0:T(8,128)(2,1)S(1)} %copy-done, bf16[512,1024]{1,0:T(8,128)(2,1)S(1)} %collective-permute-done.1.near_ref.refs_2_, f32[4,128,1024]{2,1,0:T(8,128)S(1)} %get-tuple-element.33.refs_3_, ...), custom_call_target="tpu_custom_call" | custom-call | flops 1073741824 | bytes 4194304 | tf_op jit(solution)/shard_map/pallas_call | solution.py:283
  100.3 0.0 collective-permute-done.9.refs_4_
  100.3 0.0 copy-done.2
  100.3 5.7 %shard_map.42 = (f32[4,128,1024]{2,1,0:T(8,128)S(1)}, f32[4,1,1024]{2,1,0:T(1,128)S(1)}, f32[4,1,1024]{2,1,0:T(1,128)S(1)}) custom-call(f32[1]{0:T(128)} %bitcast.refs_0_, bf16[1024,512]{1,0:T(8,128)(2,1)S(1)} %copy-done, bf16[256,1024]{1,0:T(8,128)(2,1)S(1)} %copy-done.2, bf16[256,1024]{1,0:T(8,128)(2,1)S(1)} %collective-permute-done.4.got_ref.refs_3_, ...), custom_call_target="tpu_custom_call" | custom-call | flops 1610612736 | bytes 4718592 | tf_op jit(solution)/shard_map/pallas_call | solution.py:283
  106.0 1.9 %shard_map.43 = (f32[4,128,1024]{2,1,0:T(8,128)S(1)}, f32[4,1,1024]{2,1,0:T(1,128)S(1)}, f32[4,1,1024]{2,1,0:T(1,128)S(1)}) custom-call(f32[1]{0:T(128)} %bitcast.refs_0_, bf16[1024,512]{1,0:T(8,128)(2,1)S(1)} %copy-done, bf16[384,1024]{1,0:T(8,128)(2,1)S(1)} %constant_dynamic-update-slice_fusion.refs_2_, f32[4,128,1024]{2,1,0:T(8,128)S(1)} %get-tuple-element.39.refs_3_, ...), custom_call_target="tpu_custom_call" | custom-call | flops 805306368 | bytes 3932160 | tf_op jit(solution)/shard_map/pallas_call | solution.py:283
  107.9 0.0 collective-permute-done.8.refs_2_
  107.9 4.1 %shard_map.44 = bf16[1024,512]{1,0:T(8,128)(2,1)} custom-call(f32[1]{0:T(128)} %bitcast.refs_0_, bf16[1024,512]{1,0:T(8,128)(2,1)S(1)} %copy-done, bf16[384,1024]{1,0:T(8,128)(2,1)} %collective-permute-done.8.refs_2_, f32[4,128,1024]{2,1,0:T(8,128)S(1)} %get-tuple-element.42.refs_3_, f32[4,1,1024]{2,1,0:T(1,128)S(1)} %get-tuple-element.43.refs_4_, ...), custom_call_target="tpu_custom_call" | custom-call | flops 805306368 | bytes 3932160 | tf_op jit(solution)/shard_map/pallas_call | solution.py:283
  (4 shorter events, 0.1 us)
Async XLA Ops:
  3.2 5.0 %collective-permute-start.1 = (bf16[512,1024]{1,0:T(8,128)(2,1)S(1)}, bf16[512,1024]{1,0:T(8,128)(2,1)S(1)}, u32[]{:S(2)}, u32[]{:S(2)}) collective-permute-start(bf16[512,1024]{1,0:T(8,128)(2,1)S(1)} %get-tuple-element.27), channel_id=1, source_target_pairs={{0,8},{8,0},{16,24},{24,16},{32,40},{40,32},{48,56},{56,48},{64,72... | collective-permute-start | bytes 3145736 | tf_op jit(solution)/shard_map/ppermute | solution.py:33
  5.8 20.6 %collective-permute-start = (bf16[128,1024]{1,0:T(8,128)(2,1)S(1)}, bf16[128,1024]{1,0:T(8,128)(2,1)S(1)}, u32[]{:S(2)}, u32[]{:S(2)}) collective-permute-start(bf16[128,1024]{1,0:T(8,128)(2,1)S(1)} %get-tuple-element.26), channel_id=1, source_target_pairs={{0,16},{8,24},{16,0},{24,8},{32,48},{40,56},{48,32},{56,40},{64,80... | collective-permute-start | bytes 786440 | tf_op jit(solution)/shard_map/ppermute | solution.py:33
  8.3 63.8 %copy-start = (bf16[1024,512]{1,0:T(8,128)(2,1)S(1)}, bf16[1024,512]{1,0:T(8,128)(2,1)}, u32[]{:S(2)}) copy-start(bf16[1024,512]{1,0:T(8,128)(2,1)} %refs_1_.9) | copy-start | bytes 3145732
  8.7 18.9 %collective-permute-start.2 = (bf16[128,1024]{1,0:T(8,128)(2,1)S(1)}, bf16[128,1024]{1,0:T(8,128)(2,1)S(1)}, u32[]{:S(2)}, u32[]{:S(2)}) collective-permute-start(bf16[128,1024]{1,0:T(8,128)(2,1)S(1)} %shard_map.37.both_ref), channel_id=1, source_target_pairs={{0,32},{8,56},{16,48},{24,40},{32,0},{40,24},{48,16},{56,8},{64,96... | collective-permute-start | bytes 786440 | tf_op jit(solution)/shard_map/ppermute | solution.py:33
  27.9 20.4 %copy-start.1 = (bf16[256,1024]{1,0:T(8,128)(2,1)}, bf16[256,1024]{1,0:T(8,128)(2,1)S(1)}, u32[]{:S(2)}) copy-start(bf16[256,1024]{1,0:T(8,128)(2,1)S(1)} %get-tuple-element.29.refs_2_) | copy-start | bytes 1572868
  28.0 5.9 %collective-permute-start.4 = (bf16[256,1024]{1,0:T(8,128)(2,1)S(1)}, bf16[256,1024]{1,0:T(8,128)(2,1)S(1)}, u32[]{:S(2)}, u32[]{:S(2)}) collective-permute-start(bf16[256,1024]{1,0:T(8,128)(2,1)S(1)} %get-tuple-element.29.refs_2_), channel_id=1, source_target_pairs={{0,8},{8,0},{16,24},{24,16},{32,40},{40,32},{48,56},{56,48},{64,72... | collective-permute-start | bytes 1572872 | tf_op jit(solution)/shard_map/ppermute | solution.py:33
  29.9 18.5 %collective-permute-start.3 = (bf16[128,1024]{1,0:T(8,128)(2,1)S(1)}, bf16[128,1024]{1,0:T(8,128)(2,1)S(1)}, u32[]{:S(2)}, u32[]{:S(2)}) collective-permute-start(bf16[128,1024]{1,0:T(8,128)(2,1)S(1)} %get-tuple-element.28.three_ref), channel_id=1, source_target_pairs={{0,64},{8,72},{16,80},{24,88},{32,96},{40,104},{48,112},{56,120},{... | collective-permute-start | bytes 786440 | tf_op jit(solution)/shard_map/ppermute | solution.py:33
  34.6 15.7 %collective-permute-start.5 = (bf16[128,1024]{1,0:T(8,128)(2,1)S(1)}, bf16[128,1024]{1,0:T(8,128)(2,1)S(1)}, u32[]{:S(2)}, u32[]{:S(2)}) collective-permute-start(bf16[128,1024]{1,0:T(8,128)(2,1)S(1)} %get-tuple-element.30), channel_id=1, source_target_pairs={{0,128},{8,200},{16,144},{24,216},{32,160},{40,232},{48,176},{56,2... | collective-permute-start | bytes 786440 | tf_op jit(solution)/shard_map/ppermute | solution.py:33
  40.2 19.0 %collective-permute-start.6 = (bf16[64,1024]{1,0:T(8,128)(2,1)S(1)}, bf16[64,1024]{1,0:T(8,128)(2,1)S(1)}, u32[]{:S(2)}, u32[]{:S(2)}) collective-permute-start(bf16[64,1024]{1,0:T(8,128)(2,1)S(1)} %get-tuple-element.31), channel_id=1, source_target_pairs={{0,320},{8,264},{16,336},{24,280},{32,352},{40,296},{48,368},{56,3... | collective-permute-start | bytes 393224 | tf_op jit(solution)/shard_map/ppermute | solution.py:33
  48.4 11.2 %collective-permute-start.7 = (bf16[64,1024]{1,0:T(8,128)(2,1)S(1)}, bf16[64,1024]{1,0:T(8,128)(2,1)S(1)}, u32[]{:S(2)}, u32[]{:S(2)}) collective-permute-start(bf16[64,1024]{1,0:T(8,128)(2,1)S(1)} %get-tuple-element.31), channel_id=1, source_target_pairs={{0,384},{8,456},{16,400},{24,472},{32,416},{40,488},{48,432},{56,5... | collective-permute-start | bytes 393224 | tf_op jit(solution)/shard_map/ppermute | solution.py:33
  59.6 48.3 %collective-permute-start.8 = (bf16[384,1024]{1,0:T(8,128)(2,1)S(1)}, bf16[384,1024]{1,0:T(8,128)(2,1)}, u32[]{:S(2)}, u32[]{:S(2)}) collective-permute-start(bf16[384,1024]{1,0:T(8,128)(2,1)S(1)} %constant_dynamic-update-slice_fusion.refs_2_), channel_id=1, source_target_pairs={{0,8},{8,0},{16,24},{24,16},{32,40},{40,32},{48,56},{56,48},{64,72... | collective-permute-start | bytes 2359304 | tf_op jit(solution)/shard_map/ppermute | solution.py:33
  66.0 34.3 %collective-permute-start.9 = (bf16[256,1024]{1,0:T(8,128)(2,1)}, bf16[256,1024]{1,0:T(8,128)(2,1)}, u32[]{:S(2)}, u32[]{:S(2)}) collective-permute-start(bf16[256,1024]{1,0:T(8,128)(2,1)} %get-tuple-element.32), channel_id=1, source_target_pairs={{8,16},{16,8},{24,32},{32,24},{40,48},{48,40},{56,64},{64,56},{72,... | collective-permute-start | bytes 1572872 | tf_op jit(solution)/shard_map/ppermute | solution.py:33
  97.7 2.6 %copy-start.2 = (bf16[256,1024]{1,0:T(8,128)(2,1)S(1)}, bf16[256,1024]{1,0:T(8,128)(2,1)}, u32[]{:S(2)}) copy-start(bf16[256,1024]{1,0:T(8,128)(2,1)} %copy-done.1) | copy-start | bytes 1572868

commit v9 on v8

--- a/solution.py
+++ b/solution.py
@@ -325,9 +325,14 @@
     plan += ((2, 2, 0, 256, WIDTH, True),)
     state = attend(bias, queries, [planes, planes_got, far_got], plan, state, False)
 
-    upper = jnp.concatenate([three_got, fours_got, fives_c, fives_d], axis=0)
+    plan = ((0, 0, 0, 256, WIDTH, False),)
+    middle = jnp.concatenate([three_got, fours_got], axis=0)
+    middle_got = swap(middle, other_core)
+    state = attend(bias, queries, [middle], plan, state, False)
+    state = attend(bias, queries, [middle_got], plan, state, False)
+    plan = ((0, 0, 0, 128, WIDTH, False),)
+    upper = jnp.concatenate([fives_c, fives_d], axis=0)
     upper_got = swap(upper, other_core)
-    plan = ((0, 0, 0, 384, WIDTH, False),)
     state = attend(bias, queries, [upper], plan, state, False)
     return attend(bias, queries, [upper_got], plan, state, True)
 

time: 112 us -> 104 us (0.929)
  the two profiles are of different devices: /device:TPU:39 before, /device:TPU:31 now
where the time goes in v9:
time: 104 us
  starting transfers between devices  62 us (60%)
  Pallas kernels  26.9 us (26%)
  waiting for transfers between devices  14.7 us (14%)
    ppermute x11, starting transfers between devices, swap(): return lax.ppermute(value, 'ctx', pairs)  62 us
    pallas_call x7, Pallas kernels, attend(): pl.pallas_call(functools.partial(attend_kernel, plan, bool(state), final,...  21.6 us
    ppermute x11, waiting for transfers between devices, swap(): return lax.ppermute(value, 'ctx', pairs)  14.7 us
    pallas_call x1, Pallas kernels, first_pools(): pl.pallas_call(first_kernel, in_specs=[pl.BlockSpec(memory_space=pltpu.SM...  3.21 us
  transfers between devices with their start and end apart: 11, of which 3 were waited for; matrix products, arithmetic and copies ran while one was open for 0% of the time, Pallas kernels for 20%

profile of v9, /device:TPU:31, one launch (start us, length us, event | category | flops | bytes accessed | tf_op | source)
XLA Modules:
  0.0 103.9 jit_solution(13261043734948071115)
XLA Ops:
  0.0 3.2 %first_pools.1 = (bf16[512,1024]{1,0:T(8,128)(2,1)S(1)}, bf16[256,1024]{1,0:T(8,128)(2,1)}, bf16[128,1024]{1,0:T(8,128)(2,1)S(1)}, bf16[64,1024]{1,0:T(8,128)(2,1)S(1)}) custom-call(s32[1]{0:T(128)} %bitcast.1.core_ref, bf16[1024,512]{1,0:T(8,128)(2,1)} %refs_2_.1, bf16[1024,512]{1,0:T(8,128)(2,1)} %refs_3_.1), custom_call_target="tpu_custom_call" | custom-call | flops 100000000 | bytes 4194304 | tf_op jit(solution)/shard_map/first_pools/pallas_call | solution.py:101
  3.2 0.0 copy-start
  3.2 2.7 %collective-permute-start.1 = (bf16[512,1024]{1,0:T(8,128)(2,1)S(1)}, bf16[512,1024]{1,0:T(8,128)(2,1)S(1)}, u32[]{:S(2)}, u32[]{:S(2)}) collective-permute-start(bf16[512,1024]{1,0:T(8,128)(2,1)S(1)} %get-tuple-element.33), channel_id=1, source_target_pairs={{0,8},{8,0},{16,24},{24,16},{32,40},{40,32},{48,56},{56,48},{64,72... | collective-permute-start | bytes 3145736 | tf_op jit(solution)/shard_map/ppermute | solution.py:33
  6.0 2.0 %collective-permute-start = (bf16[128,1024]{1,0:T(8,128)(2,1)S(1)}, bf16[128,1024]{1,0:T(8,128)(2,1)S(1)}, u32[]{:S(2)}, u32[]{:S(2)}) collective-permute-start(bf16[128,1024]{1,0:T(8,128)(2,1)S(1)} %get-tuple-element.32), channel_id=1, source_target_pairs={{0,16},{8,24},{16,0},{24,8},{32,48},{40,56},{48,32},{56,40},{64,80... | collective-permute-start | bytes 786440 | tf_op jit(solution)/shard_map/ppermute | solution.py:33
  7.9 0.3 collective-permute-done.1.near_ref.refs_2_
  8.2 0.4 shard_map.37.both_ref
  8.6 4.7 %collective-permute-start.2 = (bf16[128,1024]{1,0:T(8,128)(2,1)S(1)}, bf16[128,1024]{1,0:T(8,128)(2,1)S(1)}, u32[]{:S(2)}, u32[]{:S(2)}) collective-permute-start(bf16[128,1024]{1,0:T(8,128)(2,1)S(1)} %shard_map.37.both_ref), channel_id=1, source_target_pairs={{0,32},{8,56},{16,48},{24,40},{32,0},{40,24},{48,16},{56,8},{64,96... | collective-permute-start | bytes 786440 | tf_op jit(solution)/shard_map/ppermute | solution.py:33
  13.3 13.7 %collective-permute-done.one_ref = bf16[128,1024]{1,0:T(8,128)(2,1)S(1)} collective-permute-done((bf16[128,1024]{1,0:T(8,128)(2,1)S(1)}, bf16[128,1024]{1,0:T(8,128)(2,1)S(1)}, u32[]{:S(2)}, u32[]{:S(2)}) %collective-permute-start) | collective-permute-done | bytes 262176 | tf_op jit(solution)/shard_map/ppermute | solution.py:33
  27.0 0.0 collective-permute-done.2.twos_ref
  27.0 1.0 shard_map.38
  28.0 2.3 %collective-permute-start.3 = (bf16[256,1024]{1,0:T(8,128)(2,1)}, bf16[256,1024]{1,0:T(8,128)(2,1)S(1)}, u32[]{:S(2)}, u32[]{:S(2)}) collective-permute-start(bf16[256,1024]{1,0:T(8,128)(2,1)} %get-tuple-element.35.refs_2_), channel_id=1, source_target_pairs={{0,8},{8,0},{16,24},{24,16},{32,40},{40,32},{48,56},{56,48},{64,72... | collective-permute-start | bytes 1572872 | tf_op jit(solution)/shard_map/ppermute | solution.py:33
  30.4 4.0 %collective-permute-start.7 = (bf16[128,1024]{1,0:T(8,128)(2,1)S(1)}, bf16[128,1024]{1,0:T(8,128)(2,1)S(1)}, u32[]{:S(2)}, u32[]{:S(2)}) collective-permute-start(bf16[128,1024]{1,0:T(8,128)(2,1)S(1)} %get-tuple-element.34.three_ref), channel_id=1, source_target_pairs={{0,64},{8,72},{16,80},{24,88},{32,96},{40,104},{48,112},{56,120},{... | collective-permute-start | bytes 786440 | tf_op jit(solution)/shard_map/ppermute | solution.py:33
  34.4 7.6 %collective-permute-start.10 = (bf16[256,1024]{1,0:T(8,128)(2,1)}, bf16[256,1024]{1,0:T(8,128)(2,1)}, u32[]{:S(2)}, u32[]{:S(2)}) collective-permute-start(bf16[256,1024]{1,0:T(8,128)(2,1)} %get-tuple-element.38), channel_id=1, source_target_pairs={{8,16},{16,8},{24,32},{32,24},{40,48},{48,40},{56,64},{64,56},{72,... | collective-permute-start | bytes 1572872 | tf_op jit(solution)/shard_map/ppermute | solution.py:33
  42.0 0.0 collective-permute-done.3.got_ref.refs_3_
  42.1 0.7 shard_map.39
  42.8 5.3 %collective-permute-start.8 = (bf16[128,1024]{1,0:T(8,128)(2,1)S(1)}, bf16[128,1024]{1,0:T(8,128)(2,1)S(1)}, u32[]{:S(2)}, u32[]{:S(2)}) collective-permute-start(bf16[128,1024]{1,0:T(8,128)(2,1)S(1)} %get-tuple-element.37), channel_id=1, source_target_pairs={{0,128},{8,200},{16,144},{24,216},{32,160},{40,232},{48,176},{56,2... | collective-permute-start | bytes 786440 | tf_op jit(solution)/shard_map/ppermute | solution.py:33
  48.0 0.0 copy-done
  48.0 6.7 %shard_map.40 = (f32[4,128,1024]{2,1,0:T(8,128)S(1)}, f32[4,1,1024]{2,1,0:T(1,128)S(1)}, f32[4,1,1024]{2,1,0:T(1,128)S(1)}) custom-call(f32[1]{0:T(128)} %bitcast.refs_0_, bf16[1024,512]{1,0:T(8,128)(2,1)S(1)} %copy-done, bf16[1024,512]{1,0:T(8,128)(2,1)} %refs_2_.1, bf16[1024,512]{1,0:T(8,128)(2,1)} %refs_3_.1), custom_call_target="tpu_custom_call" | custom-call | flops 2147483648 | bytes 5242880 | tf_op jit(solution)/shard_map/pallas_call | solution.py:283
  54.7 0.0 collective-permute-done.7
  54.8 27.4 %collective-permute-start.4 = (bf16[64,1024]{1,0:T(8,128)(2,1)S(1)}, bf16[64,1024]{1,0:T(8,128)(2,1)S(1)}, u32[]{:S(2)}, u32[]{:S(2)}) collective-permute-start(bf16[64,1024]{1,0:T(8,128)(2,1)S(1)} %get-tuple-element.36), channel_id=1, source_target_pairs={{0,320},{8,264},{16,336},{24,280},{32,352},{40,296},{48,368},{56,3... | collective-permute-start | bytes 393224 | tf_op jit(solution)/shard_map/ppermute | solution.py:33
  82.2 1.9 %collective-permute-start.5 = (bf16[64,1024]{1,0:T(8,128)(2,1)S(1)}, bf16[64,1024]{1,0:T(8,128)(2,1)S(1)}, u32[]{:S(2)}, u32[]{:S(2)}) collective-permute-start(bf16[64,1024]{1,0:T(8,128)(2,1)S(1)} %get-tuple-element.36), channel_id=1, source_target_pairs={{0,384},{8,456},{16,400},{24,472},{32,416},{40,488},{48,432},{56,5... | collective-permute-start | bytes 393224 | tf_op jit(solution)/shard_map/ppermute | solution.py:33
  84.1 0.0 collective-permute-done.8
  84.2 1.9 %collective-permute-start.9 = (bf16[256,1024]{1,0:T(8,128)(2,1)S(1)}, bf16[256,1024]{1,0:T(8,128)(2,1)S(1)}, u32[]{:S(2)}, u32[]{:S(2)}) collective-permute-start(bf16[256,1024]{1,0:T(8,128)(2,1)S(1)} %constant_dynamic-update-slice_fusion.2.refs_2_), channel_id=1, source_target_pairs={{0,8},{8,0},{16,24},{24,16},{32,40},{40,32},{48,56},{56,48},{64,72... | collective-permute-start | bytes 1572872 | tf_op jit(solution)/shard_map/ppermute | solution.py:33
  86.1 2.4 %shard_map.41 = (f32[4,128,1024]{2,1,0:T(8,128)S(1)}, f32[4,1,1024]{2,1,0:T(1,128)S(1)}, f32[4,1,1024]{2,1,0:T(1,128)S(1)}) custom-call(f32[1]{0:T(128)} %bitcast.refs_0_, bf16[1024,512]{1,0:T(8,128)(2,1)S(1)} %copy-done, bf16[512,1024]{1,0:T(8,128)(2,1)S(1)} %collective-permute-done.1.near_ref.refs_2_, f32[4,128,1024]{2,1,0:T(8,128)S(1)} %get-tuple-element.39.refs_3_, ...), custom_call_target="tpu_custom_call" | custom-call | flops 1073741824 | bytes 4194304 | tf_op jit(solution)/shard_map/pallas_call | solution.py:283
  88.5 0.0 collective-permute-done.4
  88.5 0.6 collective-permute-done.5
  89.1 2.1 %collective-permute-start.6 = (bf16[128,1024]{1,0:T(8,128)(2,1)S(1)}, bf16[128,1024]{1,0:T(8,128)(2,1)S(1)}, u32[]{:S(2)}, u32[]{:S(2)}) collective-permute-start(bf16[128,1024]{1,0:T(8,128)(2,1)S(1)} %constant_dynamic-update-slice_fusion.refs_2_), channel_id=1, source_target_pairs={{0,8},{8,0},{16,24},{24,16},{32,40},{40,32},{48,56},{56,48},{64,72... | collective-permute-start | bytes 786440 | tf_op jit(solution)/shard_map/ppermute | solution.py:33
  91.2 0.0 collective-permute-done.10.refs_4_
  91.3 5.9 %shard_map.42 = (f32[4,128,1024]{2,1,0:T(8,128)S(1)}, f32[4,1,1024]{2,1,0:T(1,128)S(1)}, f32[4,1,1024]{2,1,0:T(1,128)S(1)}) custom-call(f32[1]{0:T(128)} %bitcast.refs_0_, bf16[1024,512]{1,0:T(8,128)(2,1)S(1)} %copy-done, bf16[256,1024]{1,0:T(8,128)(2,1)} %get-tuple-element.35.refs_2_, bf16[256,1024]{1,0:T(8,128)(2,1)S(1)} %collective-permute-done.3.got_ref.refs_3_, ...), custom_call_target="tpu_custom_call" | custom-call | flops 1610612736 | bytes 4718592 | tf_op jit(solution)/shard_map/pallas_call | solution.py:283
  97.1 1.6 %shard_map.43 = (f32[4,128,1024]{2,1,0:T(8,128)S(1)}, f32[4,1,1024]{2,1,0:T(1,128)S(1)}, f32[4,1,1024]{2,1,0:T(1,128)S(1)}) custom-call(f32[1]{0:T(128)} %bitcast.refs_0_, bf16[1024,512]{1,0:T(8,128)(2,1)S(1)} %copy-done, bf16[256,1024]{1,0:T(8,128)(2,1)S(1)} %constant_dynamic-update-slice_fusion.2.refs_2_, f32[4,128,1024]{2,1,0:T(8,128)S(1)} %get-tuple-element.45.refs_3_, ...), custom_call_target="tpu_custom_call" | custom-call | flops 536870912 | bytes 3670016 | tf_op jit(solution)/shard_map/pallas_call | solution.py:283
  98.7 0.0 collective-permute-done.9.refs_2_
  98.7 1.6 %shard_map.44 = (f32[4,128,1024]{2,1,0:T(8,128)S(1)}, f32[4,1,1024]{2,1,0:T(1,128)S(1)}, f32[4,1,1024]{2,1,0:T(1,128)S(1)}) custom-call(f32[1]{0:T(128)} %bitcast.refs_0_, bf16[1024,512]{1,0:T(8,128)(2,1)S(1)} %copy-done, bf16[256,1024]{1,0:T(8,128)(2,1)S(1)} %collective-permute-done.9.refs_2_, f32[4,128,1024]{2,1,0:T(8,128)S(1)} %get-tuple-element.48.refs_3_, ...), custom_call_target="tpu_custom_call" | custom-call | flops 536870912 | bytes 3670016 | tf_op jit(solution)/shard_map/pallas_call | solution.py:283
  100.4 1.2 %shard_map.45 = (f32[4,128,1024]{2,1,0:T(8,128)S(1)}, f32[4,1,1024]{2,1,0:T(1,128)S(1)}, f32[4,1,1024]{2,1,0:T(1,128)S(1)}) custom-call(f32[1]{0:T(128)} %bitcast.refs_0_, bf16[1024,512]{1,0:T(8,128)(2,1)S(1)} %copy-done, bf16[128,1024]{1,0:T(8,128)(2,1)S(1)} %constant_dynamic-update-slice_fusion.refs_2_, f32[4,128,1024]{2,1,0:T(8,128)S(1)} %get-tuple-element.51.refs_3_, ...), custom_call_target="tpu_custom_call" | custom-call | flops 268435456 | bytes 3407872 | tf_op jit(solution)/shard_map/pallas_call | solution.py:283
  101.6 0.0 collective-permute-done.6.refs_2_
  101.6 2.3 %shard_map.46 = bf16[1024,512]{1,0:T(8,128)(2,1)} custom-call(f32[1]{0:T(128)} %bitcast.refs_0_, bf16[1024,512]{1,0:T(8,128)(2,1)S(1)} %copy-done, bf16[128,1024]{1,0:T(8,128)(2,1)S(1)} %collective-permute-done.6.refs_2_, f32[4,128,1024]{2,1,0:T(8,128)S(1)} %get-tuple-element.54.refs_3_, f32[4,1,1024]{2,1,0:T(1,128)S(1)} %get-tuple-element.55.refs_4_, ...), custom_call_target="tpu_custom_call" | custom-call | flops 268435456 | bytes 3407872 | tf_op jit(solution)/shard_map/pallas_call | solution.py:283
  (4 shorter events, 0.1 us)
Async XLA Ops:
  3.2 44.8 %copy-start = (bf16[1024,512]{1,0:T(8,128)(2,1)S(1)}, bf16[1024,512]{1,0:T(8,128)(2,1)}, u32[]{:S(2)}) copy-start(bf16[1024,512]{1,0:T(8,128)(2,1)} %refs_1_.13) | copy-start | bytes 3145732
  3.2 5.0 %collective-permute-start.1 = (bf16[512,1024]{1,0:T(8,128)(2,1)S(1)}, bf16[512,1024]{1,0:T(8,128)(2,1)S(1)}, u32[]{:S(2)}, u32[]{:S(2)}) collective-permute-start(bf16[512,1024]{1,0:T(8,128)(2,1)S(1)} %get-tuple-element.33), channel_id=1, source_target_pairs={{0,8},{8,0},{16,24},{24,16},{32,40},{40,32},{48,56},{56,48},{64,72... | collective-permute-start | bytes 3145736 | tf_op jit(solution)/shard_map/ppermute | solution.py:33
  6.0 21.1 %collective-permute-start = (bf16[128,1024]{1,0:T(8,128)(2,1)S(1)}, bf16[128,1024]{1,0:T(8,128)(2,1)S(1)}, u32[]{:S(2)}, u32[]{:S(2)}) collective-permute-start(bf16[128,1024]{1,0:T(8,128)(2,1)S(1)} %get-tuple-element.32), channel_id=1, source_target_pairs={{0,16},{8,24},{16,0},{24,8},{32,48},{40,56},{48,32},{56,40},{64,80... | collective-permute-start | bytes 786440 | tf_op jit(solution)/shard_map/ppermute | solution.py:33
  8.6 18.4 %collective-permute-start.2 = (bf16[128,1024]{1,0:T(8,128)(2,1)S(1)}, bf16[128,1024]{1,0:T(8,128)(2,1)S(1)}, u32[]{:S(2)}, u32[]{:S(2)}) collective-permute-start(bf16[128,1024]{1,0:T(8,128)(2,1)S(1)} %shard_map.37.both_ref), channel_id=1, source_target_pairs={{0,32},{8,56},{16,48},{24,40},{32,0},{40,24},{48,16},{56,8},{64,96... | collective-permute-start | bytes 786440 | tf_op jit(solution)/shard_map/ppermute | solution.py:33
  28.0 14.0 %collective-permute-start.3 = (bf16[256,1024]{1,0:T(8,128)(2,1)}, bf16[256,1024]{1,0:T(8,128)(2,1)S(1)}, u32[]{:S(2)}, u32[]{:S(2)}) collective-permute-start(bf16[256,1024]{1,0:T(8,128)(2,1)} %get-tuple-element.35.refs_2_), channel_id=1, source_target_pairs={{0,8},{8,0},{16,24},{24,16},{32,40},{40,32},{48,56},{56,48},{64,72... | collective-permute-start | bytes 1572872 | tf_op jit(solution)/shard_map/ppermute | solution.py:33
  30.4 24.4 %collective-permute-start.7 = (bf16[128,1024]{1,0:T(8,128)(2,1)S(1)}, bf16[128,1024]{1,0:T(8,128)(2,1)S(1)}, u32[]{:S(2)}, u32[]{:S(2)}) collective-permute-start(bf16[128,1024]{1,0:T(8,128)(2,1)S(1)} %get-tuple-element.34.three_ref), channel_id=1, source_target_pairs={{0,64},{8,72},{16,80},{24,88},{32,96},{40,104},{48,112},{56,120},{... | collective-permute-start | bytes 786440 | tf_op jit(solution)/shard_map/ppermute | solution.py:33
  34.4 56.8 %collective-permute-start.10 = (bf16[256,1024]{1,0:T(8,128)(2,1)}, bf16[256,1024]{1,0:T(8,128)(2,1)}, u32[]{:S(2)}, u32[]{:S(2)}) collective-permute-start(bf16[256,1024]{1,0:T(8,128)(2,1)} %get-tuple-element.38), channel_id=1, source_target_pairs={{8,16},{16,8},{24,32},{32,24},{40,48},{48,40},{56,64},{64,56},{72,... | collective-permute-start | bytes 1572872 | tf_op jit(solution)/shard_map/ppermute | solution.py:33
  42.8 41.4 %collective-permute-start.8 = (bf16[128,1024]{1,0:T(8,128)(2,1)S(1)}, bf16[128,1024]{1,0:T(8,128)(2,1)S(1)}, u32[]{:S(2)}, u32[]{:S(2)}) collective-permute-start(bf16[128,1024]{1,0:T(8,128)(2,1)S(1)} %get-tuple-element.37), channel_id=1, source_target_pairs={{0,128},{8,200},{16,144},{24,216},{32,160},{40,232},{48,176},{56,2... | collective-permute-start | bytes 786440 | tf_op jit(solution)/shard_map/ppermute | solution.py:33
  54.8 33.7 %collective-permute-start.4 = (bf16[64,1024]{1,0:T(8,128)(2,1)S(1)}, bf16[64,1024]{1,0:T(8,128)(2,1)S(1)}, u32[]{:S(2)}, u32[]{:S(2)}) collective-permute-start(bf16[64,1024]{1,0:T(8,128)(2,1)S(1)} %get-tuple-element.36), channel_id=1, source_target_pairs={{0,320},{8,264},{16,336},{24,280},{32,352},{40,296},{48,368},{56,3... | collective-permute-start | bytes 393224 | tf_op jit(solution)/shard_map/ppermute | solution.py:33
  82.2 6.9 %collective-permute-start.5 = (bf16[64,1024]{1,0:T(8,128)(2,1)S(1)}, bf16[64,1024]{1,0:T(8,128)(2,1)S(1)}, u32[]{:S(2)}, u32[]{:S(2)}) collective-permute-start(bf16[64,1024]{1,0:T(8,128)(2,1)S(1)} %get-tuple-element.36), channel_id=1, source_target_pairs={{0,384},{8,456},{16,400},{24,472},{32,416},{40,488},{48,432},{56,5... | collective-permute-start | bytes 393224 | tf_op jit(solution)/shard_map/ppermute | solution.py:33
  84.2 14.6 %collective-permute-start.9 = (bf16[256,1024]{1,0:T(8,128)(2,1)S(1)}, bf16[256,1024]{1,0:T(8,128)(2,1)S(1)}, u32[]{:S(2)}, u32[]{:S(2)}) collective-permute-start(bf16[256,1024]{1,0:T(8,128)(2,1)S(1)} %constant_dynamic-update-slice_fusion.2.refs_2_), channel_id=1, source_target_pairs={{0,8},{8,0},{16,24},{24,16},{32,40},{40,32},{48,56},{56,48},{64,72... | collective-permute-start | bytes 1572872 | tf_op jit(solution)/shard_map/ppermute | solution.py:33
  89.1 12.5 %collective-permute-start.6 = (bf16[128,1024]{1,0:T(8,128)(2,1)S(1)}, bf16[128,1024]{1,0:T(8,128)(2,1)S(1)}, u32[]{:S(2)}, u32[]{:S(2)}) collective-permute-start(bf16[128,1024]{1,0:T(8,128)(2,1)S(1)} %constant_dynamic-update-slice_fusion.refs_2_), channel_id=1, source_target_pairs={{0,8},{8,0},{16,24},{24,16},{32,40},{40,32},{48,56},{56,48},{64,72... | collective-permute-start | bytes 786440 | tf_op jit(solution)/shard_map/ppermute | solution.py:33
